TPU v7x, 256 devices: a whole 4x4x8 slice. The times are simulated.
256 devices in a mesh: gx: 32 (over z_lo, x, y), gy: 8 (over z_hi, core).
Axes of the slice: x: 4, y: 4, z: 8 (z_hi: 4, z_lo: 2; z = z_hi * 2 + z_lo), core: 2. Of those that a mesh axis runs over, the one named last changes fastest.
Arguments:
- background_sample: float32 [64, 2, 4, 512, 1024], P(None, None, None, 'gx', 'gy'), may hold values from -6 to 6
- courant_eastward: float32 [2, 512, 1024], P(None, 'gx', 'gy'), may hold values from -0.3 to 0.3
- courant_northward: float32 [2, 512, 1024], P(None, 'gx', 'gy'), may hold values from -0.3 to 0.3
- diffusivity: float32 [512, 1024], P('gx', 'gy'), may hold values from 0.02 to 0.1
- sample_site: int32 [32, 8, 4, 128], P('gx', 'gy'), may hold values from 0 to 16383
- live_count: int32 [32, 8, 4], P('gx', 'gy'), may hold values from 1 to 128, as said below
- observed: float32 [32, 8, 4, 128], P('gx', 'gy'), may hold values from -8 to 8
- error_variance: float32 [32, 8, 4, 128], P('gx', 'gy'), may hold values from 4 to 40
- reach_mask: int32 [32, 8, 5, 5], P('gx', 'gy'), may hold values 0 or 1
Outputs:
- analysis: float32 [64, 2, 4, 512, 1024], P(None, None, None, 'gx', 'gy')
Inputs may be any that keep to these rules, and one draw needn't show every extreme that they name: Slots 0 to live_count - 1 of a tile's batch hold its observations, the rest are unused; in every batch some tile has 128 of them.
All inputs are finite; a program needn't handle non-finite values. No bound on the sum of `reach_mask` on one device may be relied on, other than what follows from the above.
Results may differ from a plain program's by a relative error of at most 0.00015.
Values sent between devices are 32-bit elements; how exact they have to be, the bound alone decides.
A program may use at most 128 MiB of HBM per device.

v0:
```python
import functools

import jax
import jax.numpy as jnp
from jax import lax
from jax.experimental import pallas as pl
from jax.experimental.pallas import tpu as pltpu
from jax.sharding import PartitionSpec as P

BATCHES = 4
RAD = 2
NS_STEPS = 6
WIDTH = 2 * RAD + 1
OFFSETS = [(dx, dy) for dx in range(-RAD, RAD + 1) for dy in range(-RAD, RAD + 1)]


def matmul_full(left, right):
    return jnp.dot(left, right, precision=lax.Precision.HIGHEST, preferred_element_type=jnp.float32)


def mixing_matrix(gram_matrix, projection):
    realisation_vectors = gram_matrix.shape[0]
    identity = jnp.eye(realisation_vectors, dtype=jnp.float32)
    precision_matrix = identity + gram_matrix / (realisation_vectors - 1)
    frobenius = jnp.sqrt(jnp.sum(precision_matrix * precision_matrix))
    iterate = precision_matrix / frobenius
    inverse = identity
    for repeat in range(NS_STEPS):
        factor = 1.5 * identity - 0.5 * matmul_full(inverse, iterate)
        iterate = matmul_full(iterate, factor)
        inverse = matmul_full(factor, inverse)
    transform = inverse / jnp.sqrt(frobenius)
    weights = matmul_full(transform, matmul_full(transform, projection)) / (realisation_vectors - 1)
    return transform + weights[:, None]


def stencil_kernel(x_ref, east_ref, west_ref, edge_ref, u_ref, v_ref, d_ref, o_ref, east_scr, west_scr):
    rows = x_ref.shape[3]
    lanes = x_ref.shape[4]
    east_scr[:, :, :, 0 : rows - 1, :] = x_ref[:, :, :, 1:rows, :]
    east_scr[:, :, :, rows - 1 : rows, :] = east_ref[...]
    west_scr[:, :, :, 1:rows, :] = x_ref[:, :, :, 0 : rows - 1, :]
    west_scr[:, :, :, 0:1, :] = west_ref[...]
    centre = x_ref[...]
    east_cell = east_scr[...]
    west_cell = west_scr[...]
    edge = edge_ref[...]
    lane = lax.broadcasted_iota(jnp.int32, centre.shape, 4)
    north_cell = jnp.where(lane == lanes - 1, edge, pltpu.roll(centre, lanes - 1, 4))
    south_cell = jnp.where(lane == 0, edge, pltpu.roll(centre, 1, 4))
    u = u_ref[...][None, :, None]
    v = v_ref[...][None, :, None]
    d = d_ref[...][None, None, None]
    flux_x = jnp.maximum(u, 0.0) * (centre - west_cell) + jnp.minimum(u, 0.0) * (east_cell - centre)
    flux_y = jnp.maximum(v, 0.0) * (centre - south_cell) + jnp.minimum(v, 0.0) * (north_cell - centre)
    spread_term = d * (east_cell + west_cell + north_cell + south_cell - 4.0 * centre)
    o_ref[...] = centre + spread_term - flux_x - flux_y


def forecast_step(cells, courant_eastward, courant_northward, diffusivity):
    nx = lax.axis_size("gx")
    ny = lax.axis_size("gy")
    rows, lanes = cells.shape[3], cells.shape[4]
    east_halo = lax.ppermute(cells[:, :, :, 0:1, :], "gx", [(i + 1, i) for i in range(nx - 1)])
    west_halo = lax.ppermute(cells[:, :, :, rows - 1 : rows, :], "gx", [(i, i + 1) for i in range(nx - 1)])
    north_halo = lax.ppermute(cells[..., 0], "gy", [(i + 1, i) for i in range(ny - 1)])
    south_halo = lax.ppermute(cells[..., lanes - 1], "gy", [(i, i + 1) for i in range(ny - 1)])
    lane = lax.broadcasted_iota(jnp.int32, cells.shape, 4)
    edge = jnp.where(
        lane == lanes - 1,
        north_halo[..., None],
        jnp.where(lane == 0, south_halo[..., None], 0.0),
    )
    block = 8
    members = cells.shape[0]
    big = pl.BlockSpec((block,) + cells.shape[1:], lambda i: (i, 0, 0, 0, 0))
    thin = pl.BlockSpec((block,) + cells.shape[1:3] + (1, lanes), lambda i: (i, 0, 0, 0, 0))
    whole3 = pl.BlockSpec(courant_eastward.shape, lambda i: (0, 0, 0))
    whole2 = pl.BlockSpec(diffusivity.shape, lambda i: (0, 0))
    return pl.pallas_call(
        stencil_kernel,
        out_shape=jax.ShapeDtypeStruct(cells.shape, cells.dtype),
        grid=(members // block,),
        in_specs=[big, thin, thin, big, whole3, whole3, whole2],
        out_specs=big,
        scratch_shapes=[
            pltpu.VMEM((block,) + cells.shape[1:], cells.dtype),
            pltpu.VMEM((block,) + cells.shape[1:], cells.dtype),
        ],
    )(cells, east_halo, west_halo, edge, courant_eastward, courant_northward, diffusivity)


def exchange_kernel(nx, ny, payload_ref, out_ref, slots, send_sem, recv_sem):
    me_x = lax.axis_index("gx")
    me_y = lax.axis_index("gy")

    def inside(x, y):
        return (x >= 0) & (x < nx) & (y >= 0) & (y < ny)

    barrier = pltpu.get_barrier_semaphore()
    partners = jnp.int32(0)
    for dx, dy in OFFSETS:
        if dx == 0 and dy == 0:
            continue
        ok = inside(me_x - dx, me_y - dy)
        partners = partners + ok.astype(jnp.int32)

        @pl.when(ok)
        def _():
            pl.semaphore_signal(
                barrier, inc=1, device_id=(me_x - dx, me_y - dy),
                device_id_type=pl.DeviceIdType.MESH,
            )

    pl.semaphore_wait(barrier, partners)

    copies = []
    for k, (dx, dy) in enumerate(OFFSETS):
        if dx == 0 and dy == 0:
            continue
        copy = pltpu.make_async_remote_copy(
            src_ref=payload_ref,
            dst_ref=slots.at[k],
            send_sem=send_sem.at[k],
            recv_sem=recv_sem.at[k],
            device_id=(me_x - dx, me_y - dy),
            device_id_type=pl.DeviceIdType.MESH,
        )
        ok = inside(me_x - dx, me_y - dy)

        @pl.when(ok)
        def _():
            copy.start()

        copies.append((k, dx, dy, copy, ok))

    out_ref[RAD * WIDTH + RAD] = payload_ref[...]
    for k, dx, dy, copy, ok in copies:
        @pl.when(ok)
        def _():
            copy.wait_send()

        arrives = inside(me_x + dx, me_y + dy)

        @pl.when(arrives)
        def _():
            copy.wait_recv()
            out_ref[k] = slots[k]

        @pl.when(jnp.logical_not(arrives))
        def _():
            out_ref[k] = jnp.zeros(out_ref.shape[1:], out_ref.dtype)


def gather_neighbourhood(payload, nx, ny):
    count = len(OFFSETS)
    return pl.pallas_call(
        functools.partial(exchange_kernel, nx, ny),
        out_shape=jax.ShapeDtypeStruct((count,) + payload.shape, payload.dtype),
        in_specs=[pl.BlockSpec(memory_space=pltpu.VMEM)],
        out_specs=pl.BlockSpec(memory_space=pltpu.VMEM),
        scratch_shapes=[
            pltpu.VMEM((count,) + payload.shape, payload.dtype),
            pltpu.SemaphoreType.DMA((count,)),
            pltpu.SemaphoreType.DMA((count,)),
        ],
        compiler_params=pltpu.CompilerParams(collective_id=0, has_side_effects=True),
    )(payload)


def on_device(
    background_sample,
    courant_eastward,
    courant_northward,
    diffusivity,
    sample_site,
    live_count,
    observed,
    error_variance,
    reach_mask,
):
    nx = lax.axis_size("gx")
    ny = lax.axis_size("gy")
    forecast = forecast_step(background_sample, courant_eastward, courant_northward, diffusivity)
    members = forecast.shape[0]
    state = forecast.reshape(members, -1)
    site_table = sample_site[0, 0]
    counts = live_count[0, 0]
    observed_here = observed[0, 0]
    variance_here = error_variance[0, 0]
    batches, slot_count = site_table.shape
    slot_index = jnp.arange(slot_count)
    mask_index = jnp.arange(WIDTH)
    centre_one = ((mask_index[:, None] == RAD) & (mask_index[None, :] == RAD)).astype(jnp.float32)
    reach_weight = jnp.maximum(reach_mask[0, 0].astype(jnp.float32), centre_one).reshape(-1)
    all_sampled = jnp.take(state, site_table.reshape(-1), axis=1).reshape(members, batches, slot_count)
    identity = jnp.eye(members, dtype=jnp.float32)
    carried = identity
    half = members * members // 128
    for batch_index in range(batches):
        if batch_index == 0:
            sampled = all_sampled[:, 0]
        else:
            sampled = matmul_full(carried, all_sampled[:, batch_index])
        prior_mean = jnp.mean(sampled, axis=0)
        live_slot = (slot_index < counts[batch_index]).astype(jnp.float32)
        error_scale = 1.0 / jnp.sqrt(variance_here[batch_index])
        scaled_rows = (live_slot * error_scale)[None, :] * (sampled - prior_mean[None, :])
        innovation = live_slot * (observed_here[batch_index] - prior_mean) * error_scale
        gram_here = matmul_full(scaled_rows, scaled_rows.T)
        proj_here = matmul_full(scaled_rows, innovation[:, None])[:, 0]
        payload = jnp.concatenate(
            [
                gram_here.reshape(half, 128),
                jnp.pad(proj_here, (0, 128 - members))[None, :],
                jnp.zeros((7, 128), jnp.float32),
            ],
            axis=0,
        )
        stack = gather_neighbourhood(payload, nx, ny)
        gram_total = jnp.sum(reach_weight[:, None, None] * stack[:, :half], axis=0).reshape(members, members)
        proj_total = jnp.sum(reach_weight[:, None] * stack[:, half, :members], axis=0)
        mixing = mixing_matrix(gram_total, proj_total)
        step = 1.0 / members + mixing.T - jnp.mean(mixing, axis=0)[:, None]
        carried = step if batch_index == 0 else matmul_full(step, carried)
    analysis = matmul_full(carried, state)
    return analysis.reshape(forecast.shape)


def solution(mesh):
    in_specs = (
        P(None, None, None, "gx", "gy"),
        P(None, "gx", "gy"),
        P(None, "gx", "gy"),
        P("gx", "gy"),
        P("gx", "gy", None, None),
        P("gx", "gy", None),
        P("gx", "gy", None, None),
        P("gx", "gy", None, None),
        P("gx", "gy", None, None),
    )
    out_specs = P(None, None, None, "gx", "gy")
    return jax.shard_map(
        on_device, mesh=mesh, in_specs=in_specs, out_specs=out_specs, check_vma=False
    )
```

profile of v0, /device:TPU:96, one launch (start us, length us, event | category | flops | bytes accessed | tf_op | source)
XLA Modules:
  0.0 195.3 jit_solution(10654119205142911318)
XLA Ops:
  0.0 2.8 %fusion.149 = (f32[64,2,4,1,128]{4,3,2,1,0:T(1,128)S(1)}, f32[64,2,4,1,128]{4,3,2,1,0:T(1,128)S(1)}) fusion(f32[64,2,4,16,128]{4,3,2,1,0:T(8,128)} %x_ref.1), kind=kLoop, calls=%fused_computation.259 | loop fusion | bytes 1048576 | tf_op jit(solution)/shard_map/slice | solution.py:65
  2.8 6.7 %collective-permute-start = (f32[64,2,4,1,128]{4,3,2,1,0:T(1,128)S(1)}, f32[64,2,4,1,128]{4,3,2,1,0:T(1,128)S(1)}, u32[]{:S(2)}, u32[]{:S(2)}) collective-permute-start(f32[64,2,4,1,128]{4,3,2,1,0:T(1,128)S(1)} %get-tuple-element.10), channel_id=1, source_target_pairs={{8,0},{16,8},{24,16},{32,24},{40,32},{48,40},{56,48},{64,56},{72,6... | collective-permute-start | bytes 786440 | tf_op jit(solution)/shard_map/ppermute | solution.py:64
  9.5 1.9 collective-permute-start.1
  11.4 8.2 %fusion.148 = (f32[64,2,4,16,1]{4,3,2,1,0:T(8,128)}, f32[64,2,4,16,1]{4,3,2,1,0:T(8,128)}) fusion(f32[64,2,4,16,128]{4,3,2,1,0:T(8,128)} %x_ref.1), kind=kLoop, calls=%fused_computation.258 | loop fusion | bytes 131072 | tf_op jit(solution)/shard_map/slice | solution.py:66
  19.6 3.7 %copy.28 = f32[64,2,4,16,1]{0,3,4,2,1:T(8,128)S(1)} copy(f32[64,2,4,16,1]{4,3,2,1,0:T(8,128)} %get-tuple-element.8) | data formatting | bytes 65536
  23.3 1.9 collective-permute-start.3
  25.2 3.7 %copy.27 = f32[64,2,4,16,1]{0,3,4,2,1:T(8,128)S(1)} copy(f32[64,2,4,16,1]{4,3,2,1,0:T(8,128)} %get-tuple-element.7) | data formatting | bytes 65536
  28.9 4.5 %collective-permute-start.2 = (f32[64,2,4,16]{0,3,2,1:T(8,128)S(1)}, f32[64,2,4,16]{0,3,2,1:T(8,128)S(1)}, u32[]{:S(2)}, u32[]{:S(2)}) collective-permute-start(f32[64,2,4,16]{0,3,2,1:T(8,128)S(1)} %bitcast.336), channel_id=1, source_target_pairs={{1,0},{2,1},{3,2},{4,3},{5,4},{6,5},{7,6},{9,8},{10,9},{11,10},{12... | collective-permute-start | bytes 98312 | tf_op jit(solution)/shard_map/ppermute | solution.py:66
  34.2 2.4 %compare_select_fusion.9 = (f32[128]{0:T(128)S(1)}, f32[128]{0:T(128)S(1)}, f32[128]{0:T(128)S(1)}, f32[128]{0:T(128)S(1)}) fusion(s32[]{:T(128)} %bitcast, f32[1,1,4,128]{3,2,1,0:T(4,128)S(1)} %copy-done.2, s32[]{:T(128)} %bitcast.2, s32[]{:T(128)} %bitcast.34, s32[]{:T(128)} %bitcast.22), kind=kLoop, calls=%fused_computation.197 | loop fusion | flops 1024 | bytes 4112 | tf_op jit(solution)/shard_map/mul | solution.py:208
  37.2 3.8 %select_select_fusion.edge_ref = f32[64,2,4,16,128]{4,3,2,1,0:T(8,128)} fusion(f32[64,2,4,16]{3,2,1,0:T(4,128)S(1)} %copy.18, f32[64,2,4,16]{3,2,1,0:T(4,128)S(1)} %copy.16, pred[128]{0:T(512)(128)(4,1)S(1)} %get-tuple-element.25, pred[128]{0:T(512)(128)(4,1)S(1)} %get-tuple-element.26), kind=kLoop, calls=%fused_computation.4 | loop fusion | flops 2097152 | bytes 4260096 | tf_op jit(solution)/shard_map/jit(_where)/select_n | solution.py:69
  42.4 9.1 %shard_map.91 = f32[64,2,4,16,128]{4,3,2,1,0:T(8,128)} custom-call(f32[64,2,4,16,128]{4,3,2,1,0:T(8,128)} %x_ref.1, f32[64,2,4,1,128]{4,3,2,1,0:T(1,128)} %copy-done, f32[64,2,4,1,128]{4,3,2,1,0:T(1,128)} %copy-done.1, f32[64,2,4,16,128]{4,3,2,1,0:T(8,128)} %select_select_fusion.edge_ref, f32[2,16,128]{2,1,0:T(8,128)} %u_ref.1, f32[2,16,128]{2,1,0:T(8,128)} %v_ref.1, ...), custom_call_target="tpu_custom_call" | custom-call | tf_op jit(solution)/shard_map/pallas_call | solution.py:80
  51.5 6.6 %copy.55 = f32[8,8,128,128]{3,1,2,0:T(8,128)} copy(f32[8,8,128,128]{3,2,1,0:T(8,128)} %bitcast.333) | data formatting | bytes 8388608
  58.1 6.9 %copy.19 = f32[64,16384]{0,1:T(8,128)} copy(f32[64,16384]{1,0:T(8,128)} %bitcast.331) | data formatting | bytes 8388608 | tf_op jit(solution)/shard_map/reshape | solution.py:186
  65.0 4.4 %gather_fusion = f32[512,64]{1,0:T(8,128)S(1)} fusion(f32[64,16384]{0,1:T(8,128)} %copy.19, s32[1024]{0:T(1024)S(1)} %pad_clamp_fusion), kind=kCustom, calls=%fused_computation | custom fusion | bytes 264192 | tf_op jit(solution)/shard_map/jit(_take)/gather | solution.py:196
  70.0 0.9 convolution_bitcast_fusion.12
  71.6 21.0 %shard_map.92 = f32[25,40,128]{2,1,0:T(8,128)} custom-call(f32[40,128]{1,0:T(8,128)} %maximum_maximum_fusion.payload_ref), custom_call_target="tpu_custom_call" | custom-call | tf_op jit(solution)/shard_map/pallas_call | solution.py:157
  92.7 1.1 multiply_reduce_fusion.3
  94.0 0.8 multiply_reduce_fusion.7
  98.1 0.9 slice.107
  101.9 17.8 %shard_map.93 = f32[25,40,128]{2,1,0:T(8,128)} custom-call(f32[40,128]{1,0:T(8,128)} %maximum_maximum_fusion.1.payload_ref), custom_call_target="tpu_custom_call" | custom-call | tf_op jit(solution)/shard_map/pallas_call | solution.py:157
  119.7 1.1 multiply_reduce_fusion.2
  121.0 0.8 multiply_reduce_fusion.6
  125.1 0.9 slice.113
  129.2 17.7 %shard_map.94 = f32[25,40,128]{2,1,0:T(8,128)} custom-call(f32[40,128]{1,0:T(8,128)} %maximum_maximum_fusion.2.payload_ref), custom_call_target="tpu_custom_call" | custom-call | tf_op jit(solution)/shard_map/pallas_call | solution.py:157
  146.9 1.1 multiply_reduce_fusion.1
  152.3 0.9 slice.119
  156.3 18.1 %shard_map.95 = f32[25,40,128]{2,1,0:T(8,128)} custom-call(f32[40,128]{1,0:T(8,128)} %maximum_maximum_fusion.3.payload_ref), custom_call_target="tpu_custom_call" | custom-call | tf_op jit(solution)/shard_map/pallas_call | solution.py:157
  174.4 1.1 multiply_reduce_fusion
  179.8 0.9 slice.123
  181.9 2.9 %copy.33 = f32[8,8,128,128]{3,2,1,0:T(8,128)S(1)} copy(f32[8,8,128,128]{3,1,2,0:T(8,128)} %copy.55) | data formatting | bytes 8388608
  184.8 6.0 %fusion = f32[64,2,4,16,128]{4,0,3,2,1:T(8,128)S(1)} fusion(f32[64,64,1,1,1]{1,0,4,3,2:T(8,128)S(1)} %convolution_bitcast_fusion, f32[2,4,16,128,64]{3,2,1,0,4:T(8,128)S(1)} %bitcast.332), kind=kOutput, calls=%fused_computation.2 | convolution fusion | flops 805306368 | bytes 8404992 | tf_op jit(solution)/shard_map/dot_general | solution.py:18
  190.8 4.4 %copy.24 = f32[64,2,4,16,128]{4,3,2,1,0:T(8,128)} copy(f32[64,2,4,16,128]{4,0,3,2,1:T(8,128)S(1)} %fusion) | data formatting | bytes 8388608 | tf_op jit(solution)/shard_map/dot_general | solution.py:18
  (167 shorter events, 26.2 us)
Async XLA Ops:
  2.8 38.2 %collective-permute-start = (f32[64,2,4,1,128]{4,3,2,1,0:T(1,128)S(1)}, f32[64,2,4,1,128]{4,3,2,1,0:T(1,128)S(1)}, u32[]{:S(2)}, u32[]{:S(2)}) collective-permute-start(f32[64,2,4,1,128]{4,3,2,1,0:T(1,128)S(1)} %get-tuple-element.10), channel_id=1, source_target_pairs={{8,0},{16,8},{24,16},{32,24},{40,32},{48,40},{56,48},{64,56},{72,6... | collective-permute-start | bytes 786440 | tf_op jit(solution)/shard_map/ppermute | solution.py:64
  9.5 31.5 %collective-permute-start.1 = (f32[64,2,4,1,128]{4,3,2,1,0:T(1,128)S(1)}, f32[64,2,4,1,128]{4,3,2,1,0:T(1,128)S(1)}, u32[]{:S(2)}, u32[]{:S(2)}) collective-permute-start(f32[64,2,4,1,128]{4,3,2,1,0:T(1,128)S(1)} %get-tuple-element.9), channel_id=1, source_target_pairs={{0,8},{8,16},{16,24},{24,32},{32,40},{40,48},{48,56},{56,64},{64,7... | collective-permute-start | bytes 786440 | tf_op jit(solution)/shard_map/ppermute | solution.py:65
  19.5 13.9 %copy-start.4 = (s32[1,1,4,128]{3,2,1,0:T(4,128)S(1)}, s32[1,1,4,128]{3,2,1,0:T(4,128)}, u32[]{:S(2)}) copy-start(s32[1,1,4,128]{3,2,1,0:T(4,128)} %param.13) | copy-start | bytes 6148
  19.5 13.9 %copy-start.5 = (s32[1,1,4]{2,1,0:T(1,128)S(1)}, s32[1,1,4]{2,1,0:T(1,128)}, u32[]{:S(2)}) copy-start(s32[1,1,4]{2,1,0:T(1,128)} %param.14) | copy-start | bytes 52
  19.5 14.6 %copy-start.6 = (s32[1,1,5,5]{3,1,2,0:T(1,128)S(1)}, s32[1,1,5,5]{3,1,2,0:T(1,128)}, u32[]{:S(2)}) copy-start(s32[1,1,5,5]{3,1,2,0:T(1,128)} %param.17) | copy-start | bytes 304
  19.5 14.6 %copy-start.2 = (f32[1,1,4,128]{3,2,1,0:T(4,128)S(1)}, f32[1,1,4,128]{3,2,1,0:T(4,128)}, u32[]{:S(2)}) copy-start(f32[1,1,4,128]{3,2,1,0:T(4,128)} %param.16) | copy-start | bytes 6148
  23.3 13.6 %collective-permute-start.3 = (f32[64,2,4,16]{0,3,2,1:T(8,128)S(1)}, f32[64,2,4,16]{0,3,2,1:T(8,128)S(1)}, u32[]{:S(2)}, u32[]{:S(2)}) collective-permute-start(f32[64,2,4,16]{0,3,2,1:T(8,128)S(1)} %bitcast.335), channel_id=1, source_target_pairs={{0,1},{1,2},{2,3},{3,4},{4,5},{5,6},{6,7},{8,9},{9,10},{10,11},{11... | collective-permute-start | bytes 98312 | tf_op jit(solution)/shard_map/ppermute | solution.py:67
  28.9 8.2 %collective-permute-start.2 = (f32[64,2,4,16]{0,3,2,1:T(8,128)S(1)}, f32[64,2,4,16]{0,3,2,1:T(8,128)S(1)}, u32[]{:S(2)}, u32[]{:S(2)}) collective-permute-start(f32[64,2,4,16]{0,3,2,1:T(8,128)S(1)} %bitcast.336), channel_id=1, source_target_pairs={{1,0},{2,1},{3,2},{4,3},{5,4},{6,5},{7,6},{9,8},{10,9},{11,10},{12... | collective-permute-start | bytes 98312 | tf_op jit(solution)/shard_map/ppermute | solution.py:66
  41.0 0.7 copy-start
  41.7 0.7 copy-start.1
  58.1 12.0 %copy-start.3 = (f32[1,1,4,128]{3,2,1,0:T(4,128)S(1)}, f32[1,1,4,128]{3,2,1,0:T(4,128)}, u32[]{:S(2)}) copy-start(f32[1,1,4,128]{3,2,1,0:T(4,128)} %param.15) | copy-start | bytes 6148
where the time goes:
time: 199 us; the launch traced here: 195 us
  Pallas kernels  83.8 us (42%)
  local copies, waits for them, and re-layouts  50.7 us (25%)
  matrix products  24 us (12%)
  other arithmetic  17.7 us (9%)
  starting transfers between devices  15 us (8%)
  between operations  4.1 us (2%)
    pallas_call x4, Pallas kernels, gather_neighbourhood(): pl.pallas_call(functools.partial(exchange_kernel, nx, ny), out_shape=jax....  74.6 us
    dot_general x91, matrix products, matmul_full(): jnp.dot(left, right, precision=lax.Precision.HIGHEST, preferred_element_t...  24 us
    unnamed x18, local copies, waits for them, and re-layouts  18.3 us
    pallas_call x1, Pallas kernels, forecast_step(): pl.pallas_call(stencil_kernel, out_shape=jax.ShapeDtypeStruct(cells.shape...  9.12 us
    slice x1, local copies, waits for them, and re-layouts, forecast_step(): cells[..., 0]  8.15 us
    reshape x1, local copies, waits for them, and re-layouts, on_device(): state = forecast.reshape(members, -1)  6.91 us
    ppermute x1, starting transfers between devices, forecast_step(): lax.ppermute(cells[:, :, :, 0:1, :], 'gx', [(i + 1, i) for i in range(nx...  6.66 us
    ppermute x1, starting transfers between devices, forecast_step(): lax.ppermute(cells[..., 0], 'gy', [(i + 1, i) for i in range(ny - 1)])  4.53 us
  transfers between devices with their start and end apart: 4, of which 0 were waited for; matrix products, arithmetic and copies ran while one was open for 12% of the time, Pallas kernels for 0%

commit v1 on v0

--- a/solution.py
+++ b/solution.py
@@ -63,13 +63,18 @@
     rows, lanes = cells.shape[3], cells.shape[4]
     east_halo = lax.ppermute(cells[:, :, :, 0:1, :], "gx", [(i + 1, i) for i in range(nx - 1)])
     west_halo = lax.ppermute(cells[:, :, :, rows - 1 : rows, :], "gx", [(i, i + 1) for i in range(nx - 1)])
-    north_halo = lax.ppermute(cells[..., 0], "gy", [(i + 1, i) for i in range(ny - 1)])
-    south_halo = lax.ppermute(cells[..., lanes - 1], "gy", [(i, i + 1) for i in range(ny - 1)])
-    lane = lax.broadcasted_iota(jnp.int32, cells.shape, 4)
-    edge = jnp.where(
-        lane == lanes - 1,
-        north_halo[..., None],
-        jnp.where(lane == 0, south_halo[..., None], 0.0),
+    lane_index = jnp.arange(lanes)
+    pick = jnp.stack([lane_index == 0, lane_index == lanes - 1]).astype(jnp.float32)
+    place = jnp.stack([lane_index == lanes - 1, lane_index == 0]).astype(jnp.float32)
+    sides = jnp.einsum(
+        "abcil,sl->sabci",
+        cells, pick, precision=lax.Precision.HIGHEST, preferred_element_type=jnp.float32,
+    )
+    north_halo = lax.ppermute(sides[0], "gy", [(i + 1, i) for i in range(ny - 1)])
+    south_halo = lax.ppermute(sides[1], "gy", [(i, i + 1) for i in range(ny - 1)])
+    edge = jnp.einsum(
+        "sabci,sl->abcil", jnp.stack([north_halo, south_halo]), place,
+        precision=lax.Precision.HIGHEST, preferred_element_type=jnp.float32,
     )
     block = 8
     members = cells.shape[0]

time: 199 us -> 192 us (0.965)
  the two profiles are of different devices: /device:TPU:96 before, /device:TPU:86 now
where the time goes in v1:
time: 192 us; the launch traced here: 191 us
  Pallas kernels  87.7 us (46%)
  matrix products  37.4 us (19%)
  local copies, waits for them, and re-layouts  35.4 us (18%)
  other arithmetic  14 us (7%)
  starting transfers between devices  12.5 us (7%)
  between operations  4.1 us (2%)
    pallas_call x4, Pallas kernels, gather_neighbourhood(): pl.pallas_call(functools.partial(exchange_kernel, nx, ny), out_shape=jax....  78.6 us
    dot_general x91, matrix products, matmul_full(): jnp.dot(left, right, precision=lax.Precision.HIGHEST, preferred_element_t...  23.9 us
    unnamed x16, local copies, waits for them, and re-layouts  10.9 us
    pallas_call x1, Pallas kernels, forecast_step(): pl.pallas_call(stencil_kernel, out_shape=jax.ShapeDtypeStruct(cells.shape...  9.12 us
    dot_general x1, matrix products, forecast_step(): jnp.einsum('abcil,sl->sabci', cells, pick, precision=lax.Precision.HIGHES...  8.5 us
    reshape x1, local copies, waits for them, and re-layouts, on_device(): state = forecast.reshape(members, -1)  6.91 us
    dot_general x1, matrix products, forecast_step(): jnp.einsum('sabci,sl->abcil', jnp.stack([north_halo, south_halo]), place,...  5.07 us
    ppermute x1, starting transfers between devices, forecast_step(): lax.ppermute(sides[0], 'gy', [(i + 1, i) for i in range(ny - 1)])  4.54 us
  transfers between devices with their start and end apart: 4, of which 0 were waited for; matrix products, arithmetic and copies ran while one was open for 6% of the time, Pallas kernels for 0%

profile of v1, /device:TPU:86, one launch (start us, length us, event | category | flops | bytes accessed | tf_op | source)
XLA Modules:
  0.0 191.1 jit_solution(13757311957780594563)
XLA Ops:
  0.0 8.5 %fusion.2 = f32[2,64,2,4,16]{1,0,4,3,2:T(2,128)S(1)} fusion(f32[64,2,4,16,128]{4,3,2,1,0:T(8,128)} %x_ref.1, pred[1,128]{1,0:T(4,128)(4,1)S(1)} %get-tuple-element.25, pred[1,128]{1,0:T(4,128)(4,1)S(1)} %get-tuple-element.26), kind=kOutput, calls=%fused_computation.4 | convolution fusion | flops 25166080 | bytes 4260096 | tf_op jit(solution)/shard_map/abcil,sl->sabci/dot_general | solution.py:69
  8.7 1.9 %collective-permute-start.3 = (f32[64,2,4,16]{0,3,2,1:T(8,128)S(1)}, f32[64,2,4,16]{0,3,2,1:T(8,128)S(1)}, u32[]{:S(2)}, u32[]{:S(2)}) collective-permute-start(f32[64,2,4,16]{0,3,2,1:T(8,128)S(1)} %bitcast.352), channel_id=1, source_target_pairs={{0,1},{1,2},{2,3},{3,4},{4,5},{5,6},{6,7},{8,9},{9,10},{10,11},{11... | collective-permute-start | bytes 98312 | tf_op jit(solution)/shard_map/ppermute | solution.py:74
  10.6 4.5 %collective-permute-start.2 = (f32[64,2,4,16]{0,3,2,1:T(8,128)S(1)}, f32[64,2,4,16]{0,3,2,1:T(8,128)S(1)}, u32[]{:S(2)}, u32[]{:S(2)}) collective-permute-start(f32[64,2,4,16]{0,3,2,1:T(8,128)S(1)} %bitcast.350), channel_id=1, source_target_pairs={{1,0},{2,1},{3,2},{4,3},{5,4},{6,5},{7,6},{9,8},{10,9},{11,10},{12... | collective-permute-start | bytes 98312 | tf_op jit(solution)/shard_map/ppermute | solution.py:73
  15.1 2.8 %fusion.157 = (f32[64,2,4,1,128]{4,3,2,1,0:T(1,128)S(1)}, f32[64,2,4,1,128]{4,3,2,1,0:T(1,128)S(1)}) fusion(f32[64,2,4,16,128]{4,3,2,1,0:T(8,128)} %x_ref.1), kind=kLoop, calls=%fused_computation.269 | loop fusion | bytes 1048576 | tf_op jit(solution)/shard_map/slice | solution.py:65
  17.9 2.4 %collective-permute-start = (f32[64,2,4,1,128]{4,3,2,1,0:T(1,128)S(1)}, f32[64,2,4,1,128]{4,3,2,1,0:T(1,128)S(1)}, u32[]{:S(2)}, u32[]{:S(2)}) collective-permute-start(f32[64,2,4,1,128]{4,3,2,1,0:T(1,128)S(1)} %get-tuple-element.8), channel_id=1, source_target_pairs={{8,0},{16,8},{24,16},{32,24},{40,32},{48,40},{56,48},{64,56},{72,6... | collective-permute-start | bytes 786440 | tf_op jit(solution)/shard_map/ppermute | solution.py:64
  20.3 3.7 %collective-permute-start.1 = (f32[64,2,4,1,128]{4,3,2,1,0:T(1,128)S(1)}, f32[64,2,4,1,128]{4,3,2,1,0:T(1,128)S(1)}, u32[]{:S(2)}, u32[]{:S(2)}) collective-permute-start(f32[64,2,4,1,128]{4,3,2,1,0:T(1,128)S(1)} %get-tuple-element.7), channel_id=1, source_target_pairs={{0,8},{8,16},{16,24},{24,32},{32,40},{40,48},{48,56},{56,64},{64,7... | collective-permute-start | bytes 786440 | tf_op jit(solution)/shard_map/ppermute | solution.py:65
  24.7 2.4 %compare_select_fusion.9 = (f32[128]{0:T(128)S(1)}, f32[128]{0:T(128)S(1)}, f32[128]{0:T(128)S(1)}, f32[128]{0:T(128)S(1)}) fusion(s32[]{:T(128)} %bitcast, f32[1,1,4,128]{3,2,1,0:T(4,128)S(1)} %copy-done.2, s32[]{:T(128)} %bitcast.2, s32[]{:T(128)} %bitcast.40, s32[]{:T(128)} %bitcast.28), kind=kLoop, calls=%fused_computation.206 | loop fusion | flops 1024 | bytes 4112 | tf_op jit(solution)/shard_map/mul | solution.py:213
  27.9 5.1 %fusion.111.edge_ref = f32[64,2,4,16,128]{4,3,2,1,0:T(8,128)} fusion(f32[2,64,2,4,16]{4,0,3,2,1:T(2,128)S(1)} %copy.20, pred[1,128]{1,0:T(4,128)(4,1)S(1)} %get-tuple-element.26, pred[1,128]{1,0:T(4,128)(4,1)S(1)} %get-tuple-element.25), kind=kOutput, calls=%fused_computation.195 | convolution fusion | flops 25166080 | bytes 4260096 | tf_op jit(solution)/shard_map/sabci,sl->abcil/dot_general | solution.py:75
  34.3 9.1 %shard_map.91 = f32[64,2,4,16,128]{4,3,2,1,0:T(8,128)} custom-call(f32[64,2,4,16,128]{4,3,2,1,0:T(8,128)} %x_ref.1, f32[64,2,4,1,128]{4,3,2,1,0:T(1,128)} %copy-done, f32[64,2,4,1,128]{4,3,2,1,0:T(1,128)} %copy-done.1, f32[64,2,4,16,128]{4,3,2,1,0:T(8,128)} %fusion.111.edge_ref, f32[2,16,128]{2,1,0:T(8,128)} %u_ref.1, f32[2,16,128]{2,1,0:T(8,128)} %v_ref.1, ...), custom_call_target="tpu_custom_call" | custom-call | tf_op jit(solution)/shard_map/pallas_call | solution.py:85
  43.4 6.6 %copy.60 = f32[8,8,128,128]{3,1,2,0:T(8,128)} copy(f32[8,8,128,128]{3,2,1,0:T(8,128)} %bitcast.348) | data formatting | bytes 8388608
  50.0 6.9 %copy.21 = f32[64,16384]{0,1:T(8,128)} copy(f32[64,16384]{1,0:T(8,128)} %bitcast.346) | data formatting | bytes 8388608 | tf_op jit(solution)/shard_map/reshape | solution.py:191
  56.9 4.4 %gather_fusion = f32[512,64]{1,0:T(8,128)S(1)} fusion(f32[64,16384]{0,1:T(8,128)} %copy.21, s32[1024]{0:T(1024)S(1)} %pad_clamp_fusion), kind=kCustom, calls=%fused_computation | custom fusion | bytes 264192 | tf_op jit(solution)/shard_map/jit(_take)/gather | solution.py:201
  62.0 0.9 convolution_bitcast_fusion.12
  63.6 25.0 %shard_map.92 = f32[25,40,128]{2,1,0:T(8,128)} custom-call(f32[40,128]{1,0:T(8,128)} %maximum_maximum_fusion.payload_ref), custom_call_target="tpu_custom_call" | custom-call | tf_op jit(solution)/shard_map/pallas_call | solution.py:162
  88.6 1.1 multiply_reduce_fusion.3
  89.9 0.8 multiply_reduce_fusion.7
  94.0 0.9 slice.107
  97.8 17.9 %shard_map.93 = f32[25,40,128]{2,1,0:T(8,128)} custom-call(f32[40,128]{1,0:T(8,128)} %maximum_maximum_fusion.1.payload_ref), custom_call_target="tpu_custom_call" | custom-call | tf_op jit(solution)/shard_map/pallas_call | solution.py:162
  115.7 1.1 multiply_reduce_fusion.2
  117.0 0.8 multiply_reduce_fusion.6
  121.1 0.9 slice.113
  125.2 17.8 %shard_map.94 = f32[25,40,128]{2,1,0:T(8,128)} custom-call(f32[40,128]{1,0:T(8,128)} %maximum_maximum_fusion.2.payload_ref), custom_call_target="tpu_custom_call" | custom-call | tf_op jit(solution)/shard_map/pallas_call | solution.py:162
  143.0 1.1 multiply_reduce_fusion.1
  144.3 0.8 multiply_reduce_fusion.5
  148.4 0.9 slice.119
  152.4 17.8 %shard_map.95 = f32[25,40,128]{2,1,0:T(8,128)} custom-call(f32[40,128]{1,0:T(8,128)} %maximum_maximum_fusion.3.payload_ref), custom_call_target="tpu_custom_call" | custom-call | tf_op jit(solution)/shard_map/pallas_call | solution.py:162
  170.3 1.1 multiply_reduce_fusion
  171.6 0.8 multiply_reduce_fusion.4
  175.7 0.9 slice.123
  177.8 2.9 %copy.36 = f32[8,8,128,128]{3,2,1,0:T(8,128)S(1)} copy(f32[8,8,128,128]{3,1,2,0:T(8,128)} %copy.60) | data formatting | bytes 8388608
  180.7 6.0 %fusion = f32[64,2,4,16,128]{4,0,3,2,1:T(8,128)S(1)} fusion(f32[64,64,1,1,1]{1,0,4,3,2:T(8,128)S(1)} %convolution_bitcast_fusion, f32[2,4,16,128,64]{3,2,1,0,4:T(8,128)S(1)} %bitcast.347), kind=kOutput, calls=%fused_computation.2 | convolution fusion | flops 805306368 | bytes 8404992 | tf_op jit(solution)/shard_map/dot_general | solution.py:18
  186.7 4.4 %copy.26 = f32[64,2,4,16,128]{4,3,2,1,0:T(8,128)} copy(f32[64,2,4,16,128]{4,0,3,2,1:T(8,128)S(1)} %fusion) | data formatting | bytes 8388608 | tf_op jit(solution)/shard_map/dot_general | solution.py:18
  (166 shorter events, 24.8 us)
Async XLA Ops:
  0.0 24.0 %copy-start.4 = (s32[1,1,4,128]{3,2,1,0:T(4,128)S(1)}, s32[1,1,4,128]{3,2,1,0:T(4,128)}, u32[]{:S(2)}) copy-start(s32[1,1,4,128]{3,2,1,0:T(4,128)} %param.13) | copy-start | bytes 6148
  0.0 24.0 %copy-start.5 = (s32[1,1,4]{2,1,0:T(1,128)S(1)}, s32[1,1,4]{2,1,0:T(1,128)}, u32[]{:S(2)}) copy-start(s32[1,1,4]{2,1,0:T(1,128)} %param.14) | copy-start | bytes 52
  0.0 24.7 %copy-start.6 = (s32[1,1,5,5]{3,1,2,0:T(1,128)S(1)}, s32[1,1,5,5]{3,1,2,0:T(1,128)}, u32[]{:S(2)}) copy-start(s32[1,1,5,5]{3,1,2,0:T(1,128)} %param.17) | copy-start | bytes 304
  0.0 24.7 %copy-start.2 = (f32[1,1,4,128]{3,2,1,0:T(4,128)S(1)}, f32[1,1,4,128]{3,2,1,0:T(4,128)}, u32[]{:S(2)}) copy-start(f32[1,1,4,128]{3,2,1,0:T(4,128)} %param.16) | copy-start | bytes 6148
  8.7 18.7 %collective-permute-start.3 = (f32[64,2,4,16]{0,3,2,1:T(8,128)S(1)}, f32[64,2,4,16]{0,3,2,1:T(8,128)S(1)}, u32[]{:S(2)}, u32[]{:S(2)}) collective-permute-start(f32[64,2,4,16]{0,3,2,1:T(8,128)S(1)} %bitcast.352), channel_id=1, source_target_pairs={{0,1},{1,2},{2,3},{3,4},{4,5},{5,6},{6,7},{8,9},{9,10},{10,11},{11... | collective-permute-start | bytes 98312 | tf_op jit(solution)/shard_map/ppermute | solution.py:74
  10.6 16.8 %collective-permute-start.2 = (f32[64,2,4,16]{0,3,2,1:T(8,128)S(1)}, f32[64,2,4,16]{0,3,2,1:T(8,128)S(1)}, u32[]{:S(2)}, u32[]{:S(2)}) collective-permute-start(f32[64,2,4,16]{0,3,2,1:T(8,128)S(1)} %bitcast.350), channel_id=1, source_target_pairs={{1,0},{2,1},{3,2},{4,3},{5,4},{6,5},{7,6},{9,8},{10,9},{11,10},{12... | collective-permute-start | bytes 98312 | tf_op jit(solution)/shard_map/ppermute | solution.py:73
  17.9 15.0 %collective-permute-start = (f32[64,2,4,1,128]{4,3,2,1,0:T(1,128)S(1)}, f32[64,2,4,1,128]{4,3,2,1,0:T(1,128)S(1)}, u32[]{:S(2)}, u32[]{:S(2)}) collective-permute-start(f32[64,2,4,1,128]{4,3,2,1,0:T(1,128)S(1)} %get-tuple-element.8), channel_id=1, source_target_pairs={{8,0},{16,8},{24,16},{32,24},{40,32},{48,40},{56,48},{64,56},{72,6... | collective-permute-start | bytes 786440 | tf_op jit(solution)/shard_map/ppermute | solution.py:64
  20.3 12.7 %collective-permute-start.1 = (f32[64,2,4,1,128]{4,3,2,1,0:T(1,128)S(1)}, f32[64,2,4,1,128]{4,3,2,1,0:T(1,128)S(1)}, u32[]{:S(2)}, u32[]{:S(2)}) collective-permute-start(f32[64,2,4,1,128]{4,3,2,1,0:T(1,128)S(1)} %get-tuple-element.7), channel_id=1, source_target_pairs={{0,8},{8,16},{16,24},{24,32},{32,40},{40,48},{48,56},{56,64},{64,7... | collective-permute-start | bytes 786440 | tf_op jit(solution)/shard_map/ppermute | solution.py:65
  32.9 0.7 copy-start
  33.6 0.7 copy-start.1
  50.0 12.0 %copy-start.3 = (f32[1,1,4,128]{3,2,1,0:T(4,128)S(1)}, f32[1,1,4,128]{3,2,1,0:T(4,128)}, u32[]{:S(2)}) copy-start(f32[1,1,4,128]{3,2,1,0:T(4,128)} %param.15) | copy-start | bytes 6148

commit v2 on v1

--- a/solution.py
+++ b/solution.py
@@ -95,9 +95,28 @@
     )(cells, east_halo, west_halo, edge, courant_eastward, courant_northward, diffusivity)
 
 
-def exchange_kernel(nx, ny, payload_ref, out_ref, slots, send_sem, recv_sem):
+def mm(left, right):
+    return jnp.dot(left, right, precision=lax.Precision.HIGHEST, preferred_element_type=jnp.float32)
+
+
+def mm_nt(left, right):
+    return lax.dot_general(
+        left, right, (((1,), (1,)), ((), ())),
+        precision=lax.Precision.HIGHEST, preferred_element_type=jnp.float32,
+    )
+
+
+def analysis_kernel(
+    nx, ny, y_ref, scale_ref, obs_ref, w_ref, out_ref,
+    slots, payload, rows_t, total, carried, send_sem, recv_sem,
+):
     me_x = lax.axis_index("gx")
     me_y = lax.axis_index("gy")
+    members = y_ref.shape[1]
+    slot_count = y_ref.shape[2]
+    wide = payload.shape[2]
+    batches = y_ref.shape[0]
+    centre_k = RAD * WIDTH + RAD
 
     def inside(x, y):
         return (x >= 0) & (x < nx) & (y >= 0) & (y < ny)
@@ -119,58 +138,113 @@
 
     pl.semaphore_wait(barrier, partners)
 
-    copies = []
-    for k, (dx, dy) in enumerate(OFFSETS):
-        if dx == 0 and dy == 0:
-            continue
-        copy = pltpu.make_async_remote_copy(
-            src_ref=payload_ref,
-            dst_ref=slots.at[k],
-            send_sem=send_sem.at[k],
-            recv_sem=recv_sem.at[k],
-            device_id=(me_x - dx, me_y - dy),
-            device_id_type=pl.DeviceIdType.MESH,
-        )
-        ok = inside(me_x - dx, me_y - dy)
-
-        @pl.when(ok)
-        def _():
-            copy.start()
-
-        copies.append((k, dx, dy, copy, ok))
-
-    out_ref[RAD * WIDTH + RAD] = payload_ref[...]
-    for k, dx, dy, copy, ok in copies:
-        @pl.when(ok)
-        def _():
-            copy.wait_send()
-
-        arrives = inside(me_x + dx, me_y + dy)
-
-        @pl.when(arrives)
-        def _():
-            copy.wait_recv()
-            out_ref[k] = slots[k]
-
-        @pl.when(jnp.logical_not(arrives))
-        def _():
-            out_ref[k] = jnp.zeros(out_ref.shape[1:], out_ref.dtype)
-
-
-def gather_neighbourhood(payload, nx, ny):
+    row = lax.broadcasted_iota(jnp.int32, (members, members), 0)
+    col = lax.broadcasted_iota(jnp.int32, (members, members), 1)
+    identity = (row == col).astype(jnp.float32)
+    carried[...] = identity
+    rows_t[...] = jnp.zeros(rows_t.shape, jnp.float32)
+
+    def batch_step(b, _):
+        par = b % 2
+        sampled = mm(carried[...], y_ref[b])
+        prior_mean = jnp.mean(sampled, axis=0, keepdims=True)
+        scale = scale_ref[b]
+        scaled_rows = scale * (sampled - prior_mean)
+        innovation = scale * (obs_ref[b] - prior_mean)
+        rows_t[0:members, :] = scaled_rows
+        rows_t[members : members + 1, :] = innovation
+        payload[par] = mm_nt(scaled_rows, rows_t[...])
+
+        copies = []
+        for k, (dx, dy) in enumerate(OFFSETS):
+            if dx == 0 and dy == 0:
+                continue
+            copy = pltpu.make_async_remote_copy(
+                src_ref=payload.at[par],
+                dst_ref=slots.at[par, k],
+                send_sem=send_sem.at[par, k],
+                recv_sem=recv_sem.at[par, k],
+                device_id=(me_x - dx, me_y - dy),
+                device_id_type=pl.DeviceIdType.MESH,
+            )
+            ok = inside(me_x - dx, me_y - dy)
+
+            @pl.when(ok)
+            def _():
+                copy.start()
+
+            copies.append((k, dx, dy, copy, ok))
+
+        total[...] = jnp.zeros(total.shape, jnp.float32)
+        for k, (dx, dy) in enumerate(OFFSETS):
+            if dx == 0 and dy == 0:
+                total[...] += w_ref[k] * payload[par]
+        for k, dx, dy, copy, ok in copies:
+            @pl.when(ok)
+            def _():
+                copy.wait_send()
+
+            arrives = inside(me_x + dx, me_y + dy)
+
+            @pl.when(arrives)
+            def _():
+                copy.wait_recv()
+                total[...] += w_ref[k] * slots[par, k]
+
+        summed = total[...]
+        gram_total = summed[:, 0:members]
+        proj_block = summed[:, members : 2 * members]
+        precision_matrix = identity + gram_total / (members - 1)
+        squares = precision_matrix * precision_matrix
+        frobenius = jnp.sqrt(jnp.sum(jnp.sum(squares, axis=1, keepdims=True), axis=0, keepdims=True))
+        iterate = precision_matrix / frobenius
+
+        def ns_step(_, pair):
+            iterate, inverse = pair
+            factor = 1.5 * identity - 0.5 * mm(inverse, iterate)
+            return mm(iterate, factor), mm(factor, inverse)
+
+        pair = (iterate, identity)
+        for _i in range(NS_STEPS):
+            pair = ns_step(_i, pair)
+        iterate, inverse = pair
+        transform = inverse / jnp.sqrt(frobenius)
+        weights = mm(transform, mm(transform, proj_block)) / (members - 1)
+        mixing = transform + weights[:, 0:1]
+        mixing_t = mm_nt(identity, mixing)
+        step = 1.0 / members + mixing_t - jnp.mean(mixing_t, axis=1, keepdims=True)
+        carried[...] = mm(step, carried[...])
+        return 0
+
+    lax.fori_loop(0, batches, batch_step, 0)
+    out_ref[...] = carried[...]
+
+
+def run_analysis(y, scale, obs, weights, nx, ny):
+    batches, members, slot_count = y.shape
     count = len(OFFSETS)
+    wide = 2 * members
     return pl.pallas_call(
-        functools.partial(exchange_kernel, nx, ny),
-        out_shape=jax.ShapeDtypeStruct((count,) + payload.shape, payload.dtype),
-        in_specs=[pl.BlockSpec(memory_space=pltpu.VMEM)],
+        functools.partial(analysis_kernel, nx, ny),
+        out_shape=jax.ShapeDtypeStruct((members, members), jnp.float32),
+        in_specs=[
+            pl.BlockSpec(memory_space=pltpu.VMEM),
+            pl.BlockSpec(memory_space=pltpu.VMEM),
+            pl.BlockSpec(memory_space=pltpu.VMEM),
+            pl.BlockSpec(memory_space=pltpu.SMEM),
+        ],
         out_specs=pl.BlockSpec(memory_space=pltpu.VMEM),
         scratch_shapes=[
-            pltpu.VMEM((count,) + payload.shape, payload.dtype),
-            pltpu.SemaphoreType.DMA((count,)),
-            pltpu.SemaphoreType.DMA((count,)),
+            pltpu.VMEM((2, count, members, wide), jnp.float32),
+            pltpu.VMEM((2, members, wide), jnp.float32),
+            pltpu.VMEM((wide, slot_count), jnp.float32),
+            pltpu.VMEM((members, wide), jnp.float32),
+            pltpu.VMEM((members, members), jnp.float32),
+            pltpu.SemaphoreType.DMA((2, count)),
+            pltpu.SemaphoreType.DMA((2, count)),
         ],
         compiler_params=pltpu.CompilerParams(collective_id=0, has_side_effects=True),
-    )(payload)
+    )(y, scale, obs, weights)
 
 
 def on_device(
@@ -199,35 +273,10 @@
     centre_one = ((mask_index[:, None] == RAD) & (mask_index[None, :] == RAD)).astype(jnp.float32)
     reach_weight = jnp.maximum(reach_mask[0, 0].astype(jnp.float32), centre_one).reshape(-1)
     all_sampled = jnp.take(state, site_table.reshape(-1), axis=1).reshape(members, batches, slot_count)
-    identity = jnp.eye(members, dtype=jnp.float32)
-    carried = identity
-    half = members * members // 128
-    for batch_index in range(batches):
-        if batch_index == 0:
-            sampled = all_sampled[:, 0]
-        else:
-            sampled = matmul_full(carried, all_sampled[:, batch_index])
-        prior_mean = jnp.mean(sampled, axis=0)
-        live_slot = (slot_index < counts[batch_index]).astype(jnp.float32)
-        error_scale = 1.0 / jnp.sqrt(variance_here[batch_index])
-        scaled_rows = (live_slot * error_scale)[None, :] * (sampled - prior_mean[None, :])
-        innovation = live_slot * (observed_here[batch_index] - prior_mean) * error_scale
-        gram_here = matmul_full(scaled_rows, scaled_rows.T)
-        proj_here = matmul_full(scaled_rows, innovation[:, None])[:, 0]
-        payload = jnp.concatenate(
-            [
-                gram_here.reshape(half, 128),
-                jnp.pad(proj_here, (0, 128 - members))[None, :],
-                jnp.zeros((7, 128), jnp.float32),
-            ],
-            axis=0,
-        )
-        stack = gather_neighbourhood(payload, nx, ny)
-        gram_total = jnp.sum(reach_weight[:, None, None] * stack[:, :half], axis=0).reshape(members, members)
-        proj_total = jnp.sum(reach_weight[:, None] * stack[:, half, :members], axis=0)
-        mixing = mixing_matrix(gram_total, proj_total)
-        step = 1.0 / members + mixing.T - jnp.mean(mixing, axis=0)[:, None]
-        carried = step if batch_index == 0 else matmul_full(step, carried)
+    y = jnp.transpose(all_sampled, (1, 0, 2))
+    live_slot = (slot_index[None, :] < counts[:, None]).astype(jnp.float32)
+    scale = (live_slot * (1.0 / jnp.sqrt(variance_here)))[:, None, :]
+    carried = run_analysis(y, scale, observed_here[:, None, :], reach_weight, nx, ny)
     analysis = matmul_full(carried, state)
     return analysis.reshape(forecast.shape)
 

time: 192 us -> 166 us (0.86)
  the two profiles are of different devices: /device:TPU:86 before, /device:TPU:96 now
where the time goes in v2:
time: 166 us; the launch traced here: 164 us
  Pallas kernels  92 us (55%)
  local copies, waits for them, and re-layouts  31.5 us (19%)
  matrix products  22 us (13%)
  starting transfers between devices  13.1 us (8%)
  waiting for transfers between devices  3.33 us (2%)
  other arithmetic  1.98 us (1%)
    pallas_call x1, Pallas kernels, run_analysis(): pl.pallas_call(functools.partial(analysis_kernel, nx, ny), out_shape=jax....  82.9 us
    unnamed x14, local copies, waits for them, and re-layouts  12.2 us
    pallas_call x1, Pallas kernels, forecast_step(): pl.pallas_call(stencil_kernel, out_shape=jax.ShapeDtypeStruct(cells.shape...  9.12 us
    dot_general x1, matrix products, forecast_step(): jnp.einsum('abcil,sl->sabci', cells, pick, precision=lax.Precision.HIGHES...  8.5 us
    dot_general x1, matrix products, matmul_full(): jnp.dot(left, right, precision=lax.Precision.HIGHEST, preferred_element_t...  8.41 us
    reshape x1, local copies, waits for them, and re-layouts, on_device(): state = forecast.reshape(members, -1)  6.9 us
    ppermute x1, starting transfers between devices, forecast_step(): lax.ppermute(cells[:, :, :, 0:1, :], 'gx', [(i + 1, i) for i in range(nx...  6.66 us
    dot_general x1, matrix products, forecast_step(): jnp.einsum('sabci,sl->abcil', jnp.stack([north_halo, south_halo]), place,...  5.07 us
  transfers between devices with their start and end apart: 4, of which 1 were waited for; matrix products, arithmetic and copies ran while one was open for 6% of the time, Pallas kernels for 0%

profile of v2, /device:TPU:96, one launch (start us, length us, event | category | flops | bytes accessed | tf_op | source)
XLA Modules:
  0.0 164.1 jit_solution(12766280067829555543)
XLA Ops:
  0.0 0.0 copy-start.5
  0.0 8.5 %fusion.2 = f32[2,64,2,4,16]{1,0,4,3,2:T(2,128)S(1)} fusion(f32[64,2,4,16,128]{4,3,2,1,0:T(8,128)} %x_ref.1, pred[1,128]{1,0:T(4,128)(4,1)S(1)} %get-tuple-element.11, pred[1,128]{1,0:T(4,128)(4,1)S(1)} %get-tuple-element.12), kind=kOutput, calls=%fused_computation.4 | convolution fusion | flops 25166080 | bytes 4260096 | tf_op jit(solution)/shard_map/abcil,sl->sabci/dot_general | solution.py:69
  8.5 0.1 fusion.14
  8.7 1.9 %collective-permute-start.2 = (f32[64,2,4,16]{0,3,2,1:T(8,128)S(1)}, f32[64,2,4,16]{0,3,2,1:T(8,128)S(1)}, u32[]{:S(2)}, u32[]{:S(2)}) collective-permute-start(f32[64,2,4,16]{0,3,2,1:T(8,128)S(1)} %bitcast.56), channel_id=1, source_target_pairs={{1,0},{2,1},{3,2},{4,3},{5,4},{6,5},{7,6},{9,8},{10,9},{11,10},{12... | collective-permute-start | bytes 98312 | tf_op jit(solution)/shard_map/ppermute | solution.py:73
  10.6 2.4 %collective-permute-start.3 = (f32[64,2,4,16]{0,3,2,1:T(8,128)S(1)}, f32[64,2,4,16]{0,3,2,1:T(8,128)S(1)}, u32[]{:S(2)}, u32[]{:S(2)}) collective-permute-start(f32[64,2,4,16]{0,3,2,1:T(8,128)S(1)} %bitcast.54), channel_id=1, source_target_pairs={{0,1},{1,2},{2,3},{3,4},{4,5},{5,6},{6,7},{8,9},{9,10},{10,11},{11... | collective-permute-start | bytes 98312 | tf_op jit(solution)/shard_map/ppermute | solution.py:74
  13.0 2.8 %fusion.13 = (f32[64,2,4,1,128]{4,3,2,1,0:T(1,128)S(1)}, f32[64,2,4,1,128]{4,3,2,1,0:T(1,128)S(1)}) fusion(f32[64,2,4,16,128]{4,3,2,1,0:T(8,128)} %x_ref.1), kind=kLoop, calls=%fused_computation.29 | loop fusion | bytes 1048576 | tf_op jit(solution)/shard_map/slice | solution.py:65
  15.8 6.7 %collective-permute-start = (f32[64,2,4,1,128]{4,3,2,1,0:T(1,128)S(1)}, f32[64,2,4,1,128]{4,3,2,1,0:T(1,128)S(1)}, u32[]{:S(2)}, u32[]{:S(2)}) collective-permute-start(f32[64,2,4,1,128]{4,3,2,1,0:T(1,128)S(1)} %get-tuple-element.8), channel_id=1, source_target_pairs={{8,0},{16,8},{24,16},{32,24},{40,32},{48,40},{56,48},{64,56},{72,6... | collective-permute-start | bytes 786440 | tf_op jit(solution)/shard_map/ppermute | solution.py:64
  22.5 2.1 %collective-permute-start.1 = (f32[64,2,4,1,128]{4,3,2,1,0:T(1,128)S(1)}, f32[64,2,4,1,128]{4,3,2,1,0:T(1,128)S(1)}, u32[]{:S(2)}, u32[]{:S(2)}) collective-permute-start(f32[64,2,4,1,128]{4,3,2,1,0:T(1,128)S(1)} %get-tuple-element.7), channel_id=1, source_target_pairs={{0,8},{8,16},{16,24},{24,32},{32,40},{40,48},{48,56},{56,64},{64,7... | collective-permute-start | bytes 786440 | tf_op jit(solution)/shard_map/ppermute | solution.py:65
  24.6 0.0 copy-done.2
  24.6 0.1 and_convert_fusion
  24.7 0.0 copy-done.3
  24.7 0.7 compare_select_fusion.1.scale_ref
  25.4 0.1 reshape.131
  25.5 0.1 convert_element_type.18
  25.6 0.5 max.4.w_ref
  26.1 0.0 collective-permute-done.2
  26.1 0.0 collective-permute-done.3
  26.1 0.4 copy.17
  26.6 5.1 %fusion.7.edge_ref = f32[64,2,4,16,128]{4,3,2,1,0:T(8,128)} fusion(f32[2,64,2,4,16]{4,0,3,2,1:T(2,128)S(1)} %copy.17, pred[1,128]{1,0:T(4,128)(4,1)S(1)} %get-tuple-element.12, pred[1,128]{1,0:T(4,128)(4,1)S(1)} %get-tuple-element.11), kind=kOutput, calls=%fused_computation.19 | convolution fusion | flops 25166080 | bytes 4260096 | tf_op jit(solution)/shard_map/sabci,sl->abcil/dot_general | solution.py:75
  31.6 0.0 collective-permute-done.east_ref
  31.6 3.3 %collective-permute-done.1.west_ref = f32[64,2,4,1,128]{4,3,2,1,0:T(1,128)S(1)} collective-permute-done((f32[64,2,4,1,128]{4,3,2,1,0:T(1,128)S(1)}, f32[64,2,4,1,128]{4,3,2,1,0:T(1,128)S(1)}, u32[]{:S(2)}, u32[]{:S(2)}) %collective-permute-start.1) | collective-permute-done | bytes 262176 | tf_op jit(solution)/shard_map/ppermute | solution.py:65
  35.0 0.7 copy-done.1
  35.7 9.1 %shard_map.91 = f32[64,2,4,16,128]{4,3,2,1,0:T(8,128)} custom-call(f32[64,2,4,16,128]{4,3,2,1,0:T(8,128)} %x_ref.1, f32[64,2,4,1,128]{4,3,2,1,0:T(1,128)} %copy-done, f32[64,2,4,1,128]{4,3,2,1,0:T(1,128)} %copy-done.1, f32[64,2,4,16,128]{4,3,2,1,0:T(8,128)} %fusion.7.edge_ref, f32[2,16,128]{2,1,0:T(8,128)} %u_ref.1, f32[2,16,128]{2,1,0:T(8,128)} %v_ref.1, ...), custom_call_target="tpu_custom_call" | custom-call | tf_op jit(solution)/shard_map/pallas_call | solution.py:85
  44.8 6.6 %copy.38 = f32[8,8,128,128]{3,1,2,0:T(8,128)} copy(f32[8,8,128,128]{3,2,1,0:T(8,128)} %bitcast.52) | data formatting | bytes 8388608
  51.4 6.9 %copy.18 = f32[64,16384]{0,1:T(8,128)} copy(f32[64,16384]{1,0:T(8,128)} %bitcast.50) | data formatting | bytes 8388608 | tf_op jit(solution)/shard_map/reshape | solution.py:265
  58.3 4.4 %gather_fusion = f32[512,64]{1,0:T(8,128)S(1)} fusion(f32[64,16384]{0,1:T(8,128)} %copy.18, s32[1024]{0:T(1024)S(1)} %pad_clamp_fusion), kind=kCustom, calls=%fused_computation | custom fusion | bytes 264192 | tf_op jit(solution)/shard_map/jit(_take)/gather | solution.py:275
  62.7 0.1 copy.20
  62.8 4.9 %copy.30 = f32[8,8,128,128]{3,2,1,0:T(8,128)} copy(f32[8,8,128,128]{3,1,2,0:T(8,128)} %copy.38) | data formatting | bytes 8388608
  67.7 0.7 select_bitcast_fusion.y_ref
  68.3 82.9 %shard_map.92 = f32[64,64]{1,0:T(8,128)} custom-call(f32[4,64,128]{2,1,0:T(8,128)} %select_bitcast_fusion.y_ref, f32[4,1,128]{2,1,0:T(1,128)} %compare_select_fusion.1.scale_ref, f32[4,1,128]{2,1,0:T(1,128)} %bitcast.61, f32[25]{0:T(128)} %max.4.w_ref), custom_call_target="tpu_custom_call" | custom-call | tf_op jit(solution)/shard_map/pallas_call | solution.py:227
  151.3 8.4 %fusion = f32[64,2,4,16,128]{4,0,3,2,1:T(8,128)S(1)} fusion(f32[2,4,16,128,64]{3,2,1,0,4:T(8,128)} %bitcast.51, f32[64,64]{1,0:T(8,128)} %shard_map.92), kind=kOutput, calls=%fused_computation.2 | convolution fusion | flops 805306368 | bytes 8404992 | tf_op jit(solution)/shard_map/dot_general | solution.py:18
  159.7 4.4 %copy.22 = f32[64,2,4,16,128]{4,3,2,1,0:T(8,128)} copy(f32[64,2,4,16,128]{4,0,3,2,1:T(8,128)S(1)} %fusion) | data formatting | bytes 8388608 | tf_op jit(solution)/shard_map/dot_general | solution.py:18
  (16 shorter events, 0.1 us)
Async XLA Ops:
  0.0 24.6 %copy-start.2 = (s32[1,1,4,128]{3,2,1,0:T(4,128)S(1)}, s32[1,1,4,128]{3,2,1,0:T(4,128)}, u32[]{:S(2)}) copy-start(s32[1,1,4,128]{3,2,1,0:T(4,128)} %param.13) | copy-start | bytes 6148
  0.0 24.7 %copy-start.3 = (s32[1,1,5,5]{3,1,2,0:T(1,128)S(1)}, s32[1,1,5,5]{3,1,2,0:T(1,128)}, u32[]{:S(2)}) copy-start(s32[1,1,5,5]{3,1,2,0:T(1,128)} %param.17) | copy-start | bytes 304
  0.0 24.7 %copy-start.4 = (f32[1,1,4,128]{3,2,1,0:T(4,128)S(1)}, f32[1,1,4,128]{3,2,1,0:T(4,128)}, u32[]{:S(2)}) copy-start(f32[1,1,4,128]{3,2,1,0:T(4,128)} %param.16) | copy-start | bytes 6148
  0.0 24.7 %copy-start.5 = (s32[1,1,4]{2,1,0:T(1,128)S(1)}, s32[1,1,4]{2,1,0:T(1,128)}, u32[]{:S(2)}) copy-start(s32[1,1,4]{2,1,0:T(1,128)} %param.14) | copy-start | bytes 52
  8.7 17.4 %collective-permute-start.2 = (f32[64,2,4,16]{0,3,2,1:T(8,128)S(1)}, f32[64,2,4,16]{0,3,2,1:T(8,128)S(1)}, u32[]{:S(2)}, u32[]{:S(2)}) collective-permute-start(f32[64,2,4,16]{0,3,2,1:T(8,128)S(1)} %bitcast.56), channel_id=1, source_target_pairs={{1,0},{2,1},{3,2},{4,3},{5,4},{6,5},{7,6},{9,8},{10,9},{11,10},{12... | collective-permute-start | bytes 98312 | tf_op jit(solution)/shard_map/ppermute | solution.py:73
  10.6 15.5 %collective-permute-start.3 = (f32[64,2,4,16]{0,3,2,1:T(8,128)S(1)}, f32[64,2,4,16]{0,3,2,1:T(8,128)S(1)}, u32[]{:S(2)}, u32[]{:S(2)}) collective-permute-start(f32[64,2,4,16]{0,3,2,1:T(8,128)S(1)} %bitcast.54), channel_id=1, source_target_pairs={{0,1},{1,2},{2,3},{3,4},{4,5},{5,6},{6,7},{8,9},{9,10},{10,11},{11... | collective-permute-start | bytes 98312 | tf_op jit(solution)/shard_map/ppermute | solution.py:74
  15.8 15.8 %collective-permute-start = (f32[64,2,4,1,128]{4,3,2,1,0:T(1,128)S(1)}, f32[64,2,4,1,128]{4,3,2,1,0:T(1,128)S(1)}, u32[]{:S(2)}, u32[]{:S(2)}) collective-permute-start(f32[64,2,4,1,128]{4,3,2,1,0:T(1,128)S(1)} %get-tuple-element.8), channel_id=1, source_target_pairs={{8,0},{16,8},{24,16},{32,24},{40,32},{48,40},{56,48},{64,56},{72,6... | collective-permute-start | bytes 786440 | tf_op jit(solution)/shard_map/ppermute | solution.py:64
  22.5 12.5 %collective-permute-start.1 = (f32[64,2,4,1,128]{4,3,2,1,0:T(1,128)S(1)}, f32[64,2,4,1,128]{4,3,2,1,0:T(1,128)S(1)}, u32[]{:S(2)}, u32[]{:S(2)}) collective-permute-start(f32[64,2,4,1,128]{4,3,2,1,0:T(1,128)S(1)} %get-tuple-element.7), channel_id=1, source_target_pairs={{0,8},{8,16},{16,24},{24,32},{32,40},{40,48},{48,56},{56,64},{64,7... | collective-permute-start | bytes 786440 | tf_op jit(solution)/shard_map/ppermute | solution.py:65
  31.6 3.3 %copy-start = (f32[64,2,4,1,128]{4,3,2,1,0:T(1,128)}, f32[64,2,4,1,128]{4,3,2,1,0:T(1,128)S(1)}, u32[]{:S(2)}) copy-start(f32[64,2,4,1,128]{4,3,2,1,0:T(1,128)S(1)} %collective-permute-done.east_ref) | copy-start | bytes 786436
  35.0 0.7 copy-start.1

commit v3 on v2

--- a/solution.py
+++ b/solution.py
@@ -34,7 +34,7 @@
     return transform + weights[:, None]
 
 
-def stencil_kernel(x_ref, east_ref, west_ref, edge_ref, u_ref, v_ref, d_ref, o_ref, east_scr, west_scr):
+def stencil_kernel(x_ref, east_ref, west_ref, edge_ref, u_ref, v_ref, d_ref, col_ref, row_ref, o_ref, s_ref, east_scr, west_scr):
     rows = x_ref.shape[3]
     lanes = x_ref.shape[4]
     east_scr[:, :, :, 0 : rows - 1, :] = x_ref[:, :, :, 1:rows, :]
@@ -54,10 +54,23 @@
     flux_x = jnp.maximum(u, 0.0) * (centre - west_cell) + jnp.minimum(u, 0.0) * (east_cell - centre)
     flux_y = jnp.maximum(v, 0.0) * (centre - south_cell) + jnp.minimum(v, 0.0) * (north_cell - centre)
     spread_term = d * (east_cell + west_cell + north_cell + south_cell - 4.0 * centre)
-    o_ref[...] = centre + spread_term - flux_x - flux_y
-
-
-def forecast_step(cells, courant_eastward, courant_northward, diffusivity):
+    result = centre + spread_term - flux_x - flux_y
+    o_ref[...] = result
+    block, rows_all = result.shape[0], result.shape[1] * result.shape[2] * rows
+    flat = result.reshape(block * rows_all, lanes)
+    high = flat.astype(jnp.bfloat16)
+    rest = flat - high.astype(jnp.float32)
+    mid = rest.astype(jnp.bfloat16)
+    low = (rest - mid.astype(jnp.float32)).astype(jnp.bfloat16)
+    pick = col_ref[...]
+    picked = jnp.dot(high, pick, preferred_element_type=jnp.float32)
+    picked = picked + jnp.dot(mid, pick, preferred_element_type=jnp.float32)
+    picked = picked + jnp.dot(low, pick, preferred_element_type=jnp.float32)
+    picked = picked.reshape(block, rows_all, picked.shape[-1]) * row_ref[...][None]
+    s_ref[...] = jnp.sum(picked, axis=1)
+
+
+def forecast_step(cells, courant_eastward, courant_northward, diffusivity, sites):
     nx = lax.axis_size("gx")
     ny = lax.axis_size("gy")
     rows, lanes = cells.shape[3], cells.shape[4]
@@ -82,17 +95,26 @@
     thin = pl.BlockSpec((block,) + cells.shape[1:3] + (1, lanes), lambda i: (i, 0, 0, 0, 0))
     whole3 = pl.BlockSpec(courant_eastward.shape, lambda i: (0, 0, 0))
     whole2 = pl.BlockSpec(diffusivity.shape, lambda i: (0, 0))
+    site_count = sites.shape[0]
+    rows_all = cells.shape[1] * cells.shape[2] * rows
+    col_pick = (sites[None, :] % lanes == jnp.arange(lanes)[:, None]).astype(jnp.bfloat16)
+    row_pick = (sites[None, :] // lanes == jnp.arange(rows_all)[:, None]).astype(jnp.float32)
+    picks = pl.BlockSpec((lanes, site_count), lambda i: (0, 0))
     return pl.pallas_call(
         stencil_kernel,
-        out_shape=jax.ShapeDtypeStruct(cells.shape, cells.dtype),
+        out_shape=(
+            jax.ShapeDtypeStruct(cells.shape, cells.dtype),
+            jax.ShapeDtypeStruct((members, site_count), cells.dtype),
+        ),
         grid=(members // block,),
-        in_specs=[big, thin, thin, big, whole3, whole3, whole2],
-        out_specs=big,
+        in_specs=[big, thin, thin, big, whole3, whole3, whole2, picks,
+                  pl.BlockSpec((rows_all, site_count), lambda i: (0, 0))],
+        out_specs=(big, pl.BlockSpec((block, site_count), lambda i: (i, 0))),
         scratch_shapes=[
             pltpu.VMEM((block,) + cells.shape[1:], cells.dtype),
             pltpu.VMEM((block,) + cells.shape[1:], cells.dtype),
         ],
-    )(cells, east_halo, west_halo, edge, courant_eastward, courant_northward, diffusivity)
+    )(cells, east_halo, west_halo, edge, courant_eastward, courant_northward, diffusivity, col_pick, row_pick)
 
 
 def mm(left, right):
@@ -247,6 +269,30 @@
     )(y, scale, obs, weights)
 
 
+def transform_kernel(k_ref, x_ref, o_ref):
+    members, rows, lanes = x_ref.shape[0], x_ref.shape[3], x_ref.shape[4]
+    sub = 8
+    parts = [x_ref[:, 0, 0, h * sub : (h + 1) * sub, :].reshape(members * sub, lanes) for h in range(rows // sub)]
+    mixed = jnp.dot(k_ref[...], jnp.concatenate(parts, axis=1),
+                    precision=lax.Precision.HIGHEST, preferred_element_type=jnp.float32)
+    for h in range(rows // sub):
+        o_ref[:, 0, 0, h * sub : (h + 1) * sub, :] = mixed[:, h * lanes : (h + 1) * lanes].reshape(members, sub, lanes)
+
+
+def apply_transform(carried, cells):
+    members, levels, fields, rows, lanes = cells.shape
+    sub = 8
+    kron = (carried[:, None, :, None] * jnp.eye(sub, dtype=jnp.float32)[None, :, None, :]).reshape(members * sub, members * sub)
+    block = pl.BlockSpec((members, 1, 1, rows, lanes), lambda a, b: (0, a, b, 0, 0))
+    return pl.pallas_call(
+        transform_kernel,
+        out_shape=jax.ShapeDtypeStruct(cells.shape, cells.dtype),
+        grid=(levels, fields),
+        in_specs=[pl.BlockSpec((members * sub, members * sub), lambda a, b: (0, 0)), block],
+        out_specs=block,
+    )(kron, cells)
+
+
 def on_device(
     background_sample,
     courant_eastward,
@@ -260,10 +306,11 @@
 ):
     nx = lax.axis_size("gx")
     ny = lax.axis_size("gy")
-    forecast = forecast_step(background_sample, courant_eastward, courant_northward, diffusivity)
+    site_table = sample_site[0, 0]
+    forecast, gathered = forecast_step(
+        background_sample, courant_eastward, courant_northward, diffusivity, site_table.reshape(-1)
+    )
     members = forecast.shape[0]
-    state = forecast.reshape(members, -1)
-    site_table = sample_site[0, 0]
     counts = live_count[0, 0]
     observed_here = observed[0, 0]
     variance_here = error_variance[0, 0]
@@ -272,13 +319,12 @@
     mask_index = jnp.arange(WIDTH)
     centre_one = ((mask_index[:, None] == RAD) & (mask_index[None, :] == RAD)).astype(jnp.float32)
     reach_weight = jnp.maximum(reach_mask[0, 0].astype(jnp.float32), centre_one).reshape(-1)
-    all_sampled = jnp.take(state, site_table.reshape(-1), axis=1).reshape(members, batches, slot_count)
+    all_sampled = gathered.reshape(members, batches, slot_count)
     y = jnp.transpose(all_sampled, (1, 0, 2))
     live_slot = (slot_index[None, :] < counts[:, None]).astype(jnp.float32)
     scale = (live_slot * (1.0 / jnp.sqrt(variance_here)))[:, None, :]
     carried = run_analysis(y, scale, observed_here[:, None, :], reach_weight, nx, ny)
-    analysis = matmul_full(carried, state)
-    return analysis.reshape(forecast.shape)
+    return apply_transform(carried, forecast)
 
 
 def solution(mesh):

time: 166 us -> 170 us (1.024)
  the two profiles are of different devices: /device:TPU:96 before, /device:TPU:4 now
where the time goes in v3:
time: 170 us; the launch traced here: 169 us
  Pallas kernels  114 us (67%)
  local copies, waits for them, and re-layouts  19.3 us (11%)
  matrix products  13.6 us (8%)
  starting transfers between devices  11 us (6%)
  other arithmetic  10.9 us (6%)
    pallas_call x1, Pallas kernels, run_analysis(): pl.pallas_call(functools.partial(analysis_kernel, nx, ny), out_shape=jax....  90.6 us
    mul x1, local copies, waits for them, and re-layouts, apply_transform(): carried[:, None, :, None]  13.4 us
    pallas_call x1, Pallas kernels, forecast_step(): pl.pallas_call(stencil_kernel, out_shape=(jax.ShapeDtypeStruct(cells.shap...  11.7 us
    pallas_call x1, Pallas kernels, apply_transform(): pl.pallas_call(transform_kernel, out_shape=jax.ShapeDtypeStruct(cells.sha...  11.5 us
    mul x1, other arithmetic, apply_transform(): carried[:, None, :, None]  8.7 us
    dot_general x1, matrix products, forecast_step(): jnp.einsum('abcil,sl->sabci', cells, pick, precision=lax.Precision.HIGHES...  8.5 us
    dot_general x1, matrix products, forecast_step(): jnp.einsum('sabci,sl->abcil', jnp.stack([north_halo, south_halo]), place,...  5.07 us
    ppermute x1, starting transfers between devices, forecast_step(): lax.ppermute(cells[:, :, :, 0:1, :], 'gx', [(i + 1, i) for i in range(nx...  4.47 us
  transfers between devices with their start and end apart: 4, of which 0 were waited for; matrix products, arithmetic and copies ran while one was open for 6% of the time, Pallas kernels for 0%

profile of v3, /device:TPU:4, one launch (start us, length us, event | category | flops | bytes accessed | tf_op | source)
XLA Modules:
  0.0 168.7 jit_solution(14706273710010488060)
XLA Ops:
  0.0 0.0 copy-start.5
  0.0 8.5 %fusion = f32[2,64,2,4,16]{1,0,4,3,2:T(2,128)S(1)} fusion(f32[64,2,4,16,128]{4,3,2,1,0:T(8,128)} %x_ref.1, pred[1,128]{1,0:T(4,128)(4,1)S(1)} %get-tuple-element.15, pred[1,128]{1,0:T(4,128)(4,1)S(1)} %get-tuple-element.16), kind=kOutput, calls=%fused_computation.1 | convolution fusion | flops 25166080 | bytes 4260096 | tf_op jit(solution)/shard_map/abcil,sl->sabci/dot_general | solution.py:82
  8.5 0.1 fusion.15
  8.7 1.7 %collective-permute-start.3 = (f32[64,2,4,16]{0,3,2,1:T(8,128)S(1)}, f32[64,2,4,16]{0,3,2,1:T(8,128)S(1)}, u32[]{:S(2)}, u32[]{:S(2)}) collective-permute-start(f32[64,2,4,16]{0,3,2,1:T(8,128)S(1)} %bitcast.53), channel_id=1, source_target_pairs={{0,1},{1,2},{2,3},{3,4},{4,5},{5,6},{6,7},{8,9},{9,10},{10,11},{11... | collective-permute-start | bytes 98312 | tf_op jit(solution)/shard_map/ppermute | solution.py:87
  10.4 1.3 collective-permute-start.2
  11.7 2.8 %fusion.14 = (f32[64,2,4,1,128]{4,3,2,1,0:T(1,128)S(1)}, f32[64,2,4,1,128]{4,3,2,1,0:T(1,128)S(1)}) fusion(f32[64,2,4,16,128]{4,3,2,1,0:T(8,128)} %x_ref.1), kind=kLoop, calls=%fused_computation.36 | loop fusion | bytes 1048576 | tf_op jit(solution)/shard_map/slice | solution.py:78
  14.5 3.5 %collective-permute-start.1 = (f32[64,2,4,1,128]{4,3,2,1,0:T(1,128)S(1)}, f32[64,2,4,1,128]{4,3,2,1,0:T(1,128)S(1)}, u32[]{:S(2)}, u32[]{:S(2)}) collective-permute-start(f32[64,2,4,1,128]{4,3,2,1,0:T(1,128)S(1)} %get-tuple-element.9), channel_id=1, source_target_pairs={{0,8},{8,16},{16,24},{24,32},{32,40},{40,48},{48,56},{56,64},{64,7... | collective-permute-start | bytes 786440 | tf_op jit(solution)/shard_map/ppermute | solution.py:78
  18.0 4.5 %collective-permute-start = (f32[64,2,4,1,128]{4,3,2,1,0:T(1,128)S(1)}, f32[64,2,4,1,128]{4,3,2,1,0:T(1,128)S(1)}, u32[]{:S(2)}, u32[]{:S(2)}) collective-permute-start(f32[64,2,4,1,128]{4,3,2,1,0:T(1,128)S(1)} %get-tuple-element.10), channel_id=1, source_target_pairs={{8,0},{16,8},{24,16},{32,24},{40,32},{48,40},{56,48},{64,56},{72,6... | collective-permute-start | bytes 786440 | tf_op jit(solution)/shard_map/ppermute | solution.py:77
  22.5 0.0 copy-done.4
  22.5 0.1 and_convert_fusion
  22.6 0.0 copy-done.2
  22.6 0.0 copy-done.3
  22.6 0.0 copy-done.5
  22.6 0.7 compare_select_fusion.scale_ref
  23.3 0.8 fusion.2
  24.1 0.1 reshape.188
  24.2 0.1 convert_element_type.33
  24.2 0.6 max.4.w_ref
  24.8 0.0 collective-permute-done.3
  24.8 0.0 collective-permute-done.2
  24.9 0.4 copy.15
  25.3 5.1 %fusion.9.edge_ref = f32[64,2,4,16,128]{4,3,2,1,0:T(8,128)} fusion(f32[2,64,2,4,16]{4,0,3,2,1:T(2,128)S(1)} %copy.15, pred[1,128]{1,0:T(4,128)(4,1)S(1)} %get-tuple-element.16, pred[1,128]{1,0:T(4,128)(4,1)S(1)} %get-tuple-element.15), kind=kOutput, calls=%fused_computation.27 | convolution fusion | flops 25166080 | bytes 4260096 | tf_op jit(solution)/shard_map/sabci,sl->abcil/dot_general | solution.py:88
  30.4 0.0 collective-permute-done.1.west_ref
  30.4 0.0 collective-permute-done.east_ref
  30.4 0.7 copy-done
  31.1 0.1 copy-done.1
  31.2 11.7 %shard_map.91 = (f32[64,2,4,16,128]{4,3,2,1,0:T(8,128)}, f32[64,512]{1,0:T(8,128)}) custom-call(f32[64,2,4,16,128]{4,3,2,1,0:T(8,128)} %x_ref.1, f32[64,2,4,1,128]{4,3,2,1,0:T(1,128)} %copy-done.1, f32[64,2,4,1,128]{4,3,2,1,0:T(1,128)} %copy-done, f32[64,2,4,16,128]{4,3,2,1,0:T(8,128)} %fusion.9.edge_ref, f32[2,16,128]{2,1,0:T(8,128)} %u_ref.1, ...), custom_call_target="tpu_custom_call" | custom-call | tf_op jit(solution)/shard_map/pallas_call | solution.py:103
  42.9 1.6 bitcast_bitcast_fusion.y_ref
  44.5 90.6 %shard_map.92 = f32[64,64]{1,0:T(8,128)} custom-call(f32[4,64,128]{2,1,0:T(8,128)} %bitcast_bitcast_fusion.y_ref, f32[4,1,128]{2,1,0:T(1,128)} %compare_select_fusion.scale_ref, f32[4,1,128]{2,1,0:T(1,128)} %bitcast.56, f32[25]{0:T(128)} %max.4.w_ref), custom_call_target="tpu_custom_call" | custom-call | tf_op jit(solution)/shard_map/pallas_call | solution.py:249
  135.1 8.7 %broadcast_multiply_fusion = f32[64,8,64,8]{3,2,1,0:T(8,128)} fusion(f32[8,8]{1,0:T(8,128)S(1)} %fusion.4, f32[64,64]{1,0:T(8,128)} %shard_map.92), kind=kLoop, calls=%fused_computation | loop fusion | flops 262144 | bytes 1065216 | tf_op jit(solution)/shard_map/mul | solution.py:285
  143.8 13.4 %mul.24.k_ref = f32[512,512]{1,0:T(8,128)} reshape(f32[64,8,64,8]{3,2,1,0:T(8,128)} %broadcast_multiply_fusion) | data formatting | bytes 2097152 | tf_op jit(solution)/shard_map/mul | solution.py:285
  157.3 11.5 %shard_map.93 = f32[64,2,4,16,128]{4,3,2,1,0:T(8,128)} custom-call(f32[512,512]{1,0:T(8,128)} %mul.24.k_ref, f32[64,2,4,16,128]{4,3,2,1,0:T(8,128)} %get-tuple-element.8.x_ref), custom_call_target="tpu_custom_call" | custom-call | tf_op jit(solution)/shard_map/pallas_call | solution.py:287
  (12 shorter events, 0.1 us)
Async XLA Ops:
  0.0 22.5 %copy-start.4 = (f32[1,1,4,128]{3,2,1,0:T(4,128)S(1)}, f32[1,1,4,128]{3,2,1,0:T(4,128)}, u32[]{:S(2)}) copy-start(f32[1,1,4,128]{3,2,1,0:T(4,128)} %param.16) | copy-start | bytes 6148
  0.0 22.6 %copy-start.2 = (s32[1,1,5,5]{3,1,2,0:T(1,128)S(1)}, s32[1,1,5,5]{3,1,2,0:T(1,128)}, u32[]{:S(2)}) copy-start(s32[1,1,5,5]{3,1,2,0:T(1,128)} %param.17) | copy-start | bytes 304
  0.0 22.6 %copy-start.3 = (s32[1,1,4,128]{3,2,1,0:T(4,128)S(1)}, s32[1,1,4,128]{3,2,1,0:T(4,128)}, u32[]{:S(2)}) copy-start(s32[1,1,4,128]{3,2,1,0:T(4,128)} %param.13) | copy-start | bytes 6148
  0.0 22.6 %copy-start.5 = (s32[1,1,4]{2,1,0:T(1,128)S(1)}, s32[1,1,4]{2,1,0:T(1,128)}, u32[]{:S(2)}) copy-start(s32[1,1,4]{2,1,0:T(1,128)} %param.14) | copy-start | bytes 52
  8.7 16.2 %collective-permute-start.3 = (f32[64,2,4,16]{0,3,2,1:T(8,128)S(1)}, f32[64,2,4,16]{0,3,2,1:T(8,128)S(1)}, u32[]{:S(2)}, u32[]{:S(2)}) collective-permute-start(f32[64,2,4,16]{0,3,2,1:T(8,128)S(1)} %bitcast.53), channel_id=1, source_target_pairs={{0,1},{1,2},{2,3},{3,4},{4,5},{5,6},{6,7},{8,9},{9,10},{10,11},{11... | collective-permute-start | bytes 98312 | tf_op jit(solution)/shard_map/ppermute | solution.py:87
  10.4 14.4 %collective-permute-start.2 = (f32[64,2,4,16]{0,3,2,1:T(8,128)S(1)}, f32[64,2,4,16]{0,3,2,1:T(8,128)S(1)}, u32[]{:S(2)}, u32[]{:S(2)}) collective-permute-start(f32[64,2,4,16]{0,3,2,1:T(8,128)S(1)} %bitcast.51), channel_id=1, source_target_pairs={{1,0},{2,1},{3,2},{4,3},{5,4},{6,5},{7,6},{9,8},{10,9},{11,10},{12... | collective-permute-start | bytes 98312 | tf_op jit(solution)/shard_map/ppermute | solution.py:86
  14.5 15.9 %collective-permute-start.1 = (f32[64,2,4,1,128]{4,3,2,1,0:T(1,128)S(1)}, f32[64,2,4,1,128]{4,3,2,1,0:T(1,128)S(1)}, u32[]{:S(2)}, u32[]{:S(2)}) collective-permute-start(f32[64,2,4,1,128]{4,3,2,1,0:T(1,128)S(1)} %get-tuple-element.9), channel_id=1, source_target_pairs={{0,8},{8,16},{16,24},{24,32},{32,40},{40,48},{48,56},{56,64},{64,7... | collective-permute-start | bytes 786440 | tf_op jit(solution)/shard_map/ppermute | solution.py:78
  18.0 12.4 %collective-permute-start = (f32[64,2,4,1,128]{4,3,2,1,0:T(1,128)S(1)}, f32[64,2,4,1,128]{4,3,2,1,0:T(1,128)S(1)}, u32[]{:S(2)}, u32[]{:S(2)}) collective-permute-start(f32[64,2,4,1,128]{4,3,2,1,0:T(1,128)S(1)} %get-tuple-element.10), channel_id=1, source_target_pairs={{8,0},{16,8},{24,16},{32,24},{40,32},{48,40},{56,48},{64,56},{72,6... | collective-permute-start | bytes 786440 | tf_op jit(solution)/shard_map/ppermute | solution.py:77
  30.4 0.7 copy-start
  30.4 0.8 copy-start.1

commit v4 on v3

--- a/solution.py
+++ b/solution.py
@@ -269,11 +269,26 @@
     )(y, scale, obs, weights)
 
 
-def transform_kernel(k_ref, x_ref, o_ref):
+def transform_kernel(p_ref, x_ref, o_ref, k_scr):
     members, rows, lanes = x_ref.shape[0], x_ref.shape[3], x_ref.shape[4]
     sub = 8
-    parts = [x_ref[:, 0, 0, h * sub : (h + 1) * sub, :].reshape(members * sub, lanes) for h in range(rows // sub)]
-    mixed = jnp.dot(k_ref[...], jnp.concatenate(parts, axis=1),
+    size = members * sub
+
+    @pl.when((pl.program_id(0) == 0) & (pl.program_id(1) == 0))
+    def _():
+        spread = (
+            lax.broadcasted_iota(jnp.int32, (size, members), 0) // sub
+            == lax.broadcasted_iota(jnp.int32, (size, members), 1)
+        ).astype(jnp.float32)
+        full = mm_nt(mm(spread, p_ref[...]), spread)
+        same = (
+            lax.broadcasted_iota(jnp.int32, (size, size), 0) % sub
+            == lax.broadcasted_iota(jnp.int32, (size, size), 1) % sub
+        )
+        k_scr[...] = jnp.where(same, full, 0.0)
+
+    parts = [x_ref[:, 0, 0, h * sub : (h + 1) * sub, :].reshape(size, lanes) for h in range(rows // sub)]
+    mixed = jnp.dot(k_scr[...], jnp.concatenate(parts, axis=1),
                     precision=lax.Precision.HIGHEST, preferred_element_type=jnp.float32)
     for h in range(rows // sub):
         o_ref[:, 0, 0, h * sub : (h + 1) * sub, :] = mixed[:, h * lanes : (h + 1) * lanes].reshape(members, sub, lanes)
@@ -282,15 +297,16 @@
 def apply_transform(carried, cells):
     members, levels, fields, rows, lanes = cells.shape
     sub = 8
-    kron = (carried[:, None, :, None] * jnp.eye(sub, dtype=jnp.float32)[None, :, None, :]).reshape(members * sub, members * sub)
     block = pl.BlockSpec((members, 1, 1, rows, lanes), lambda a, b: (0, a, b, 0, 0))
     return pl.pallas_call(
         transform_kernel,
         out_shape=jax.ShapeDtypeStruct(cells.shape, cells.dtype),
         grid=(levels, fields),
-        in_specs=[pl.BlockSpec((members * sub, members * sub), lambda a, b: (0, 0)), block],
+        in_specs=[pl.BlockSpec((members, members), lambda a, b: (0, 0)), block],
         out_specs=block,
-    )(kron, cells)
+        scratch_shapes=[pltpu.VMEM((members * sub, members * sub), jnp.float32)],
+        compiler_params=pltpu.CompilerParams(dimension_semantics=("arbitrary", "arbitrary")),
+    )(carried, cells)
 
 
 def on_device(

time: 170 us -> 146 us (0.86)
  the two profiles are of different devices: /device:TPU:4 before, /device:TPU:96 now
where the time goes in v4:
time: 146 us; the launch traced here: 145 us
  Pallas kernels  108 us (74%)
  matrix products  13.6 us (9%)
  starting transfers between devices  12.9 us (9%)
  local copies, waits for them, and re-layouts  5.78 us (4%)
  waiting for transfers between devices  2.74 us (2%)
  other arithmetic  2.11 us (1%)
    pallas_call x1, Pallas kernels, run_analysis(): pl.pallas_call(functools.partial(analysis_kernel, nx, ny), out_shape=jax....  83.3 us
    pallas_call x1, Pallas kernels, apply_transform(): pl.pallas_call(transform_kernel, out_shape=jax.ShapeDtypeStruct(cells.sha...  12.7 us
    pallas_call x1, Pallas kernels, forecast_step(): pl.pallas_call(stencil_kernel, out_shape=(jax.ShapeDtypeStruct(cells.shap...  11.8 us
    dot_general x1, matrix products, forecast_step(): jnp.einsum('abcil,sl->sabci', cells, pick, precision=lax.Precision.HIGHES...  8.5 us
    ppermute x1, starting transfers between devices, forecast_step(): lax.ppermute(cells[:, :, :, 0:1, :], 'gx', [(i + 1, i) for i in range(nx...  6.66 us
    dot_general x1, matrix products, forecast_step(): jnp.einsum('sabci,sl->abcil', jnp.stack([north_halo, south_halo]), place,...  5.07 us
  transfers between devices with their start and end apart: 4, of which 1 were waited for; matrix products, arithmetic and copies ran while one was open for 7% of the time, Pallas kernels for 0%

profile of v4, /device:TPU:96, one launch (start us, length us, event | category | flops | bytes accessed | tf_op | source)
XLA Modules:
  0.0 144.9 jit_solution(6644502219203003469)
XLA Ops:
  0.0 0.0 copy-start.3
  0.0 0.0 copy-start.4
  0.0 0.0 copy-start.2
  0.0 8.5 %fusion = f32[2,64,2,4,16]{1,0,4,3,2:T(2,128)S(1)} fusion(f32[64,2,4,16,128]{4,3,2,1,0:T(8,128)} %x_ref.1, pred[1,128]{1,0:T(4,128)(4,1)S(1)} %get-tuple-element.15, pred[1,128]{1,0:T(4,128)(4,1)S(1)} %get-tuple-element.16), kind=kOutput, calls=%fused_computation | convolution fusion | flops 25166080 | bytes 4260096 | tf_op jit(solution)/shard_map/abcil,sl->sabci/dot_general | solution.py:82
  8.5 0.1 fusion.14
  8.7 1.9 %collective-permute-start.2 = (f32[64,2,4,16]{0,3,2,1:T(8,128)S(1)}, f32[64,2,4,16]{0,3,2,1:T(8,128)S(1)}, u32[]{:S(2)}, u32[]{:S(2)}) collective-permute-start(f32[64,2,4,16]{0,3,2,1:T(8,128)S(1)} %bitcast.51), channel_id=1, source_target_pairs={{1,0},{2,1},{3,2},{4,3},{5,4},{6,5},{7,6},{9,8},{10,9},{11,10},{12... | collective-permute-start | bytes 98312 | tf_op jit(solution)/shard_map/ppermute | solution.py:86
  10.6 2.4 %collective-permute-start.3 = (f32[64,2,4,16]{0,3,2,1:T(8,128)S(1)}, f32[64,2,4,16]{0,3,2,1:T(8,128)S(1)}, u32[]{:S(2)}, u32[]{:S(2)}) collective-permute-start(f32[64,2,4,16]{0,3,2,1:T(8,128)S(1)} %bitcast.49), channel_id=1, source_target_pairs={{0,1},{1,2},{2,3},{3,4},{4,5},{5,6},{6,7},{8,9},{9,10},{10,11},{11... | collective-permute-start | bytes 98312 | tf_op jit(solution)/shard_map/ppermute | solution.py:87
  13.0 2.8 %fusion.13 = (f32[64,2,4,1,128]{4,3,2,1,0:T(1,128)S(1)}, f32[64,2,4,1,128]{4,3,2,1,0:T(1,128)S(1)}) fusion(f32[64,2,4,16,128]{4,3,2,1,0:T(8,128)} %x_ref.1), kind=kLoop, calls=%fused_computation.33 | loop fusion | bytes 1048576 | tf_op jit(solution)/shard_map/slice | solution.py:78
  15.8 6.7 %collective-permute-start = (f32[64,2,4,1,128]{4,3,2,1,0:T(1,128)S(1)}, f32[64,2,4,1,128]{4,3,2,1,0:T(1,128)S(1)}, u32[]{:S(2)}, u32[]{:S(2)}) collective-permute-start(f32[64,2,4,1,128]{4,3,2,1,0:T(1,128)S(1)} %get-tuple-element.10), channel_id=1, source_target_pairs={{8,0},{16,8},{24,16},{32,24},{40,32},{48,40},{56,48},{64,56},{72,6... | collective-permute-start | bytes 786440 | tf_op jit(solution)/shard_map/ppermute | solution.py:77
  22.5 1.9 %collective-permute-start.1 = (f32[64,2,4,1,128]{4,3,2,1,0:T(1,128)S(1)}, f32[64,2,4,1,128]{4,3,2,1,0:T(1,128)S(1)}, u32[]{:S(2)}, u32[]{:S(2)}) collective-permute-start(f32[64,2,4,1,128]{4,3,2,1,0:T(1,128)S(1)} %get-tuple-element.9), channel_id=1, source_target_pairs={{0,8},{8,16},{16,24},{24,32},{32,40},{40,48},{48,56},{56,64},{64,7... | collective-permute-start | bytes 786440 | tf_op jit(solution)/shard_map/ppermute | solution.py:78
  24.4 0.0 copy-done.3
  24.4 0.1 and_convert_fusion
  24.5 0.0 copy-done.4
  24.5 0.8 fusion.2
  25.3 0.0 copy-done.5
  25.3 0.6 compare_select_fusion.scale_ref
  26.0 0.0 copy-done.2
  26.0 0.1 reshape.175
  26.1 0.1 convert_element_type.26
  26.1 0.5 max.4.w_ref
  26.7 0.0 collective-permute-done.2
  26.7 0.0 collective-permute-done.3
  26.7 0.4 copy.15
  27.1 5.1 %fusion.8.edge_ref = f32[64,2,4,16,128]{4,3,2,1,0:T(8,128)} fusion(f32[2,64,2,4,16]{4,0,3,2,1:T(2,128)S(1)} %copy.15, pred[1,128]{1,0:T(4,128)(4,1)S(1)} %get-tuple-element.16, pred[1,128]{1,0:T(4,128)(4,1)S(1)} %get-tuple-element.15), kind=kOutput, calls=%fused_computation.24 | convolution fusion | flops 25166080 | bytes 4260096 | tf_op jit(solution)/shard_map/sabci,sl->abcil/dot_general | solution.py:88
  32.2 0.0 collective-permute-done.east_ref
  32.2 2.7 %collective-permute-done.1.west_ref = f32[64,2,4,1,128]{4,3,2,1,0:T(1,128)S(1)} collective-permute-done((f32[64,2,4,1,128]{4,3,2,1,0:T(1,128)S(1)}, f32[64,2,4,1,128]{4,3,2,1,0:T(1,128)S(1)}, u32[]{:S(2)}, u32[]{:S(2)}) %collective-permute-start.1) | collective-permute-done | bytes 262176 | tf_op jit(solution)/shard_map/ppermute | solution.py:78
  35.0 0.0 copy-done
  35.0 0.7 copy-done.1
  35.7 11.8 %shard_map.91 = (f32[64,2,4,16,128]{4,3,2,1,0:T(8,128)}, f32[64,512]{1,0:T(8,128)}) custom-call(f32[64,2,4,16,128]{4,3,2,1,0:T(8,128)} %x_ref.1, f32[64,2,4,1,128]{4,3,2,1,0:T(1,128)} %copy-done, f32[64,2,4,1,128]{4,3,2,1,0:T(1,128)} %copy-done.1, f32[64,2,4,16,128]{4,3,2,1,0:T(8,128)} %fusion.8.edge_ref, f32[2,16,128]{2,1,0:T(8,128)} %u_ref.1, ...), custom_call_target="tpu_custom_call" | custom-call | tf_op jit(solution)/shard_map/pallas_call | solution.py:103
  47.4 1.6 %bitcast_bitcast_fusion.y_ref = f32[4,64,128]{2,1,0:T(8,128)} fusion(f32[64,512]{1,0:T(8,128)} %get-tuple-element.7), kind=kLoop, calls=%fused_computation.6 | loop fusion | bytes 262144 | tf_op jit(solution)/shard_map/transpose | solution.py:339
  49.0 83.3 %shard_map.92.p_ref = f32[64,64]{1,0:T(8,128)} custom-call(f32[4,64,128]{2,1,0:T(8,128)} %bitcast_bitcast_fusion.y_ref, f32[4,1,128]{2,1,0:T(1,128)} %compare_select_fusion.scale_ref, f32[4,1,128]{2,1,0:T(1,128)} %bitcast.54, f32[25]{0:T(128)} %max.4.w_ref), custom_call_target="tpu_custom_call" | custom-call | tf_op jit(solution)/shard_map/pallas_call | solution.py:249
  132.3 12.7 %shard_map.93 = f32[64,2,4,16,128]{4,3,2,1,0:T(8,128)} custom-call(f32[64,64]{1,0:T(8,128)} %shard_map.92.p_ref, f32[64,2,4,16,128]{4,3,2,1,0:T(8,128)} %get-tuple-element.8.x_ref), custom_call_target="tpu_custom_call" | custom-call | tf_op jit(solution)/shard_map/pallas_call | solution.py:301
  (9 shorter events, 0.1 us)
Async XLA Ops:
  0.0 24.4 %copy-start.3 = (s32[1,1,4,128]{3,2,1,0:T(4,128)S(1)}, s32[1,1,4,128]{3,2,1,0:T(4,128)}, u32[]{:S(2)}) copy-start(s32[1,1,4,128]{3,2,1,0:T(4,128)} %param.13) | copy-start | bytes 6148
  0.0 24.5 %copy-start.4 = (f32[1,1,4,128]{3,2,1,0:T(4,128)S(1)}, f32[1,1,4,128]{3,2,1,0:T(4,128)}, u32[]{:S(2)}) copy-start(f32[1,1,4,128]{3,2,1,0:T(4,128)} %param.16) | copy-start | bytes 6148
  0.0 25.3 %copy-start.5 = (s32[1,1,4]{2,1,0:T(1,128)S(1)}, s32[1,1,4]{2,1,0:T(1,128)}, u32[]{:S(2)}) copy-start(s32[1,1,4]{2,1,0:T(1,128)} %param.14) | copy-start | bytes 52
  0.0 26.0 %copy-start.2 = (s32[1,1,5,5]{3,1,2,0:T(1,128)S(1)}, s32[1,1,5,5]{3,1,2,0:T(1,128)}, u32[]{:S(2)}) copy-start(s32[1,1,5,5]{3,1,2,0:T(1,128)} %param.17) | copy-start | bytes 304
  8.7 18.0 %collective-permute-start.2 = (f32[64,2,4,16]{0,3,2,1:T(8,128)S(1)}, f32[64,2,4,16]{0,3,2,1:T(8,128)S(1)}, u32[]{:S(2)}, u32[]{:S(2)}) collective-permute-start(f32[64,2,4,16]{0,3,2,1:T(8,128)S(1)} %bitcast.51), channel_id=1, source_target_pairs={{1,0},{2,1},{3,2},{4,3},{5,4},{6,5},{7,6},{9,8},{10,9},{11,10},{12... | collective-permute-start | bytes 98312 | tf_op jit(solution)/shard_map/ppermute | solution.py:86
  10.6 16.1 %collective-permute-start.3 = (f32[64,2,4,16]{0,3,2,1:T(8,128)S(1)}, f32[64,2,4,16]{0,3,2,1:T(8,128)S(1)}, u32[]{:S(2)}, u32[]{:S(2)}) collective-permute-start(f32[64,2,4,16]{0,3,2,1:T(8,128)S(1)} %bitcast.49), channel_id=1, source_target_pairs={{0,1},{1,2},{2,3},{3,4},{4,5},{5,6},{6,7},{8,9},{9,10},{10,11},{11... | collective-permute-start | bytes 98312 | tf_op jit(solution)/shard_map/ppermute | solution.py:87
  15.8 16.4 %collective-permute-start = (f32[64,2,4,1,128]{4,3,2,1,0:T(1,128)S(1)}, f32[64,2,4,1,128]{4,3,2,1,0:T(1,128)S(1)}, u32[]{:S(2)}, u32[]{:S(2)}) collective-permute-start(f32[64,2,4,1,128]{4,3,2,1,0:T(1,128)S(1)} %get-tuple-element.10), channel_id=1, source_target_pairs={{8,0},{16,8},{24,16},{32,24},{40,32},{48,40},{56,48},{64,56},{72,6... | collective-permute-start | bytes 786440 | tf_op jit(solution)/shard_map/ppermute | solution.py:77
  22.5 12.5 %collective-permute-start.1 = (f32[64,2,4,1,128]{4,3,2,1,0:T(1,128)S(1)}, f32[64,2,4,1,128]{4,3,2,1,0:T(1,128)S(1)}, u32[]{:S(2)}, u32[]{:S(2)}) collective-permute-start(f32[64,2,4,1,128]{4,3,2,1,0:T(1,128)S(1)} %get-tuple-element.9), channel_id=1, source_target_pairs={{0,8},{8,16},{16,24},{24,32},{32,40},{40,48},{48,56},{56,64},{64,7... | collective-permute-start | bytes 786440 | tf_op jit(solution)/shard_map/ppermute | solution.py:78
  32.2 2.7 %copy-start = (f32[64,2,4,1,128]{4,3,2,1,0:T(1,128)}, f32[64,2,4,1,128]{4,3,2,1,0:T(1,128)S(1)}, u32[]{:S(2)}) copy-start(f32[64,2,4,1,128]{4,3,2,1,0:T(1,128)S(1)} %collective-permute-done.east_ref) | copy-start | bytes 786436
  34.9 0.7 copy-start.1

commit v5 on v4

--- a/solution.py
+++ b/solution.py
@@ -289,7 +289,7 @@
 
     parts = [x_ref[:, 0, 0, h * sub : (h + 1) * sub, :].reshape(size, lanes) for h in range(rows // sub)]
     mixed = jnp.dot(k_scr[...], jnp.concatenate(parts, axis=1),
-                    precision=lax.Precision.HIGHEST, preferred_element_type=jnp.float32)
+                    precision=lax.Precision.HIGH, preferred_element_type=jnp.float32)
     for h in range(rows // sub):
         o_ref[:, 0, 0, h * sub : (h + 1) * sub, :] = mixed[:, h * lanes : (h + 1) * lanes].reshape(members, sub, lanes)
 

time: 146 us -> 144 us (0.986)
  Pallas kernels: 108 us -> 105 us
    pallas_call x1, Pallas kernels: 12.7 us -> 10.2 us  [apply_transform(): pl.pallas_call(transform_kernel, out_shape=jax.ShapeDtypeStruct(cells.sha...]
where the time goes in v5:
time: 144 us; the launch traced here: 143 us
  Pallas kernels  105 us (73%)
  matrix products  13.6 us (9%)
  starting transfers between devices  12.9 us (9%)
  local copies, waits for them, and re-layouts  5.78 us (4%)
  waiting for transfers between devices  2.74 us (2%)
  other arithmetic  2.11 us (1%)
    pallas_call x1, Pallas kernels, run_analysis(): pl.pallas_call(functools.partial(analysis_kernel, nx, ny), out_shape=jax....  83.3 us
    pallas_call x1, Pallas kernels, forecast_step(): pl.pallas_call(stencil_kernel, out_shape=(jax.ShapeDtypeStruct(cells.shap...  11.8 us
    pallas_call x1, Pallas kernels, apply_transform(): pl.pallas_call(transform_kernel, out_shape=jax.ShapeDtypeStruct(cells.sha...  10.2 us
    dot_general x1, matrix products, forecast_step(): jnp.einsum('abcil,sl->sabci', cells, pick, precision=lax.Precision.HIGHES...  8.5 us
    ppermute x1, starting transfers between devices, forecast_step(): lax.ppermute(cells[:, :, :, 0:1, :], 'gx', [(i + 1, i) for i in range(nx...  6.66 us
    dot_general x1, matrix products, forecast_step(): jnp.einsum('sabci,sl->abcil', jnp.stack([north_halo, south_halo]), place,...  5.07 us
  transfers between devices with their start and end apart: 4, of which 1 were waited for; matrix products, arithmetic and copies ran while one was open for 7% of the time, Pallas kernels for 0%

profile of v5, /device:TPU:96, one launch (start us, length us, event | category | flops | bytes accessed | tf_op | source)
XLA Modules:
  0.0 142.5 jit_solution(466949115017103430)
XLA Ops:
  0.0 0.0 copy-start.3
  0.0 0.0 copy-start.4
  0.0 0.0 copy-start.2
  0.0 8.5 %fusion = f32[2,64,2,4,16]{1,0,4,3,2:T(2,128)S(1)} fusion(f32[64,2,4,16,128]{4,3,2,1,0:T(8,128)} %x_ref.1, pred[1,128]{1,0:T(4,128)(4,1)S(1)} %get-tuple-element.15, pred[1,128]{1,0:T(4,128)(4,1)S(1)} %get-tuple-element.16), kind=kOutput, calls=%fused_computation | convolution fusion | flops 25166080 | bytes 4260096 | tf_op jit(solution)/shard_map/abcil,sl->sabci/dot_general | solution.py:82
  8.5 0.1 fusion.14
  8.7 1.9 %collective-permute-start.2 = (f32[64,2,4,16]{0,3,2,1:T(8,128)S(1)}, f32[64,2,4,16]{0,3,2,1:T(8,128)S(1)}, u32[]{:S(2)}, u32[]{:S(2)}) collective-permute-start(f32[64,2,4,16]{0,3,2,1:T(8,128)S(1)} %bitcast.51), channel_id=1, source_target_pairs={{1,0},{2,1},{3,2},{4,3},{5,4},{6,5},{7,6},{9,8},{10,9},{11,10},{12... | collective-permute-start | bytes 98312 | tf_op jit(solution)/shard_map/ppermute | solution.py:86
  10.6 2.4 %collective-permute-start.3 = (f32[64,2,4,16]{0,3,2,1:T(8,128)S(1)}, f32[64,2,4,16]{0,3,2,1:T(8,128)S(1)}, u32[]{:S(2)}, u32[]{:S(2)}) collective-permute-start(f32[64,2,4,16]{0,3,2,1:T(8,128)S(1)} %bitcast.49), channel_id=1, source_target_pairs={{0,1},{1,2},{2,3},{3,4},{4,5},{5,6},{6,7},{8,9},{9,10},{10,11},{11... | collective-permute-start | bytes 98312 | tf_op jit(solution)/shard_map/ppermute | solution.py:87
  13.0 2.8 %fusion.13 = (f32[64,2,4,1,128]{4,3,2,1,0:T(1,128)S(1)}, f32[64,2,4,1,128]{4,3,2,1,0:T(1,128)S(1)}) fusion(f32[64,2,4,16,128]{4,3,2,1,0:T(8,128)} %x_ref.1), kind=kLoop, calls=%fused_computation.33 | loop fusion | bytes 1048576 | tf_op jit(solution)/shard_map/slice | solution.py:78
  15.8 6.7 %collective-permute-start = (f32[64,2,4,1,128]{4,3,2,1,0:T(1,128)S(1)}, f32[64,2,4,1,128]{4,3,2,1,0:T(1,128)S(1)}, u32[]{:S(2)}, u32[]{:S(2)}) collective-permute-start(f32[64,2,4,1,128]{4,3,2,1,0:T(1,128)S(1)} %get-tuple-element.10), channel_id=1, source_target_pairs={{8,0},{16,8},{24,16},{32,24},{40,32},{48,40},{56,48},{64,56},{72,6... | collective-permute-start | bytes 786440 | tf_op jit(solution)/shard_map/ppermute | solution.py:77
  22.5 1.9 %collective-permute-start.1 = (f32[64,2,4,1,128]{4,3,2,1,0:T(1,128)S(1)}, f32[64,2,4,1,128]{4,3,2,1,0:T(1,128)S(1)}, u32[]{:S(2)}, u32[]{:S(2)}) collective-permute-start(f32[64,2,4,1,128]{4,3,2,1,0:T(1,128)S(1)} %get-tuple-element.9), channel_id=1, source_target_pairs={{0,8},{8,16},{16,24},{24,32},{32,40},{40,48},{48,56},{56,64},{64,7... | collective-permute-start | bytes 786440 | tf_op jit(solution)/shard_map/ppermute | solution.py:78
  24.4 0.0 copy-done.3
  24.4 0.1 and_convert_fusion
  24.5 0.0 copy-done.4
  24.5 0.8 fusion.2
  25.3 0.0 copy-done.5
  25.3 0.6 compare_select_fusion.scale_ref
  26.0 0.0 copy-done.2
  26.0 0.1 reshape.175
  26.1 0.1 convert_element_type.26
  26.1 0.5 max.4.w_ref
  26.7 0.0 collective-permute-done.2
  26.7 0.0 collective-permute-done.3
  26.7 0.4 copy.15
  27.1 5.1 %fusion.8.edge_ref = f32[64,2,4,16,128]{4,3,2,1,0:T(8,128)} fusion(f32[2,64,2,4,16]{4,0,3,2,1:T(2,128)S(1)} %copy.15, pred[1,128]{1,0:T(4,128)(4,1)S(1)} %get-tuple-element.16, pred[1,128]{1,0:T(4,128)(4,1)S(1)} %get-tuple-element.15), kind=kOutput, calls=%fused_computation.24 | convolution fusion | flops 25166080 | bytes 4260096 | tf_op jit(solution)/shard_map/sabci,sl->abcil/dot_general | solution.py:88
  32.2 0.0 collective-permute-done.east_ref
  32.2 2.7 %collective-permute-done.1.west_ref = f32[64,2,4,1,128]{4,3,2,1,0:T(1,128)S(1)} collective-permute-done((f32[64,2,4,1,128]{4,3,2,1,0:T(1,128)S(1)}, f32[64,2,4,1,128]{4,3,2,1,0:T(1,128)S(1)}, u32[]{:S(2)}, u32[]{:S(2)}) %collective-permute-start.1) | collective-permute-done | bytes 262176 | tf_op jit(solution)/shard_map/ppermute | solution.py:78
  35.0 0.0 copy-done
  35.0 0.7 copy-done.1
  35.7 11.8 %shard_map.91 = (f32[64,2,4,16,128]{4,3,2,1,0:T(8,128)}, f32[64,512]{1,0:T(8,128)}) custom-call(f32[64,2,4,16,128]{4,3,2,1,0:T(8,128)} %x_ref.1, f32[64,2,4,1,128]{4,3,2,1,0:T(1,128)} %copy-done, f32[64,2,4,1,128]{4,3,2,1,0:T(1,128)} %copy-done.1, f32[64,2,4,16,128]{4,3,2,1,0:T(8,128)} %fusion.8.edge_ref, f32[2,16,128]{2,1,0:T(8,128)} %u_ref.1, ...), custom_call_target="tpu_custom_call" | custom-call | tf_op jit(solution)/shard_map/pallas_call | solution.py:103
  47.4 1.6 %bitcast_bitcast_fusion.y_ref = f32[4,64,128]{2,1,0:T(8,128)} fusion(f32[64,512]{1,0:T(8,128)} %get-tuple-element.7), kind=kLoop, calls=%fused_computation.6 | loop fusion | bytes 262144 | tf_op jit(solution)/shard_map/transpose | solution.py:339
  49.0 83.3 %shard_map.92.p_ref = f32[64,64]{1,0:T(8,128)} custom-call(f32[4,64,128]{2,1,0:T(8,128)} %bitcast_bitcast_fusion.y_ref, f32[4,1,128]{2,1,0:T(1,128)} %compare_select_fusion.scale_ref, f32[4,1,128]{2,1,0:T(1,128)} %bitcast.54, f32[25]{0:T(128)} %max.4.w_ref), custom_call_target="tpu_custom_call" | custom-call | tf_op jit(solution)/shard_map/pallas_call | solution.py:249
  132.3 10.2 %shard_map.93 = f32[64,2,4,16,128]{4,3,2,1,0:T(8,128)} custom-call(f32[64,64]{1,0:T(8,128)} %shard_map.92.p_ref, f32[64,2,4,16,128]{4,3,2,1,0:T(8,128)} %get-tuple-element.8.x_ref), custom_call_target="tpu_custom_call" | custom-call | tf_op jit(solution)/shard_map/pallas_call | solution.py:301
  (9 shorter events, 0.1 us)
Async XLA Ops:
  0.0 24.4 %copy-start.3 = (s32[1,1,4,128]{3,2,1,0:T(4,128)S(1)}, s32[1,1,4,128]{3,2,1,0:T(4,128)}, u32[]{:S(2)}) copy-start(s32[1,1,4,128]{3,2,1,0:T(4,128)} %param.13) | copy-start | bytes 6148
  0.0 24.5 %copy-start.4 = (f32[1,1,4,128]{3,2,1,0:T(4,128)S(1)}, f32[1,1,4,128]{3,2,1,0:T(4,128)}, u32[]{:S(2)}) copy-start(f32[1,1,4,128]{3,2,1,0:T(4,128)} %param.16) | copy-start | bytes 6148
  0.0 25.3 %copy-start.5 = (s32[1,1,4]{2,1,0:T(1,128)S(1)}, s32[1,1,4]{2,1,0:T(1,128)}, u32[]{:S(2)}) copy-start(s32[1,1,4]{2,1,0:T(1,128)} %param.14) | copy-start | bytes 52
  0.0 26.0 %copy-start.2 = (s32[1,1,5,5]{3,1,2,0:T(1,128)S(1)}, s32[1,1,5,5]{3,1,2,0:T(1,128)}, u32[]{:S(2)}) copy-start(s32[1,1,5,5]{3,1,2,0:T(1,128)} %param.17) | copy-start | bytes 304
  8.7 18.0 %collective-permute-start.2 = (f32[64,2,4,16]{0,3,2,1:T(8,128)S(1)}, f32[64,2,4,16]{0,3,2,1:T(8,128)S(1)}, u32[]{:S(2)}, u32[]{:S(2)}) collective-permute-start(f32[64,2,4,16]{0,3,2,1:T(8,128)S(1)} %bitcast.51), channel_id=1, source_target_pairs={{1,0},{2,1},{3,2},{4,3},{5,4},{6,5},{7,6},{9,8},{10,9},{11,10},{12... | collective-permute-start | bytes 98312 | tf_op jit(solution)/shard_map/ppermute | solution.py:86
  10.6 16.1 %collective-permute-start.3 = (f32[64,2,4,16]{0,3,2,1:T(8,128)S(1)}, f32[64,2,4,16]{0,3,2,1:T(8,128)S(1)}, u32[]{:S(2)}, u32[]{:S(2)}) collective-permute-start(f32[64,2,4,16]{0,3,2,1:T(8,128)S(1)} %bitcast.49), channel_id=1, source_target_pairs={{0,1},{1,2},{2,3},{3,4},{4,5},{5,6},{6,7},{8,9},{9,10},{10,11},{11... | collective-permute-start | bytes 98312 | tf_op jit(solution)/shard_map/ppermute | solution.py:87
  15.8 16.4 %collective-permute-start = (f32[64,2,4,1,128]{4,3,2,1,0:T(1,128)S(1)}, f32[64,2,4,1,128]{4,3,2,1,0:T(1,128)S(1)}, u32[]{:S(2)}, u32[]{:S(2)}) collective-permute-start(f32[64,2,4,1,128]{4,3,2,1,0:T(1,128)S(1)} %get-tuple-element.10), channel_id=1, source_target_pairs={{8,0},{16,8},{24,16},{32,24},{40,32},{48,40},{56,48},{64,56},{72,6... | collective-permute-start | bytes 786440 | tf_op jit(solution)/shard_map/ppermute | solution.py:77
  22.5 12.5 %collective-permute-start.1 = (f32[64,2,4,1,128]{4,3,2,1,0:T(1,128)S(1)}, f32[64,2,4,1,128]{4,3,2,1,0:T(1,128)S(1)}, u32[]{:S(2)}, u32[]{:S(2)}) collective-permute-start(f32[64,2,4,1,128]{4,3,2,1,0:T(1,128)S(1)} %get-tuple-element.9), channel_id=1, source_target_pairs={{0,8},{8,16},{16,24},{24,32},{32,40},{40,48},{48,56},{56,64},{64,7... | collective-permute-start | bytes 786440 | tf_op jit(solution)/shard_map/ppermute | solution.py:78
  32.2 2.7 %copy-start = (f32[64,2,4,1,128]{4,3,2,1,0:T(1,128)}, f32[64,2,4,1,128]{4,3,2,1,0:T(1,128)S(1)}, u32[]{:S(2)}) copy-start(f32[64,2,4,1,128]{4,3,2,1,0:T(1,128)S(1)} %collective-permute-done.east_ref) | copy-start | bytes 786436
  34.9 0.7 copy-start.1

commit v6 on v5

--- a/solution.py
+++ b/solution.py
@@ -130,7 +130,7 @@
 
 def analysis_kernel(
     nx, ny, y_ref, scale_ref, obs_ref, w_ref, out_ref,
-    slots, payload, rows_t, total, carried, send_sem, recv_sem,
+    slots, payload, rows_t, rows_u, total, carried, send_sem, recv_sem,
 ):
     me_x = lax.axis_index("gx")
     me_y = lax.axis_index("gy")
@@ -160,11 +160,22 @@
 
     pl.semaphore_wait(barrier, partners)
 
+    half = members // 2
     row = lax.broadcasted_iota(jnp.int32, (members, members), 0)
     col = lax.broadcasted_iota(jnp.int32, (members, members), 1)
     identity = (row == col).astype(jnp.float32)
+    pair_row = lax.broadcasted_iota(jnp.int32, (half, members), 0)
+    pair_col = lax.broadcasted_iota(jnp.int32, (half, members), 1)
+    take_even = (pair_col == 2 * pair_row).astype(jnp.float32)
+    take_odd = (pair_col == 2 * pair_row + 1).astype(jnp.float32)
+    spread_row = lax.broadcasted_iota(jnp.int32, (members, half), 0)
+    spread_col = lax.broadcasted_iota(jnp.int32, (members, half), 1)
+    put_even = (spread_row == 2 * spread_col).astype(jnp.float32)
+    put_odd = (spread_row == 2 * spread_col + 1).astype(jnp.float32)
+    first_row = lax.broadcasted_iota(jnp.int32, (8, slot_count), 0) == 0
     carried[...] = identity
     rows_t[...] = jnp.zeros(rows_t.shape, jnp.float32)
+    rows_u[...] = jnp.zeros(rows_u.shape, jnp.float32)
 
     def batch_step(b, _):
         par = b % 2
@@ -174,8 +185,11 @@
         scaled_rows = scale * (sampled - prior_mean)
         innovation = scale * (obs_ref[b] - prior_mean)
         rows_t[0:members, :] = scaled_rows
-        rows_t[members : members + 1, :] = innovation
-        payload[par] = mm_nt(scaled_rows, rows_t[...])
+        rows_u[members : 2 * members, :] = scaled_rows
+        lead = mm_nt(mm(take_even, scaled_rows), rows_t[...]) + mm_nt(mm(take_odd, scaled_rows), rows_u[...])
+        tail = mm_nt(jnp.where(first_row, innovation, 0.0), rows_t[...])
+        payload[par, 0:half, :] = lead
+        payload[par, half : half + 8, :] = tail
 
         copies = []
         for k, (dx, dy) in enumerate(OFFSETS):
@@ -214,8 +228,9 @@
                 total[...] += w_ref[k] * slots[par, k]
 
         summed = total[...]
-        gram_total = summed[:, 0:members]
-        proj_block = summed[:, members : 2 * members]
+        packed = summed[0:half, :]
+        gram_total = mm(put_even, packed[:, 0:members]) + mm(put_odd, packed[:, members : 2 * members])
+        proj_rows = summed[half : half + 8, 0:members]
         precision_matrix = identity + gram_total / (members - 1)
         squares = precision_matrix * precision_matrix
         frobenius = jnp.sqrt(jnp.sum(jnp.sum(squares, axis=1, keepdims=True), axis=0, keepdims=True))
@@ -231,9 +246,8 @@
             pair = ns_step(_i, pair)
         iterate, inverse = pair
         transform = inverse / jnp.sqrt(frobenius)
-        weights = mm(transform, mm(transform, proj_block)) / (members - 1)
-        mixing = transform + weights[:, 0:1]
-        mixing_t = mm_nt(identity, mixing)
+        weights = mm_nt(mm_nt(proj_rows, transform), transform) / (members - 1)
+        mixing_t = mm_nt(identity, transform) + weights[0:1, :]
         step = 1.0 / members + mixing_t - jnp.mean(mixing_t, axis=1, keepdims=True)
         carried[...] = mm(step, carried[...])
         return 0
@@ -246,6 +260,7 @@
     batches, members, slot_count = y.shape
     count = len(OFFSETS)
     wide = 2 * members
+    packed_rows = members // 2 + 8
     return pl.pallas_call(
         functools.partial(analysis_kernel, nx, ny),
         out_shape=jax.ShapeDtypeStruct((members, members), jnp.float32),
@@ -257,10 +272,11 @@
         ],
         out_specs=pl.BlockSpec(memory_space=pltpu.VMEM),
         scratch_shapes=[
-            pltpu.VMEM((2, count, members, wide), jnp.float32),
-            pltpu.VMEM((2, members, wide), jnp.float32),
+            pltpu.VMEM((2, count, packed_rows, wide), jnp.float32),
+            pltpu.VMEM((2, packed_rows, wide), jnp.float32),
             pltpu.VMEM((wide, slot_count), jnp.float32),
-            pltpu.VMEM((members, wide), jnp.float32),
+            pltpu.VMEM((wide, slot_count), jnp.float32),
+            pltpu.VMEM((packed_rows, wide), jnp.float32),
             pltpu.VMEM((members, members), jnp.float32),
             pltpu.SemaphoreType.DMA((2, count)),
             pltpu.SemaphoreType.DMA((2, count)),

time: 144 us -> 129 us (0.90)
  the two profiles are of different devices: /device:TPU:96 before, /device:TPU:4 now
where the time goes in v6:
time: 129 us
  Pallas kernels  94.2 us (73%)
  matrix products  13.6 us (11%)
  starting transfers between devices  11.1 us (9%)
  local copies, waits for them, and re-layouts  5.78 us (4%)
  other arithmetic  2.11 us (2%)
  waiting for transfers between devices  1.73 us (1%)
    pallas_call x1, Pallas kernels, run_analysis(): pl.pallas_call(functools.partial(analysis_kernel, nx, ny), out_shape=jax....  72.2 us
    pallas_call x1, Pallas kernels, forecast_step(): pl.pallas_call(stencil_kernel, out_shape=(jax.ShapeDtypeStruct(cells.shap...  11.8 us
    pallas_call x1, Pallas kernels, apply_transform(): pl.pallas_call(transform_kernel, out_shape=jax.ShapeDtypeStruct(cells.sha...  10.2 us
    dot_general x1, matrix products, forecast_step(): jnp.einsum('abcil,sl->sabci', cells, pick, precision=lax.Precision.HIGHES...  8.5 us
    dot_general x1, matrix products, forecast_step(): jnp.einsum('sabci,sl->abcil', jnp.stack([north_halo, south_halo]), place,...  5.07 us
    ppermute x1, starting transfers between devices, forecast_step(): lax.ppermute(cells[:, :, :, 0:1, :], 'gx', [(i + 1, i) for i in range(nx...  4.89 us
    ppermute x1, starting transfers between devices, forecast_step(): lax.ppermute(sides[1], 'gy', [(i, i + 1) for i in range(ny - 1)])  3.03 us
    slice x1, local copies, waits for them, and re-layouts, forecast_step(): cells[:, :, :, rows - 1:rows, :]  2.79 us
  transfers between devices with their start and end apart: 4, of which 1 were waited for; matrix products, arithmetic and copies ran while one was open for 8% of the time, Pallas kernels for 0%

profile of v6, /device:TPU:4, one launch (start us, length us, event | category | flops | bytes accessed | tf_op | source)
XLA Modules:
  0.0 128.7 jit_solution(1449582015368824937)
XLA Ops:
  0.0 0.0 copy-start.3
  0.0 0.0 copy-start.4
  0.0 0.0 copy-start.2
  0.0 8.5 %fusion = f32[2,64,2,4,16]{1,0,4,3,2:T(2,128)S(1)} fusion(f32[64,2,4,16,128]{4,3,2,1,0:T(8,128)} %x_ref.1, pred[1,128]{1,0:T(4,128)(4,1)S(1)} %get-tuple-element.15, pred[1,128]{1,0:T(4,128)(4,1)S(1)} %get-tuple-element.16), kind=kOutput, calls=%fused_computation | convolution fusion | flops 25166080 | bytes 4260096 | tf_op jit(solution)/shard_map/abcil,sl->sabci/dot_general | solution.py:82
  8.5 0.1 fusion.14
  8.7 1.3 %collective-permute-start.2 = (f32[64,2,4,16]{0,3,2,1:T(8,128)S(1)}, f32[64,2,4,16]{0,3,2,1:T(8,128)S(1)}, u32[]{:S(2)}, u32[]{:S(2)}) collective-permute-start(f32[64,2,4,16]{0,3,2,1:T(8,128)S(1)} %bitcast.51), channel_id=1, source_target_pairs={{1,0},{2,1},{3,2},{4,3},{5,4},{6,5},{7,6},{9,8},{10,9},{11,10},{12... | collective-permute-start | bytes 98312 | tf_op jit(solution)/shard_map/ppermute | solution.py:86
  10.0 3.0 %collective-permute-start.3 = (f32[64,2,4,16]{0,3,2,1:T(8,128)S(1)}, f32[64,2,4,16]{0,3,2,1:T(8,128)S(1)}, u32[]{:S(2)}, u32[]{:S(2)}) collective-permute-start(f32[64,2,4,16]{0,3,2,1:T(8,128)S(1)} %bitcast.49), channel_id=1, source_target_pairs={{0,1},{1,2},{2,3},{3,4},{4,5},{5,6},{6,7},{8,9},{9,10},{10,11},{11... | collective-permute-start | bytes 98312 | tf_op jit(solution)/shard_map/ppermute | solution.py:87
  13.0 2.8 %fusion.13 = (f32[64,2,4,1,128]{4,3,2,1,0:T(1,128)S(1)}, f32[64,2,4,1,128]{4,3,2,1,0:T(1,128)S(1)}) fusion(f32[64,2,4,16,128]{4,3,2,1,0:T(8,128)} %x_ref.1), kind=kLoop, calls=%fused_computation.33 | loop fusion | bytes 1048576 | tf_op jit(solution)/shard_map/slice | solution.py:78
  15.8 4.9 %collective-permute-start = (f32[64,2,4,1,128]{4,3,2,1,0:T(1,128)S(1)}, f32[64,2,4,1,128]{4,3,2,1,0:T(1,128)S(1)}, u32[]{:S(2)}, u32[]{:S(2)}) collective-permute-start(f32[64,2,4,1,128]{4,3,2,1,0:T(1,128)S(1)} %get-tuple-element.10), channel_id=1, source_target_pairs={{8,0},{16,8},{24,16},{32,24},{40,32},{48,40},{56,48},{64,56},{72,6... | collective-permute-start | bytes 786440 | tf_op jit(solution)/shard_map/ppermute | solution.py:77
  20.7 1.9 %collective-permute-start.1 = (f32[64,2,4,1,128]{4,3,2,1,0:T(1,128)S(1)}, f32[64,2,4,1,128]{4,3,2,1,0:T(1,128)S(1)}, u32[]{:S(2)}, u32[]{:S(2)}) collective-permute-start(f32[64,2,4,1,128]{4,3,2,1,0:T(1,128)S(1)} %get-tuple-element.9), channel_id=1, source_target_pairs={{0,8},{8,16},{16,24},{24,32},{32,40},{40,48},{48,56},{56,64},{64,7... | collective-permute-start | bytes 786440 | tf_op jit(solution)/shard_map/ppermute | solution.py:78
  22.6 0.0 copy-done.3
  22.7 0.1 and_convert_fusion
  22.7 0.0 copy-done.4
  22.7 0.8 fusion.2
  23.5 0.0 copy-done.5
  23.5 0.6 compare_select_fusion.scale_ref
  24.2 0.0 copy-done.2
  24.2 0.1 reshape.175
  24.3 0.1 convert_element_type.26
  24.4 0.5 max.4.w_ref
  24.9 0.0 collective-permute-done.2
  24.9 0.0 collective-permute-done.3
  24.9 0.4 copy.15
  25.4 5.1 %fusion.8.edge_ref = f32[64,2,4,16,128]{4,3,2,1,0:T(8,128)} fusion(f32[2,64,2,4,16]{4,0,3,2,1:T(2,128)S(1)} %copy.15, pred[1,128]{1,0:T(4,128)(4,1)S(1)} %get-tuple-element.16, pred[1,128]{1,0:T(4,128)(4,1)S(1)} %get-tuple-element.15), kind=kOutput, calls=%fused_computation.24 | convolution fusion | flops 25166080 | bytes 4260096 | tf_op jit(solution)/shard_map/sabci,sl->abcil/dot_general | solution.py:88
  30.4 0.0 collective-permute-done.east_ref
  30.4 1.7 %collective-permute-done.1.west_ref = f32[64,2,4,1,128]{4,3,2,1,0:T(1,128)S(1)} collective-permute-done((f32[64,2,4,1,128]{4,3,2,1,0:T(1,128)S(1)}, f32[64,2,4,1,128]{4,3,2,1,0:T(1,128)S(1)}, u32[]{:S(2)}, u32[]{:S(2)}) %collective-permute-start.1) | collective-permute-done | bytes 262176 | tf_op jit(solution)/shard_map/ppermute | solution.py:78
  32.2 0.0 copy-done
  32.2 0.7 copy-done.1
  32.9 11.8 %shard_map.91 = (f32[64,2,4,16,128]{4,3,2,1,0:T(8,128)}, f32[64,512]{1,0:T(8,128)}) custom-call(f32[64,2,4,16,128]{4,3,2,1,0:T(8,128)} %x_ref.1, f32[64,2,4,1,128]{4,3,2,1,0:T(1,128)} %copy-done, f32[64,2,4,1,128]{4,3,2,1,0:T(1,128)} %copy-done.1, f32[64,2,4,16,128]{4,3,2,1,0:T(8,128)} %fusion.8.edge_ref, f32[2,16,128]{2,1,0:T(8,128)} %u_ref.1, ...), custom_call_target="tpu_custom_call" | custom-call | tf_op jit(solution)/shard_map/pallas_call | solution.py:103
  44.6 1.6 %bitcast_bitcast_fusion.y_ref = f32[4,64,128]{2,1,0:T(8,128)} fusion(f32[64,512]{1,0:T(8,128)} %get-tuple-element.7), kind=kLoop, calls=%fused_computation.6 | loop fusion | bytes 262144 | tf_op jit(solution)/shard_map/transpose | solution.py:355
  46.2 72.2 %shard_map.92.p_ref = f32[64,64]{1,0:T(8,128)} custom-call(f32[4,64,128]{2,1,0:T(8,128)} %bitcast_bitcast_fusion.y_ref, f32[4,1,128]{2,1,0:T(1,128)} %compare_select_fusion.scale_ref, f32[4,1,128]{2,1,0:T(1,128)} %bitcast.54, f32[25]{0:T(128)} %max.4.w_ref), custom_call_target="tpu_custom_call" | custom-call | tf_op jit(solution)/shard_map/pallas_call | solution.py:264
  118.5 10.2 %shard_map.93 = f32[64,2,4,16,128]{4,3,2,1,0:T(8,128)} custom-call(f32[64,64]{1,0:T(8,128)} %shard_map.92.p_ref, f32[64,2,4,16,128]{4,3,2,1,0:T(8,128)} %get-tuple-element.8.x_ref), custom_call_target="tpu_custom_call" | custom-call | tf_op jit(solution)/shard_map/pallas_call | solution.py:317
  (9 shorter events, 0.1 us)
Async XLA Ops:
  0.0 22.6 %copy-start.3 = (s32[1,1,4,128]{3,2,1,0:T(4,128)S(1)}, s32[1,1,4,128]{3,2,1,0:T(4,128)}, u32[]{:S(2)}) copy-start(s32[1,1,4,128]{3,2,1,0:T(4,128)} %param.13) | copy-start | bytes 6148
  0.0 22.7 %copy-start.4 = (f32[1,1,4,128]{3,2,1,0:T(4,128)S(1)}, f32[1,1,4,128]{3,2,1,0:T(4,128)}, u32[]{:S(2)}) copy-start(f32[1,1,4,128]{3,2,1,0:T(4,128)} %param.16) | copy-start | bytes 6148
  0.0 23.5 %copy-start.5 = (s32[1,1,4]{2,1,0:T(1,128)S(1)}, s32[1,1,4]{2,1,0:T(1,128)}, u32[]{:S(2)}) copy-start(s32[1,1,4]{2,1,0:T(1,128)} %param.14) | copy-start | bytes 52
  0.0 24.2 %copy-start.2 = (s32[1,1,5,5]{3,1,2,0:T(1,128)S(1)}, s32[1,1,5,5]{3,1,2,0:T(1,128)}, u32[]{:S(2)}) copy-start(s32[1,1,5,5]{3,1,2,0:T(1,128)} %param.17) | copy-start | bytes 304
  8.7 16.3 %collective-permute-start.2 = (f32[64,2,4,16]{0,3,2,1:T(8,128)S(1)}, f32[64,2,4,16]{0,3,2,1:T(8,128)S(1)}, u32[]{:S(2)}, u32[]{:S(2)}) collective-permute-start(f32[64,2,4,16]{0,3,2,1:T(8,128)S(1)} %bitcast.51), channel_id=1, source_target_pairs={{1,0},{2,1},{3,2},{4,3},{5,4},{6,5},{7,6},{9,8},{10,9},{11,10},{12... | collective-permute-start | bytes 98312 | tf_op jit(solution)/shard_map/ppermute | solution.py:86
  10.0 15.0 %collective-permute-start.3 = (f32[64,2,4,16]{0,3,2,1:T(8,128)S(1)}, f32[64,2,4,16]{0,3,2,1:T(8,128)S(1)}, u32[]{:S(2)}, u32[]{:S(2)}) collective-permute-start(f32[64,2,4,16]{0,3,2,1:T(8,128)S(1)} %bitcast.49), channel_id=1, source_target_pairs={{0,1},{1,2},{2,3},{3,4},{4,5},{5,6},{6,7},{8,9},{9,10},{10,11},{11... | collective-permute-start | bytes 98312 | tf_op jit(solution)/shard_map/ppermute | solution.py:87
  15.8 14.7 %collective-permute-start = (f32[64,2,4,1,128]{4,3,2,1,0:T(1,128)S(1)}, f32[64,2,4,1,128]{4,3,2,1,0:T(1,128)S(1)}, u32[]{:S(2)}, u32[]{:S(2)}) collective-permute-start(f32[64,2,4,1,128]{4,3,2,1,0:T(1,128)S(1)} %get-tuple-element.10), channel_id=1, source_target_pairs={{8,0},{16,8},{24,16},{32,24},{40,32},{48,40},{56,48},{64,56},{72,6... | collective-permute-start | bytes 786440 | tf_op jit(solution)/shard_map/ppermute | solution.py:77
  20.7 11.5 %collective-permute-start.1 = (f32[64,2,4,1,128]{4,3,2,1,0:T(1,128)S(1)}, f32[64,2,4,1,128]{4,3,2,1,0:T(1,128)S(1)}, u32[]{:S(2)}, u32[]{:S(2)}) collective-permute-start(f32[64,2,4,1,128]{4,3,2,1,0:T(1,128)S(1)} %get-tuple-element.9), channel_id=1, source_target_pairs={{0,8},{8,16},{16,24},{24,32},{32,40},{40,48},{48,56},{56,64},{64,7... | collective-permute-start | bytes 786440 | tf_op jit(solution)/shard_map/ppermute | solution.py:78
  30.4 1.7 %copy-start = (f32[64,2,4,1,128]{4,3,2,1,0:T(1,128)}, f32[64,2,4,1,128]{4,3,2,1,0:T(1,128)S(1)}, u32[]{:S(2)}) copy-start(f32[64,2,4,1,128]{4,3,2,1,0:T(1,128)S(1)} %collective-permute-done.east_ref) | copy-start | bytes 786436
  32.2 0.7 copy-start.1

commit v7 on v6

--- a/solution.py
+++ b/solution.py
@@ -34,7 +34,7 @@
     return transform + weights[:, None]
 
 
-def stencil_kernel(x_ref, east_ref, west_ref, edge_ref, u_ref, v_ref, d_ref, col_ref, row_ref, o_ref, s_ref, east_scr, west_scr):
+def stencil_kernel(x_ref, east_ref, west_ref, halo_ref, u_ref, v_ref, d_ref, col_ref, row_ref, o_ref, s_ref, east_scr, west_scr):
     rows = x_ref.shape[3]
     lanes = x_ref.shape[4]
     east_scr[:, :, :, 0 : rows - 1, :] = x_ref[:, :, :, 1:rows, :]
@@ -44,10 +44,14 @@
     centre = x_ref[...]
     east_cell = east_scr[...]
     west_cell = west_scr[...]
-    edge = edge_ref[...]
+    sides = halo_ref[...]
+    padded = jnp.concatenate([sides, jnp.zeros((lanes - sides.shape[0], sides.shape[1]), jnp.float32)], axis=0)
+    columns = jnp.transpose(padded)
+    north_edge = jnp.broadcast_to(columns[:, 0:1], columns.shape).reshape(centre.shape)
+    south_edge = jnp.broadcast_to(columns[:, 1:2], columns.shape).reshape(centre.shape)
     lane = lax.broadcasted_iota(jnp.int32, centre.shape, 4)
-    north_cell = jnp.where(lane == lanes - 1, edge, pltpu.roll(centre, lanes - 1, 4))
-    south_cell = jnp.where(lane == 0, edge, pltpu.roll(centre, 1, 4))
+    north_cell = jnp.where(lane == lanes - 1, north_edge, pltpu.roll(centre, lanes - 1, 4))
+    south_cell = jnp.where(lane == 0, south_edge, pltpu.roll(centre, 1, 4))
     u = u_ref[...][None, :, None]
     v = v_ref[...][None, :, None]
     d = d_ref[...][None, None, None]
@@ -70,25 +74,32 @@
     s_ref[...] = jnp.sum(picked, axis=1)
 
 
+def pick_kernel(p_ref, x_ref, o_ref):
+    o_ref[...] = mm_nt(p_ref[...], x_ref[...])
+
+
 def forecast_step(cells, courant_eastward, courant_northward, diffusivity, sites):
     nx = lax.axis_size("gx")
     ny = lax.axis_size("gy")
     rows, lanes = cells.shape[3], cells.shape[4]
     east_halo = lax.ppermute(cells[:, :, :, 0:1, :], "gx", [(i + 1, i) for i in range(nx - 1)])
     west_halo = lax.ppermute(cells[:, :, :, rows - 1 : rows, :], "gx", [(i, i + 1) for i in range(nx - 1)])
+    flat_rows = cells.size // lanes
     lane_index = jnp.arange(lanes)
-    pick = jnp.stack([lane_index == 0, lane_index == lanes - 1]).astype(jnp.float32)
-    place = jnp.stack([lane_index == lanes - 1, lane_index == 0]).astype(jnp.float32)
-    sides = jnp.einsum(
-        "abcil,sl->sabci",
-        cells, pick, precision=lax.Precision.HIGHEST, preferred_element_type=jnp.float32,
-    )
-    north_halo = lax.ppermute(sides[0], "gy", [(i + 1, i) for i in range(ny - 1)])
-    south_halo = lax.ppermute(sides[1], "gy", [(i, i + 1) for i in range(ny - 1)])
-    edge = jnp.einsum(
-        "sabci,sl->abcil", jnp.stack([north_halo, south_halo]), place,
-        precision=lax.Precision.HIGHEST, preferred_element_type=jnp.float32,
-    )
+    pick = jnp.zeros((8, lanes), jnp.float32)
+    pick = pick.at[0].set((lane_index == 0).astype(jnp.float32))
+    pick = pick.at[1].set((lane_index == lanes - 1).astype(jnp.float32))
+    part = flat_rows // 8
+    sides = pl.pallas_call(
+        pick_kernel,
+        out_shape=jax.ShapeDtypeStruct((8, flat_rows), jnp.float32),
+        grid=(8,),
+        in_specs=[pl.BlockSpec((8, lanes), lambda i: (0, 0)), pl.BlockSpec((part, lanes), lambda i: (i, 0))],
+        out_specs=pl.BlockSpec((8, part), lambda i: (0, i)),
+    )(pick, cells.reshape(flat_rows, lanes))
+    north_halo = lax.ppermute(sides[0:1], "gy", [(i + 1, i) for i in range(ny - 1)])
+    south_halo = lax.ppermute(sides[1:2], "gy", [(i, i + 1) for i in range(ny - 1)])
+    edge = jnp.concatenate([north_halo, south_halo, jnp.zeros((6, flat_rows), jnp.float32)], axis=0)
     block = 8
     members = cells.shape[0]
     big = pl.BlockSpec((block,) + cells.shape[1:], lambda i: (i, 0, 0, 0, 0))
@@ -107,7 +118,7 @@
             jax.ShapeDtypeStruct((members, site_count), cells.dtype),
         ),
         grid=(members // block,),
-        in_specs=[big, thin, thin, big, whole3, whole3, whole2, picks,
+        in_specs=[big, thin, thin, pl.BlockSpec((8, flat_rows // (members // block)), lambda i: (0, i)), whole3, whole3, whole2, picks,
                   pl.BlockSpec((rows_all, site_count), lambda i: (0, 0))],
         out_specs=(big, pl.BlockSpec((block, site_count), lambda i: (i, 0))),
         scratch_shapes=[

time: 129 us -> 130 us (level)
  the two profiles are of different devices: /device:TPU:4 before, /device:TPU:96 now
where the time goes in v7:
time: 130 us
  Pallas kernels  104 us (80%)
  starting transfers between devices  14.4 us (11%)
  local copies, waits for them, and re-layouts  7.03 us (5%)
  other arithmetic  2.9 us (2%)
  waiting for transfers between devices  1.48 us (1%)
    pallas_call x1, Pallas kernels, run_analysis(): pl.pallas_call(functools.partial(analysis_kernel, nx, ny), out_shape=jax....  69.1 us
    pallas_call x1, Pallas kernels, forecast_step(): pl.pallas_call(stencil_kernel, out_shape=(jax.ShapeDtypeStruct(cells.shap...  16.6 us
    pallas_call x1, Pallas kernels, apply_transform(): pl.pallas_call(transform_kernel, out_shape=jax.ShapeDtypeStruct(cells.sha...  10.2 us
    pallas_call x1, Pallas kernels, forecast_step(): pl.pallas_call(pick_kernel, out_shape=jax.ShapeDtypeStruct((8, flat_rows)...  7.65 us
    ppermute x1, starting transfers between devices, forecast_step(): lax.ppermute(cells[:, :, :, 0:1, :], 'gx', [(i + 1, i) for i in range(nx...  6.58 us
    ppermute x1, starting transfers between devices, forecast_step(): lax.ppermute(cells[:, :, :, rows - 1:rows, :], 'gx', [(i, i + 1) for i in...  3.48 us
    slice x1, local copies, waits for them, and re-layouts, forecast_step(): cells[:, :, :, rows - 1:rows, :]  2.79 us
  transfers between devices with their start and end apart: 4, of which 1 were waited for; matrix products, arithmetic and copies ran while one was open for 5% of the time, Pallas kernels for 0%

profile of v7, /device:TPU:96, one launch (start us, length us, event | category | flops | bytes accessed | tf_op | source)
XLA Modules:
  0.0 129.6 jit_solution(5922982053636904092)
XLA Ops:
  0.0 0.0 copy-start.5
  0.0 0.0 copy-start.3
  0.1 0.6 copy-done.2
  0.7 7.6 %shard_map.91 = f32[8,8192]{1,0:T(8,128)} custom-call(f32[8,128]{1,0:T(8,128)} %copy-done.2, f32[8192,128]{1,0:T(8,128)} %bitcast.33), custom_call_target="tpu_custom_call" | custom-call | tf_op jit(solution)/shard_map/pallas_call | solution.py:93
  8.3 1.1 fusion.5
  9.4 1.9 %collective-permute-start.2 = (f32[1,8192]{1,0:T(1,128)S(1)}, f32[1,8192]{1,0:T(1,128)S(1)}, u32[]{:S(2)}, u32[]{:S(2)}) collective-permute-start(f32[1,8192]{1,0:T(1,128)S(1)} %get-tuple-element.35), channel_id=1, source_target_pairs={{1,0},{2,1},{3,2},{4,3},{5,4},{6,5},{7,6},{9,8},{10,9},{11,10},{12... | collective-permute-start | bytes 98312 | tf_op jit(solution)/shard_map/ppermute | solution.py:100
  11.4 2.4 %collective-permute-start.3 = (f32[1,8192]{1,0:T(1,128)S(1)}, f32[1,8192]{1,0:T(1,128)S(1)}, u32[]{:S(2)}, u32[]{:S(2)}) collective-permute-start(f32[1,8192]{1,0:T(1,128)S(1)} %get-tuple-element.36), channel_id=1, source_target_pairs={{0,1},{1,2},{2,3},{3,4},{4,5},{5,6},{6,7},{8,9},{9,10},{10,11},{11... | collective-permute-start | bytes 98312 | tf_op jit(solution)/shard_map/ppermute | solution.py:101
  13.8 2.8 %fusion.4 = (f32[64,2,4,1,128]{4,3,2,1,0:T(1,128)S(1)}, f32[64,2,4,1,128]{4,3,2,1,0:T(1,128)S(1)}) fusion(f32[64,2,4,16,128]{4,3,2,1,0:T(8,128)} %x_ref.1), kind=kLoop, calls=%fused_computation.23 | loop fusion | bytes 1048576 | tf_op jit(solution)/shard_map/slice | solution.py:86
  16.6 3.5 %collective-permute-start.1 = (f32[64,2,4,1,128]{4,3,2,1,0:T(1,128)S(1)}, f32[64,2,4,1,128]{4,3,2,1,0:T(1,128)S(1)}, u32[]{:S(2)}, u32[]{:S(2)}) collective-permute-start(f32[64,2,4,1,128]{4,3,2,1,0:T(1,128)S(1)} %get-tuple-element.33), channel_id=1, source_target_pairs={{0,8},{8,16},{16,24},{24,32},{32,40},{40,48},{48,56},{56,64},{64,7... | collective-permute-start | bytes 786440 | tf_op jit(solution)/shard_map/ppermute | solution.py:86
  20.1 6.6 %collective-permute-start = (f32[64,2,4,1,128]{4,3,2,1,0:T(1,128)S(1)}, f32[64,2,4,1,128]{4,3,2,1,0:T(1,128)S(1)}, u32[]{:S(2)}, u32[]{:S(2)}) collective-permute-start(f32[64,2,4,1,128]{4,3,2,1,0:T(1,128)S(1)} %get-tuple-element.34), channel_id=1, source_target_pairs={{8,0},{16,8},{24,16},{32,24},{40,32},{48,40},{56,48},{64,56},{72,6... | collective-permute-start | bytes 786440 | tf_op jit(solution)/shard_map/ppermute | solution.py:85
  26.7 0.0 copy-done.5
  26.7 0.1 and_convert_fusion
  26.8 0.0 copy-done.4
  26.8 0.0 copy-done.6
  26.8 0.6 compare_select_fusion.scale_ref
  27.4 0.8 fusion
  28.2 0.0 copy-done.3
  28.3 0.1 reshape.227
  28.3 0.1 convert_element_type.39
  28.4 0.1 pad.8.clone
  28.5 0.5 max.4.w_ref
  29.0 0.0 collective-permute-done.2
  29.0 0.0 collective-permute-done.3
  29.0 0.8 maximum_maximum_fusion.halo_ref
  29.8 0.0 collective-permute-done.1.west_ref
  29.8 1.5 %collective-permute-done.east_ref = f32[64,2,4,1,128]{4,3,2,1,0:T(1,128)S(1)} collective-permute-done((f32[64,2,4,1,128]{4,3,2,1,0:T(1,128)S(1)}, f32[64,2,4,1,128]{4,3,2,1,0:T(1,128)S(1)}, u32[]{:S(2)}, u32[]{:S(2)}) %collective-permute-start) | collective-permute-done | bytes 262176 | tf_op jit(solution)/shard_map/ppermute | solution.py:85
  31.3 0.0 copy-done
  31.3 0.7 copy-done.1
  32.0 16.6 %shard_map.92 = (f32[64,2,4,16,128]{4,3,2,1,0:T(8,128)}, f32[64,512]{1,0:T(8,128)}) custom-call(f32[64,2,4,16,128]{4,3,2,1,0:T(8,128)} %x_ref.1, f32[64,2,4,1,128]{4,3,2,1,0:T(1,128)} %copy-done.1, f32[64,2,4,1,128]{4,3,2,1,0:T(1,128)} %copy-done, f32[8,8192]{1,0:T(8,128)} %maximum_maximum_fusion.halo_ref, f32[2,16,128]{2,1,0:T(8,128)} %u_ref.1, ...), custom_call_target="tpu_custom_call" | custom-call | tf_op jit(solution)/shard_map/pallas_call | solution.py:114
  48.6 1.6 %bitcast_bitcast_fusion.y_ref = f32[4,64,128]{2,1,0:T(8,128)} fusion(f32[64,512]{1,0:T(8,128)} %get-tuple-element.31), kind=kLoop, calls=%fused_computation.5 | loop fusion | bytes 262144 | tf_op jit(solution)/shard_map/transpose | solution.py:366
  50.2 69.1 %shard_map.93.p_ref = f32[64,64]{1,0:T(8,128)} custom-call(f32[4,64,128]{2,1,0:T(8,128)} %bitcast_bitcast_fusion.y_ref, f32[4,1,128]{2,1,0:T(1,128)} %compare_select_fusion.scale_ref, f32[4,1,128]{2,1,0:T(1,128)} %bitcast.35, f32[25]{0:T(128)} %max.4.w_ref), custom_call_target="tpu_custom_call" | custom-call | tf_op jit(solution)/shard_map/pallas_call | solution.py:275
  119.3 10.2 %shard_map.94 = f32[64,2,4,16,128]{4,3,2,1,0:T(8,128)} custom-call(f32[64,64]{1,0:T(8,128)} %shard_map.93.p_ref, f32[64,2,4,16,128]{4,3,2,1,0:T(8,128)} %get-tuple-element.32.x_ref), custom_call_target="tpu_custom_call" | custom-call | tf_op jit(solution)/shard_map/pallas_call | solution.py:328
  (14 shorter events, 0.1 us)
Async XLA Ops:
  0.0 26.7 %copy-start.5 = (f32[1,1,4,128]{3,2,1,0:T(4,128)S(1)}, f32[1,1,4,128]{3,2,1,0:T(4,128)}, u32[]{:S(2)}) copy-start(f32[1,1,4,128]{3,2,1,0:T(4,128)} %param.20) | copy-start | bytes 6148
  0.0 26.8 %copy-start.4 = (s32[1,1,4,128]{3,2,1,0:T(4,128)S(1)}, s32[1,1,4,128]{3,2,1,0:T(4,128)}, u32[]{:S(2)}) copy-start(s32[1,1,4,128]{3,2,1,0:T(4,128)} %param.17) | copy-start | bytes 6148
  0.0 26.8 %copy-start.6 = (s32[1,1,4]{2,1,0:T(1,128)S(1)}, s32[1,1,4]{2,1,0:T(1,128)}, u32[]{:S(2)}) copy-start(s32[1,1,4]{2,1,0:T(1,128)} %param.18) | copy-start | bytes 52
  0.0 28.2 %copy-start.3 = (s32[1,1,5,5]{3,1,2,0:T(1,128)S(1)}, s32[1,1,5,5]{3,1,2,0:T(1,128)}, u32[]{:S(2)}) copy-start(s32[1,1,5,5]{3,1,2,0:T(1,128)} %param.21) | copy-start | bytes 304
  0.1 0.6 copy-start.2
  9.4 19.6 %collective-permute-start.2 = (f32[1,8192]{1,0:T(1,128)S(1)}, f32[1,8192]{1,0:T(1,128)S(1)}, u32[]{:S(2)}, u32[]{:S(2)}) collective-permute-start(f32[1,8192]{1,0:T(1,128)S(1)} %get-tuple-element.35), channel_id=1, source_target_pairs={{1,0},{2,1},{3,2},{4,3},{5,4},{6,5},{7,6},{9,8},{10,9},{11,10},{12... | collective-permute-start | bytes 98312 | tf_op jit(solution)/shard_map/ppermute | solution.py:100
  11.4 17.7 %collective-permute-start.3 = (f32[1,8192]{1,0:T(1,128)S(1)}, f32[1,8192]{1,0:T(1,128)S(1)}, u32[]{:S(2)}, u32[]{:S(2)}) collective-permute-start(f32[1,8192]{1,0:T(1,128)S(1)} %get-tuple-element.36), channel_id=1, source_target_pairs={{0,1},{1,2},{2,3},{3,4},{4,5},{5,6},{6,7},{8,9},{9,10},{10,11},{11... | collective-permute-start | bytes 98312 | tf_op jit(solution)/shard_map/ppermute | solution.py:101
  16.6 13.3 %collective-permute-start.1 = (f32[64,2,4,1,128]{4,3,2,1,0:T(1,128)S(1)}, f32[64,2,4,1,128]{4,3,2,1,0:T(1,128)S(1)}, u32[]{:S(2)}, u32[]{:S(2)}) collective-permute-start(f32[64,2,4,1,128]{4,3,2,1,0:T(1,128)S(1)} %get-tuple-element.33), channel_id=1, source_target_pairs={{0,8},{8,16},{16,24},{24,32},{32,40},{40,48},{48,56},{56,64},{64,7... | collective-permute-start | bytes 786440 | tf_op jit(solution)/shard_map/ppermute | solution.py:86
  20.1 11.2 %collective-permute-start = (f32[64,2,4,1,128]{4,3,2,1,0:T(1,128)S(1)}, f32[64,2,4,1,128]{4,3,2,1,0:T(1,128)S(1)}, u32[]{:S(2)}, u32[]{:S(2)}) collective-permute-start(f32[64,2,4,1,128]{4,3,2,1,0:T(1,128)S(1)} %get-tuple-element.34), channel_id=1, source_target_pairs={{8,0},{16,8},{24,16},{32,24},{40,32},{48,40},{56,48},{64,56},{72,6... | collective-permute-start | bytes 786440 | tf_op jit(solution)/shard_map/ppermute | solution.py:85
  29.8 1.5 %copy-start = (f32[64,2,4,1,128]{4,3,2,1,0:T(1,128)}, f32[64,2,4,1,128]{4,3,2,1,0:T(1,128)S(1)}, u32[]{:S(2)}) copy-start(f32[64,2,4,1,128]{4,3,2,1,0:T(1,128)S(1)} %collective-permute-done.1.west_ref) | copy-start | bytes 786436
  31.3 0.7 copy-start.1

commit v8 on v6

--- a/solution.py
+++ b/solution.py
@@ -239,7 +239,8 @@
         def ns_step(_, pair):
             iterate, inverse = pair
             factor = 1.5 * identity - 0.5 * mm(inverse, iterate)
-            return mm(iterate, factor), mm(factor, inverse)
+            both = mm(jnp.concatenate([iterate, inverse], axis=0), factor)
+            return both[0:members], both[members : 2 * members]
 
         pair = (iterate, identity)
         for _i in range(NS_STEPS):

time: 129 us -> 128 us (level)
  the two profiles are of different devices: /device:TPU:4 before, /device:TPU:96 now
where the time goes in v8:
time: 128 us; the launch traced here: 127 us
  Pallas kernels  89.9 us (70%)
  matrix products  13.6 us (11%)
  starting transfers between devices  12.9 us (10%)
  local copies, waits for them, and re-layouts  5.78 us (5%)
  waiting for transfers between devices  2.74 us (2%)
  other arithmetic  2.11 us (2%)
    pallas_call x1, Pallas kernels, run_analysis(): pl.pallas_call(functools.partial(analysis_kernel, nx, ny), out_shape=jax....  67.9 us
    pallas_call x1, Pallas kernels, forecast_step(): pl.pallas_call(stencil_kernel, out_shape=(jax.ShapeDtypeStruct(cells.shap...  11.8 us
    pallas_call x1, Pallas kernels, apply_transform(): pl.pallas_call(transform_kernel, out_shape=jax.ShapeDtypeStruct(cells.sha...  10.2 us
    dot_general x1, matrix products, forecast_step(): jnp.einsum('abcil,sl->sabci', cells, pick, precision=lax.Precision.HIGHES...  8.5 us
    ppermute x1, starting transfers between devices, forecast_step(): lax.ppermute(cells[:, :, :, 0:1, :], 'gx', [(i + 1, i) for i in range(nx...  6.66 us
    dot_general x1, matrix products, forecast_step(): jnp.einsum('sabci,sl->abcil', jnp.stack([north_halo, south_halo]), place,...  5.07 us
    slice x1, local copies, waits for them, and re-layouts, forecast_step(): cells[:, :, :, rows - 1:rows, :]  2.79 us
    ppermute x1, waiting for transfers between devices, forecast_step(): lax.ppermute(cells[:, :, :, rows - 1:rows, :], 'gx', [(i, i + 1) for i in...  2.73 us
  transfers between devices with their start and end apart: 4, of which 1 were waited for; matrix products, arithmetic and copies ran while one was open for 8% of the time, Pallas kernels for 0%

profile of v8, /device:TPU:96, one launch (start us, length us, event | category | flops | bytes accessed | tf_op | source)
XLA Modules:
  0.0 127.1 jit_solution(1154088365021057602)
XLA Ops:
  0.0 0.0 copy-start.3
  0.0 0.0 copy-start.4
  0.0 0.0 copy-start.2
  0.0 8.5 %fusion = f32[2,64,2,4,16]{1,0,4,3,2:T(2,128)S(1)} fusion(f32[64,2,4,16,128]{4,3,2,1,0:T(8,128)} %x_ref.1, pred[1,128]{1,0:T(4,128)(4,1)S(1)} %get-tuple-element.15, pred[1,128]{1,0:T(4,128)(4,1)S(1)} %get-tuple-element.16), kind=kOutput, calls=%fused_computation | convolution fusion | flops 25166080 | bytes 4260096 | tf_op jit(solution)/shard_map/abcil,sl->sabci/dot_general | solution.py:82
  8.5 0.1 fusion.14
  8.7 1.9 %collective-permute-start.2 = (f32[64,2,4,16]{0,3,2,1:T(8,128)S(1)}, f32[64,2,4,16]{0,3,2,1:T(8,128)S(1)}, u32[]{:S(2)}, u32[]{:S(2)}) collective-permute-start(f32[64,2,4,16]{0,3,2,1:T(8,128)S(1)} %bitcast.51), channel_id=1, source_target_pairs={{1,0},{2,1},{3,2},{4,3},{5,4},{6,5},{7,6},{9,8},{10,9},{11,10},{12... | collective-permute-start | bytes 98312 | tf_op jit(solution)/shard_map/ppermute | solution.py:86
  10.6 2.4 %collective-permute-start.3 = (f32[64,2,4,16]{0,3,2,1:T(8,128)S(1)}, f32[64,2,4,16]{0,3,2,1:T(8,128)S(1)}, u32[]{:S(2)}, u32[]{:S(2)}) collective-permute-start(f32[64,2,4,16]{0,3,2,1:T(8,128)S(1)} %bitcast.49), channel_id=1, source_target_pairs={{0,1},{1,2},{2,3},{3,4},{4,5},{5,6},{6,7},{8,9},{9,10},{10,11},{11... | collective-permute-start | bytes 98312 | tf_op jit(solution)/shard_map/ppermute | solution.py:87
  13.0 2.8 %fusion.13 = (f32[64,2,4,1,128]{4,3,2,1,0:T(1,128)S(1)}, f32[64,2,4,1,128]{4,3,2,1,0:T(1,128)S(1)}) fusion(f32[64,2,4,16,128]{4,3,2,1,0:T(8,128)} %x_ref.1), kind=kLoop, calls=%fused_computation.33 | loop fusion | bytes 1048576 | tf_op jit(solution)/shard_map/slice | solution.py:78
  15.8 6.7 %collective-permute-start = (f32[64,2,4,1,128]{4,3,2,1,0:T(1,128)S(1)}, f32[64,2,4,1,128]{4,3,2,1,0:T(1,128)S(1)}, u32[]{:S(2)}, u32[]{:S(2)}) collective-permute-start(f32[64,2,4,1,128]{4,3,2,1,0:T(1,128)S(1)} %get-tuple-element.10), channel_id=1, source_target_pairs={{8,0},{16,8},{24,16},{32,24},{40,32},{48,40},{56,48},{64,56},{72,6... | collective-permute-start | bytes 786440 | tf_op jit(solution)/shard_map/ppermute | solution.py:77
  22.5 1.9 %collective-permute-start.1 = (f32[64,2,4,1,128]{4,3,2,1,0:T(1,128)S(1)}, f32[64,2,4,1,128]{4,3,2,1,0:T(1,128)S(1)}, u32[]{:S(2)}, u32[]{:S(2)}) collective-permute-start(f32[64,2,4,1,128]{4,3,2,1,0:T(1,128)S(1)} %get-tuple-element.9), channel_id=1, source_target_pairs={{0,8},{8,16},{16,24},{24,32},{32,40},{40,48},{48,56},{56,64},{64,7... | collective-permute-start | bytes 786440 | tf_op jit(solution)/shard_map/ppermute | solution.py:78
  24.4 0.0 copy-done.3
  24.4 0.1 and_convert_fusion
  24.5 0.0 copy-done.4
  24.5 0.8 fusion.2
  25.3 0.0 copy-done.5
  25.3 0.6 compare_select_fusion.scale_ref
  26.0 0.0 copy-done.2
  26.0 0.1 reshape.175
  26.1 0.1 convert_element_type.26
  26.1 0.5 max.4.w_ref
  26.7 0.0 collective-permute-done.2
  26.7 0.0 collective-permute-done.3
  26.7 0.4 copy.15
  27.1 5.1 %fusion.8.edge_ref = f32[64,2,4,16,128]{4,3,2,1,0:T(8,128)} fusion(f32[2,64,2,4,16]{4,0,3,2,1:T(2,128)S(1)} %copy.15, pred[1,128]{1,0:T(4,128)(4,1)S(1)} %get-tuple-element.16, pred[1,128]{1,0:T(4,128)(4,1)S(1)} %get-tuple-element.15), kind=kOutput, calls=%fused_computation.24 | convolution fusion | flops 25166080 | bytes 4260096 | tf_op jit(solution)/shard_map/sabci,sl->abcil/dot_general | solution.py:88
  32.2 0.0 collective-permute-done.east_ref
  32.2 2.7 %collective-permute-done.1.west_ref = f32[64,2,4,1,128]{4,3,2,1,0:T(1,128)S(1)} collective-permute-done((f32[64,2,4,1,128]{4,3,2,1,0:T(1,128)S(1)}, f32[64,2,4,1,128]{4,3,2,1,0:T(1,128)S(1)}, u32[]{:S(2)}, u32[]{:S(2)}) %collective-permute-start.1) | collective-permute-done | bytes 262176 | tf_op jit(solution)/shard_map/ppermute | solution.py:78
  35.0 0.0 copy-done
  35.0 0.7 copy-done.1
  35.7 11.8 %shard_map.91 = (f32[64,2,4,16,128]{4,3,2,1,0:T(8,128)}, f32[64,512]{1,0:T(8,128)}) custom-call(f32[64,2,4,16,128]{4,3,2,1,0:T(8,128)} %x_ref.1, f32[64,2,4,1,128]{4,3,2,1,0:T(1,128)} %copy-done, f32[64,2,4,1,128]{4,3,2,1,0:T(1,128)} %copy-done.1, f32[64,2,4,16,128]{4,3,2,1,0:T(8,128)} %fusion.8.edge_ref, f32[2,16,128]{2,1,0:T(8,128)} %u_ref.1, ...), custom_call_target="tpu_custom_call" | custom-call | tf_op jit(solution)/shard_map/pallas_call | solution.py:103
  47.4 1.6 %bitcast_bitcast_fusion.y_ref = f32[4,64,128]{2,1,0:T(8,128)} fusion(f32[64,512]{1,0:T(8,128)} %get-tuple-element.7), kind=kLoop, calls=%fused_computation.6 | loop fusion | bytes 262144 | tf_op jit(solution)/shard_map/transpose | solution.py:356
  49.0 67.9 %shard_map.92.p_ref = f32[64,64]{1,0:T(8,128)} custom-call(f32[4,64,128]{2,1,0:T(8,128)} %bitcast_bitcast_fusion.y_ref, f32[4,1,128]{2,1,0:T(1,128)} %compare_select_fusion.scale_ref, f32[4,1,128]{2,1,0:T(1,128)} %bitcast.54, f32[25]{0:T(128)} %max.4.w_ref), custom_call_target="tpu_custom_call" | custom-call | tf_op jit(solution)/shard_map/pallas_call | solution.py:265
  116.9 10.2 %shard_map.93 = f32[64,2,4,16,128]{4,3,2,1,0:T(8,128)} custom-call(f32[64,64]{1,0:T(8,128)} %shard_map.92.p_ref, f32[64,2,4,16,128]{4,3,2,1,0:T(8,128)} %get-tuple-element.8.x_ref), custom_call_target="tpu_custom_call" | custom-call | tf_op jit(solution)/shard_map/pallas_call | solution.py:318
  (9 shorter events, 0.1 us)
Async XLA Ops:
  0.0 24.4 %copy-start.3 = (s32[1,1,4,128]{3,2,1,0:T(4,128)S(1)}, s32[1,1,4,128]{3,2,1,0:T(4,128)}, u32[]{:S(2)}) copy-start(s32[1,1,4,128]{3,2,1,0:T(4,128)} %param.13) | copy-start | bytes 6148
  0.0 24.5 %copy-start.4 = (f32[1,1,4,128]{3,2,1,0:T(4,128)S(1)}, f32[1,1,4,128]{3,2,1,0:T(4,128)}, u32[]{:S(2)}) copy-start(f32[1,1,4,128]{3,2,1,0:T(4,128)} %param.16) | copy-start | bytes 6148
  0.0 25.3 %copy-start.5 = (s32[1,1,4]{2,1,0:T(1,128)S(1)}, s32[1,1,4]{2,1,0:T(1,128)}, u32[]{:S(2)}) copy-start(s32[1,1,4]{2,1,0:T(1,128)} %param.14) | copy-start | bytes 52
  0.0 26.0 %copy-start.2 = (s32[1,1,5,5]{3,1,2,0:T(1,128)S(1)}, s32[1,1,5,5]{3,1,2,0:T(1,128)}, u32[]{:S(2)}) copy-start(s32[1,1,5,5]{3,1,2,0:T(1,128)} %param.17) | copy-start | bytes 304
  8.7 18.0 %collective-permute-start.2 = (f32[64,2,4,16]{0,3,2,1:T(8,128)S(1)}, f32[64,2,4,16]{0,3,2,1:T(8,128)S(1)}, u32[]{:S(2)}, u32[]{:S(2)}) collective-permute-start(f32[64,2,4,16]{0,3,2,1:T(8,128)S(1)} %bitcast.51), channel_id=1, source_target_pairs={{1,0},{2,1},{3,2},{4,3},{5,4},{6,5},{7,6},{9,8},{10,9},{11,10},{12... | collective-permute-start | bytes 98312 | tf_op jit(solution)/shard_map/ppermute | solution.py:86
  10.6 16.1 %collective-permute-start.3 = (f32[64,2,4,16]{0,3,2,1:T(8,128)S(1)}, f32[64,2,4,16]{0,3,2,1:T(8,128)S(1)}, u32[]{:S(2)}, u32[]{:S(2)}) collective-permute-start(f32[64,2,4,16]{0,3,2,1:T(8,128)S(1)} %bitcast.49), channel_id=1, source_target_pairs={{0,1},{1,2},{2,3},{3,4},{4,5},{5,6},{6,7},{8,9},{9,10},{10,11},{11... | collective-permute-start | bytes 98312 | tf_op jit(solution)/shard_map/ppermute | solution.py:87
  15.8 16.4 %collective-permute-start = (f32[64,2,4,1,128]{4,3,2,1,0:T(1,128)S(1)}, f32[64,2,4,1,128]{4,3,2,1,0:T(1,128)S(1)}, u32[]{:S(2)}, u32[]{:S(2)}) collective-permute-start(f32[64,2,4,1,128]{4,3,2,1,0:T(1,128)S(1)} %get-tuple-element.10), channel_id=1, source_target_pairs={{8,0},{16,8},{24,16},{32,24},{40,32},{48,40},{56,48},{64,56},{72,6... | collective-permute-start | bytes 786440 | tf_op jit(solution)/shard_map/ppermute | solution.py:77
  22.5 12.5 %collective-permute-start.1 = (f32[64,2,4,1,128]{4,3,2,1,0:T(1,128)S(1)}, f32[64,2,4,1,128]{4,3,2,1,0:T(1,128)S(1)}, u32[]{:S(2)}, u32[]{:S(2)}) collective-permute-start(f32[64,2,4,1,128]{4,3,2,1,0:T(1,128)S(1)} %get-tuple-element.9), channel_id=1, source_target_pairs={{0,8},{8,16},{16,24},{24,32},{32,40},{40,48},{48,56},{56,64},{64,7... | collective-permute-start | bytes 786440 | tf_op jit(solution)/shard_map/ppermute | solution.py:78
  32.2 2.7 %copy-start = (f32[64,2,4,1,128]{4,3,2,1,0:T(1,128)}, f32[64,2,4,1,128]{4,3,2,1,0:T(1,128)S(1)}, u32[]{:S(2)}) copy-start(f32[64,2,4,1,128]{4,3,2,1,0:T(1,128)S(1)} %collective-permute-done.east_ref) | copy-start | bytes 786436
  34.9 0.7 copy-start.1

commit v9 on v8

--- a/solution.py
+++ b/solution.py
@@ -286,34 +286,16 @@
     )(y, scale, obs, weights)
 
 
-def transform_kernel(p_ref, x_ref, o_ref, k_scr):
-    members, rows, lanes = x_ref.shape[0], x_ref.shape[3], x_ref.shape[4]
-    sub = 8
-    size = members * sub
-
-    @pl.when((pl.program_id(0) == 0) & (pl.program_id(1) == 0))
-    def _():
-        spread = (
-            lax.broadcasted_iota(jnp.int32, (size, members), 0) // sub
-            == lax.broadcasted_iota(jnp.int32, (size, members), 1)
-        ).astype(jnp.float32)
-        full = mm_nt(mm(spread, p_ref[...]), spread)
-        same = (
-            lax.broadcasted_iota(jnp.int32, (size, size), 0) % sub
-            == lax.broadcasted_iota(jnp.int32, (size, size), 1) % sub
-        )
-        k_scr[...] = jnp.where(same, full, 0.0)
-
-    parts = [x_ref[:, 0, 0, h * sub : (h + 1) * sub, :].reshape(size, lanes) for h in range(rows // sub)]
-    mixed = jnp.dot(k_scr[...], jnp.concatenate(parts, axis=1),
-                    precision=lax.Precision.HIGH, preferred_element_type=jnp.float32)
-    for h in range(rows // sub):
-        o_ref[:, 0, 0, h * sub : (h + 1) * sub, :] = mixed[:, h * lanes : (h + 1) * lanes].reshape(members, sub, lanes)
+def transform_kernel(p_ref, x_ref, o_ref):
+    rows = x_ref.shape[3]
+    mix = p_ref[...]
+    for i in range(rows):
+        o_ref[:, 0, 0, i, :] = jnp.dot(mix, x_ref[:, 0, 0, i, :],
+                                       precision=lax.Precision.HIGH, preferred_element_type=jnp.float32)
 
 
 def apply_transform(carried, cells):
     members, levels, fields, rows, lanes = cells.shape
-    sub = 8
     block = pl.BlockSpec((members, 1, 1, rows, lanes), lambda a, b: (0, a, b, 0, 0))
     return pl.pallas_call(
         transform_kernel,
@@ -321,8 +303,6 @@
         grid=(levels, fields),
         in_specs=[pl.BlockSpec((members, members), lambda a, b: (0, 0)), block],
         out_specs=block,
-        scratch_shapes=[pltpu.VMEM((members * sub, members * sub), jnp.float32)],
-        compiler_params=pltpu.CompilerParams(dimension_semantics=("arbitrary", "arbitrary")),
     )(carried, cells)
 
 

time: 128 us -> 127 us (level)
  no operation moved by 1% of the time
where the time goes in v9:
time: 127 us; the launch traced here: 126 us
  Pallas kernels  88.9 us (70%)
  matrix products  13.6 us (11%)
  starting transfers between devices  12.9 us (10%)
  local copies, waits for them, and re-layouts  5.78 us (5%)
  waiting for transfers between devices  2.74 us (2%)
  other arithmetic  2.11 us (2%)
    pallas_call x1, Pallas kernels, run_analysis(): pl.pallas_call(functools.partial(analysis_kernel, nx, ny), out_shape=jax....  67.9 us
    pallas_call x1, Pallas kernels, forecast_step(): pl.pallas_call(stencil_kernel, out_shape=(jax.ShapeDtypeStruct(cells.shap...  11.8 us
    pallas_call x1, Pallas kernels, apply_transform(): pl.pallas_call(transform_kernel, out_shape=jax.ShapeDtypeStruct(cells.sha...  9.24 us
    dot_general x1, matrix products, forecast_step(): jnp.einsum('abcil,sl->sabci', cells, pick, precision=lax.Precision.HIGHES...  8.5 us
    ppermute x1, starting transfers between devices, forecast_step(): lax.ppermute(cells[:, :, :, 0:1, :], 'gx', [(i + 1, i) for i in range(nx...  6.66 us
    dot_general x1, matrix products, forecast_step(): jnp.einsum('sabci,sl->abcil', jnp.stack([north_halo, south_halo]), place,...  5.07 us
    slice x1, local copies, waits for them, and re-layouts, forecast_step(): cells[:, :, :, rows - 1:rows, :]  2.79 us
    ppermute x1, waiting for transfers between devices, forecast_step(): lax.ppermute(cells[:, :, :, rows - 1:rows, :], 'gx', [(i, i + 1) for i in...  2.73 us
  transfers between devices with their start and end apart: 4, of which 1 were waited for; matrix products, arithmetic and copies ran while one was open for 8% of the time, Pallas kernels for 0%

profile of v9, /device:TPU:96, one launch (start us, length us, event | category | flops | bytes accessed | tf_op | source)
XLA Modules:
  0.0 126.1 jit_solution(15070274289437847423)
XLA Ops:
  0.0 0.0 copy-start.3
  0.0 0.0 copy-start.4
  0.0 0.0 copy-start.2
  0.0 8.5 %fusion = f32[2,64,2,4,16]{1,0,4,3,2:T(2,128)S(1)} fusion(f32[64,2,4,16,128]{4,3,2,1,0:T(8,128)} %x_ref.1, pred[1,128]{1,0:T(4,128)(4,1)S(1)} %get-tuple-element.15, pred[1,128]{1,0:T(4,128)(4,1)S(1)} %get-tuple-element.16), kind=kOutput, calls=%fused_computation | convolution fusion | flops 25166080 | bytes 4260096 | tf_op jit(solution)/shard_map/abcil,sl->sabci/dot_general | solution.py:82
  8.5 0.1 fusion.14
  8.7 1.9 %collective-permute-start.2 = (f32[64,2,4,16]{0,3,2,1:T(8,128)S(1)}, f32[64,2,4,16]{0,3,2,1:T(8,128)S(1)}, u32[]{:S(2)}, u32[]{:S(2)}) collective-permute-start(f32[64,2,4,16]{0,3,2,1:T(8,128)S(1)} %bitcast.51), channel_id=1, source_target_pairs={{1,0},{2,1},{3,2},{4,3},{5,4},{6,5},{7,6},{9,8},{10,9},{11,10},{12... | collective-permute-start | bytes 98312 | tf_op jit(solution)/shard_map/ppermute | solution.py:86
  10.6 2.4 %collective-permute-start.3 = (f32[64,2,4,16]{0,3,2,1:T(8,128)S(1)}, f32[64,2,4,16]{0,3,2,1:T(8,128)S(1)}, u32[]{:S(2)}, u32[]{:S(2)}) collective-permute-start(f32[64,2,4,16]{0,3,2,1:T(8,128)S(1)} %bitcast.49), channel_id=1, source_target_pairs={{0,1},{1,2},{2,3},{3,4},{4,5},{5,6},{6,7},{8,9},{9,10},{10,11},{11... | collective-permute-start | bytes 98312 | tf_op jit(solution)/shard_map/ppermute | solution.py:87
  13.0 2.8 %fusion.13 = (f32[64,2,4,1,128]{4,3,2,1,0:T(1,128)S(1)}, f32[64,2,4,1,128]{4,3,2,1,0:T(1,128)S(1)}) fusion(f32[64,2,4,16,128]{4,3,2,1,0:T(8,128)} %x_ref.1), kind=kLoop, calls=%fused_computation.33 | loop fusion | bytes 1048576 | tf_op jit(solution)/shard_map/slice | solution.py:78
  15.8 6.7 %collective-permute-start = (f32[64,2,4,1,128]{4,3,2,1,0:T(1,128)S(1)}, f32[64,2,4,1,128]{4,3,2,1,0:T(1,128)S(1)}, u32[]{:S(2)}, u32[]{:S(2)}) collective-permute-start(f32[64,2,4,1,128]{4,3,2,1,0:T(1,128)S(1)} %get-tuple-element.10), channel_id=1, source_target_pairs={{8,0},{16,8},{24,16},{32,24},{40,32},{48,40},{56,48},{64,56},{72,6... | collective-permute-start | bytes 786440 | tf_op jit(solution)/shard_map/ppermute | solution.py:77
  22.5 1.9 %collective-permute-start.1 = (f32[64,2,4,1,128]{4,3,2,1,0:T(1,128)S(1)}, f32[64,2,4,1,128]{4,3,2,1,0:T(1,128)S(1)}, u32[]{:S(2)}, u32[]{:S(2)}) collective-permute-start(f32[64,2,4,1,128]{4,3,2,1,0:T(1,128)S(1)} %get-tuple-element.9), channel_id=1, source_target_pairs={{0,8},{8,16},{16,24},{24,32},{32,40},{40,48},{48,56},{56,64},{64,7... | collective-permute-start | bytes 786440 | tf_op jit(solution)/shard_map/ppermute | solution.py:78
  24.4 0.0 copy-done.3
  24.4 0.1 and_convert_fusion
  24.5 0.0 copy-done.4
  24.5 0.8 fusion.2
  25.3 0.0 copy-done.5
  25.3 0.6 compare_select_fusion.scale_ref
  26.0 0.0 copy-done.2
  26.0 0.1 reshape.175
  26.1 0.1 convert_element_type.26
  26.1 0.5 max.4.w_ref
  26.7 0.0 collective-permute-done.2
  26.7 0.0 collective-permute-done.3
  26.7 0.4 copy.15
  27.1 5.1 %fusion.8.edge_ref = f32[64,2,4,16,128]{4,3,2,1,0:T(8,128)} fusion(f32[2,64,2,4,16]{4,0,3,2,1:T(2,128)S(1)} %copy.15, pred[1,128]{1,0:T(4,128)(4,1)S(1)} %get-tuple-element.16, pred[1,128]{1,0:T(4,128)(4,1)S(1)} %get-tuple-element.15), kind=kOutput, calls=%fused_computation.24 | convolution fusion | flops 25166080 | bytes 4260096 | tf_op jit(solution)/shard_map/sabci,sl->abcil/dot_general | solution.py:88
  32.2 0.0 collective-permute-done.east_ref
  32.2 2.7 %collective-permute-done.1.west_ref = f32[64,2,4,1,128]{4,3,2,1,0:T(1,128)S(1)} collective-permute-done((f32[64,2,4,1,128]{4,3,2,1,0:T(1,128)S(1)}, f32[64,2,4,1,128]{4,3,2,1,0:T(1,128)S(1)}, u32[]{:S(2)}, u32[]{:S(2)}) %collective-permute-start.1) | collective-permute-done | bytes 262176 | tf_op jit(solution)/shard_map/ppermute | solution.py:78
  35.0 0.0 copy-done
  35.0 0.7 copy-done.1
  35.7 11.8 %shard_map.91 = (f32[64,2,4,16,128]{4,3,2,1,0:T(8,128)}, f32[64,512]{1,0:T(8,128)}) custom-call(f32[64,2,4,16,128]{4,3,2,1,0:T(8,128)} %x_ref.1, f32[64,2,4,1,128]{4,3,2,1,0:T(1,128)} %copy-done, f32[64,2,4,1,128]{4,3,2,1,0:T(1,128)} %copy-done.1, f32[64,2,4,16,128]{4,3,2,1,0:T(8,128)} %fusion.8.edge_ref, f32[2,16,128]{2,1,0:T(8,128)} %u_ref.1, ...), custom_call_target="tpu_custom_call" | custom-call | tf_op jit(solution)/shard_map/pallas_call | solution.py:103
  47.4 1.6 %bitcast_bitcast_fusion.y_ref = f32[4,64,128]{2,1,0:T(8,128)} fusion(f32[64,512]{1,0:T(8,128)} %get-tuple-element.7), kind=kLoop, calls=%fused_computation.6 | loop fusion | bytes 262144 | tf_op jit(solution)/shard_map/transpose | solution.py:336
  49.0 67.9 %shard_map.92.p_ref = f32[64,64]{1,0:T(8,128)} custom-call(f32[4,64,128]{2,1,0:T(8,128)} %bitcast_bitcast_fusion.y_ref, f32[4,1,128]{2,1,0:T(1,128)} %compare_select_fusion.scale_ref, f32[4,1,128]{2,1,0:T(1,128)} %bitcast.54, f32[25]{0:T(128)} %max.4.w_ref), custom_call_target="tpu_custom_call" | custom-call | tf_op jit(solution)/shard_map/pallas_call | solution.py:265
  116.9 9.2 %shard_map.93 = f32[64,2,4,16,128]{4,3,2,1,0:T(8,128)} custom-call(f32[64,64]{1,0:T(8,128)} %shard_map.92.p_ref, f32[64,2,4,16,128]{4,3,2,1,0:T(8,128)} %get-tuple-element.8.x_ref), custom_call_target="tpu_custom_call" | custom-call | tf_op jit(solution)/shard_map/pallas_call | solution.py:300
  (9 shorter events, 0.1 us)
Async XLA Ops:
  0.0 24.4 %copy-start.3 = (s32[1,1,4,128]{3,2,1,0:T(4,128)S(1)}, s32[1,1,4,128]{3,2,1,0:T(4,128)}, u32[]{:S(2)}) copy-start(s32[1,1,4,128]{3,2,1,0:T(4,128)} %param.13) | copy-start | bytes 6148
  0.0 24.5 %copy-start.4 = (f32[1,1,4,128]{3,2,1,0:T(4,128)S(1)}, f32[1,1,4,128]{3,2,1,0:T(4,128)}, u32[]{:S(2)}) copy-start(f32[1,1,4,128]{3,2,1,0:T(4,128)} %param.16) | copy-start | bytes 6148
  0.0 25.3 %copy-start.5 = (s32[1,1,4]{2,1,0:T(1,128)S(1)}, s32[1,1,4]{2,1,0:T(1,128)}, u32[]{:S(2)}) copy-start(s32[1,1,4]{2,1,0:T(1,128)} %param.14) | copy-start | bytes 52
  0.0 26.0 %copy-start.2 = (s32[1,1,5,5]{3,1,2,0:T(1,128)S(1)}, s32[1,1,5,5]{3,1,2,0:T(1,128)}, u32[]{:S(2)}) copy-start(s32[1,1,5,5]{3,1,2,0:T(1,128)} %param.17) | copy-start | bytes 304
  8.7 18.0 %collective-permute-start.2 = (f32[64,2,4,16]{0,3,2,1:T(8,128)S(1)}, f32[64,2,4,16]{0,3,2,1:T(8,128)S(1)}, u32[]{:S(2)}, u32[]{:S(2)}) collective-permute-start(f32[64,2,4,16]{0,3,2,1:T(8,128)S(1)} %bitcast.51), channel_id=1, source_target_pairs={{1,0},{2,1},{3,2},{4,3},{5,4},{6,5},{7,6},{9,8},{10,9},{11,10},{12... | collective-permute-start | bytes 98312 | tf_op jit(solution)/shard_map/ppermute | solution.py:86
  10.6 16.1 %collective-permute-start.3 = (f32[64,2,4,16]{0,3,2,1:T(8,128)S(1)}, f32[64,2,4,16]{0,3,2,1:T(8,128)S(1)}, u32[]{:S(2)}, u32[]{:S(2)}) collective-permute-start(f32[64,2,4,16]{0,3,2,1:T(8,128)S(1)} %bitcast.49), channel_id=1, source_target_pairs={{0,1},{1,2},{2,3},{3,4},{4,5},{5,6},{6,7},{8,9},{9,10},{10,11},{11... | collective-permute-start | bytes 98312 | tf_op jit(solution)/shard_map/ppermute | solution.py:87
  15.8 16.4 %collective-permute-start = (f32[64,2,4,1,128]{4,3,2,1,0:T(1,128)S(1)}, f32[64,2,4,1,128]{4,3,2,1,0:T(1,128)S(1)}, u32[]{:S(2)}, u32[]{:S(2)}) collective-permute-start(f32[64,2,4,1,128]{4,3,2,1,0:T(1,128)S(1)} %get-tuple-element.10), channel_id=1, source_target_pairs={{8,0},{16,8},{24,16},{32,24},{40,32},{48,40},{56,48},{64,56},{72,6... | collective-permute-start | bytes 786440 | tf_op jit(solution)/shard_map/ppermute | solution.py:77
  22.5 12.5 %collective-permute-start.1 = (f32[64,2,4,1,128]{4,3,2,1,0:T(1,128)S(1)}, f32[64,2,4,1,128]{4,3,2,1,0:T(1,128)S(1)}, u32[]{:S(2)}, u32[]{:S(2)}) collective-permute-start(f32[64,2,4,1,128]{4,3,2,1,0:T(1,128)S(1)} %get-tuple-element.9), channel_id=1, source_target_pairs={{0,8},{8,16},{16,24},{24,32},{32,40},{40,48},{48,56},{56,64},{64,7... | collective-permute-start | bytes 786440 | tf_op jit(solution)/shard_map/ppermute | solution.py:78
  32.2 2.7 %copy-start = (f32[64,2,4,1,128]{4,3,2,1,0:T(1,128)}, f32[64,2,4,1,128]{4,3,2,1,0:T(1,128)S(1)}, u32[]{:S(2)}) copy-start(f32[64,2,4,1,128]{4,3,2,1,0:T(1,128)S(1)} %collective-permute-done.east_ref) | copy-start | bytes 786436
  34.9 0.7 copy-start.1

commit v10 on v9

--- a/solution.py
+++ b/solution.py
@@ -44,10 +44,24 @@
     centre = x_ref[...]
     east_cell = east_scr[...]
     west_cell = west_scr[...]
-    edge = edge_ref[...]
+    sides = edge_ref[...]
+    count = centre.size // lanes
+    spread = (
+        lax.broadcasted_iota(jnp.int32, (count, sides.shape[1]), 0) // rows
+        == lax.broadcasted_iota(jnp.int32, (count, sides.shape[1]), 1)
+    ).astype(jnp.float32)
+    own = (
+        lax.broadcasted_iota(jnp.int32, (count, lanes), 0) % rows
+        == lax.broadcasted_iota(jnp.int32, (count, lanes), 1)
+    )
+
+    def expand(side):
+        column = jnp.sum(jnp.where(own, mm(spread, side), 0.0), axis=1, keepdims=True)
+        return jnp.broadcast_to(column, (count, lanes)).reshape(centre.shape)
+
     lane = lax.broadcasted_iota(jnp.int32, centre.shape, 4)
-    north_cell = jnp.where(lane == lanes - 1, edge, pltpu.roll(centre, lanes - 1, 4))
-    south_cell = jnp.where(lane == 0, edge, pltpu.roll(centre, 1, 4))
+    north_cell = jnp.where(lane == lanes - 1, expand(sides[0]), pltpu.roll(centre, lanes - 1, 4))
+    south_cell = jnp.where(lane == 0, expand(sides[1]), pltpu.roll(centre, 1, 4))
     u = u_ref[...][None, :, None]
     v = v_ref[...][None, :, None]
     d = d_ref[...][None, None, None]
@@ -78,17 +92,14 @@
     west_halo = lax.ppermute(cells[:, :, :, rows - 1 : rows, :], "gx", [(i, i + 1) for i in range(nx - 1)])
     lane_index = jnp.arange(lanes)
     pick = jnp.stack([lane_index == 0, lane_index == lanes - 1]).astype(jnp.float32)
-    place = jnp.stack([lane_index == lanes - 1, lane_index == 0]).astype(jnp.float32)
     sides = jnp.einsum(
         "abcil,sl->sabci",
         cells, pick, precision=lax.Precision.HIGHEST, preferred_element_type=jnp.float32,
     )
     north_halo = lax.ppermute(sides[0], "gy", [(i + 1, i) for i in range(ny - 1)])
     south_halo = lax.ppermute(sides[1], "gy", [(i, i + 1) for i in range(ny - 1)])
-    edge = jnp.einsum(
-        "sabci,sl->abcil", jnp.stack([north_halo, south_halo]), place,
-        precision=lax.Precision.HIGHEST, preferred_element_type=jnp.float32,
-    )
+    flat_halo = jnp.stack([north_halo, south_halo]).reshape(2, -1, rows)
+    edge = jnp.pad(flat_halo, ((0, 0), (0, 0), (0, lanes - rows)))
     block = 8
     members = cells.shape[0]
     big = pl.BlockSpec((block,) + cells.shape[1:], lambda i: (i, 0, 0, 0, 0))
@@ -107,7 +118,7 @@
             jax.ShapeDtypeStruct((members, site_count), cells.dtype),
         ),
         grid=(members // block,),
-        in_specs=[big, thin, thin, big, whole3, whole3, whole2, picks,
+        in_specs=[big, thin, thin, pl.BlockSpec((2, block * cells.shape[1] * cells.shape[2], lanes), lambda i: (0, i, 0)), whole3, whole3, whole2, picks,
                   pl.BlockSpec((rows_all, site_count), lambda i: (0, 0))],
         out_specs=(big, pl.BlockSpec((block, site_count), lambda i: (i, 0))),
         scratch_shapes=[

time: 127 us -> 152 us (1.20)
  Pallas kernels: 88.9 us -> 114 us
  matrix products: 13.6 us -> 8.5 us
  starting transfers between devices: 12.9 us -> 16.5 us
    pallas_call x1, Pallas kernels: 11.8 us -> 37.6 us  [forecast_step(): pl.pallas_call(stencil_kernel, out_shape=(jax.ShapeDtypeStruct(cells.shap...]
    dot_general x1 -> x0, matrix products: 5.07 us -> none  [forecast_step(): jnp.einsum('sabci,sl->abcil', jnp.stack([north_halo, south_halo]), place,...]
    ppermute x1, starting transfers between devices: 1.92 us -> 4.54 us  [forecast_step(): lax.ppermute(sides[0], 'gy', [(i + 1, i) for i in range(ny - 1)])]
    ppermute x1, starting transfers between devices: 1.92 us -> 3.48 us  [forecast_step(): lax.ppermute(cells[:, :, :, rows - 1:rows, :], 'gx', [(i, i + 1) for i in...]
  transfers between devices with their start and end apart: 4 -> 4, of which waited for: 1 -> 2; matrix products, arithmetic and copies ran while one was open for 8% -> 4% of each run, Pallas kernels for 0% -> 0%
where the time goes in v10:
time: 152 us; the launch traced here: 150 us
  Pallas kernels  114 us (75%)
  starting transfers between devices  16.5 us (11%)
  matrix products  8.5 us (6%)
  local copies, waits for them, and re-layouts  5.67 us (4%)
  waiting for transfers between devices  3 us (2%)
  other arithmetic  2.95 us (2%)
    pallas_call x1, Pallas kernels, run_analysis(): pl.pallas_call(functools.partial(analysis_kernel, nx, ny), out_shape=jax....  66.7 us
    pallas_call x1, Pallas kernels, forecast_step(): pl.pallas_call(stencil_kernel, out_shape=(jax.ShapeDtypeStruct(cells.shap...  37.6 us
    pallas_call x1, Pallas kernels, apply_transform(): pl.pallas_call(transform_kernel, out_shape=jax.ShapeDtypeStruct(cells.sha...  9.24 us
    dot_general x1, matrix products, forecast_step(): jnp.einsum('abcil,sl->sabci', cells, pick, precision=lax.Precision.HIGHES...  8.5 us
    ppermute x1, starting transfers between devices, forecast_step(): lax.ppermute(cells[:, :, :, 0:1, :], 'gx', [(i + 1, i) for i in range(nx...  6.58 us
    ppermute x1, starting transfers between devices, forecast_step(): lax.ppermute(sides[0], 'gy', [(i + 1, i) for i in range(ny - 1)])  4.54 us
    ppermute x1, starting transfers between devices, forecast_step(): lax.ppermute(cells[:, :, :, rows - 1:rows, :], 'gx', [(i, i + 1) for i in...  3.48 us
  transfers between devices with their start and end apart: 4, of which 2 were waited for; matrix products, arithmetic and copies ran while one was open for 4% of the time, Pallas kernels for 0%

profile of v10, /device:TPU:96, one launch (start us, length us, event | category | flops | bytes accessed | tf_op | source)
XLA Modules:
  0.0 150.4 jit_solution(15922732755890458027)
XLA Ops:
  0.0 0.0 copy-start.4
  0.0 0.0 copy-start.2
  0.0 8.5 %fusion = f32[2,64,2,4,16]{1,0,4,3,2:T(2,128)S(1)} fusion(f32[64,2,4,16,128]{4,3,2,1,0:T(8,128)} %x_ref.1, pred[1,128]{1,0:T(4,128)(4,1)S(1)} %get-tuple-element.15, pred[1,128]{1,0:T(4,128)(4,1)S(1)} %get-tuple-element.16), kind=kOutput, calls=%fused_computation | convolution fusion | flops 25166080 | bytes 4260096 | tf_op jit(solution)/shard_map/abcil,sl->sabci/dot_general | solution.py:95
  8.5 0.1 fusion.10
  8.7 1.9 %collective-permute-start.3 = (f32[64,2,4,16]{0,3,2,1:T(8,128)S(1)}, f32[64,2,4,16]{0,3,2,1:T(8,128)S(1)}, u32[]{:S(2)}, u32[]{:S(2)}) collective-permute-start(f32[64,2,4,16]{0,3,2,1:T(8,128)S(1)} %bitcast.43), channel_id=1, source_target_pairs={{0,1},{1,2},{2,3},{3,4},{4,5},{5,6},{6,7},{8,9},{9,10},{10,11},{11... | collective-permute-start | bytes 98312 | tf_op jit(solution)/shard_map/ppermute | solution.py:100
  10.6 4.5 %collective-permute-start.2 = (f32[64,2,4,16]{0,3,2,1:T(8,128)S(1)}, f32[64,2,4,16]{0,3,2,1:T(8,128)S(1)}, u32[]{:S(2)}, u32[]{:S(2)}) collective-permute-start(f32[64,2,4,16]{0,3,2,1:T(8,128)S(1)} %bitcast.44), channel_id=1, source_target_pairs={{1,0},{2,1},{3,2},{4,3},{5,4},{6,5},{7,6},{9,8},{10,9},{11,10},{12... | collective-permute-start | bytes 98312 | tf_op jit(solution)/shard_map/ppermute | solution.py:99
  15.1 2.8 %fusion.9 = (f32[64,2,4,1,128]{4,3,2,1,0:T(1,128)S(1)}, f32[64,2,4,1,128]{4,3,2,1,0:T(1,128)S(1)}) fusion(f32[64,2,4,16,128]{4,3,2,1,0:T(8,128)} %x_ref.1), kind=kLoop, calls=%fused_computation.29 | loop fusion | bytes 1048576 | tf_op jit(solution)/shard_map/slice | solution.py:92
  17.9 3.5 %collective-permute-start.1 = (f32[64,2,4,1,128]{4,3,2,1,0:T(1,128)S(1)}, f32[64,2,4,1,128]{4,3,2,1,0:T(1,128)S(1)}, u32[]{:S(2)}, u32[]{:S(2)}) collective-permute-start(f32[64,2,4,1,128]{4,3,2,1,0:T(1,128)S(1)} %get-tuple-element.9), channel_id=1, source_target_pairs={{0,8},{8,16},{16,24},{24,32},{32,40},{40,48},{48,56},{56,64},{64,7... | collective-permute-start | bytes 786440 | tf_op jit(solution)/shard_map/ppermute | solution.py:92
  21.4 6.6 %collective-permute-start = (f32[64,2,4,1,128]{4,3,2,1,0:T(1,128)S(1)}, f32[64,2,4,1,128]{4,3,2,1,0:T(1,128)S(1)}, u32[]{:S(2)}, u32[]{:S(2)}) collective-permute-start(f32[64,2,4,1,128]{4,3,2,1,0:T(1,128)S(1)} %get-tuple-element.10), channel_id=1, source_target_pairs={{8,0},{16,8},{24,16},{32,24},{40,32},{48,40},{56,48},{64,56},{72,6... | collective-permute-start | bytes 786440 | tf_op jit(solution)/shard_map/ppermute | solution.py:91
  28.0 0.0 copy-done.4
  28.0 0.1 and_convert_fusion
  28.1 0.0 copy-done.3
  28.1 0.8 fusion.2
  28.9 0.0 copy-done.5
  28.9 0.6 compare_select_fusion.scale_ref
  29.6 0.0 copy-done.2
  29.6 0.1 reshape.180
  29.7 0.1 convert_element_type.27
  29.8 0.5 max.4.w_ref
  30.3 0.0 collective-permute-done.2
  30.3 0.2 copy.28
  30.5 0.0 collective-permute-done.3
  30.5 0.2 copy.29
  30.6 0.8 select_maximum_fusion.edge_ref
  31.5 1.6 %collective-permute-done.1.west_ref = f32[64,2,4,1,128]{4,3,2,1,0:T(1,128)S(1)} collective-permute-done((f32[64,2,4,1,128]{4,3,2,1,0:T(1,128)S(1)}, f32[64,2,4,1,128]{4,3,2,1,0:T(1,128)S(1)}, u32[]{:S(2)}, u32[]{:S(2)}) %collective-permute-start.1) | collective-permute-done | bytes 262176 | tf_op jit(solution)/shard_map/ppermute | solution.py:92
  33.1 1.4 collective-permute-done.east_ref
  34.5 0.0 copy-done
  34.5 0.7 copy-done.1
  35.2 37.6 %shard_map.91 = (f32[64,2,4,16,128]{4,3,2,1,0:T(8,128)}, f32[64,512]{1,0:T(8,128)}) custom-call(f32[64,2,4,16,128]{4,3,2,1,0:T(8,128)} %x_ref.1, f32[64,2,4,1,128]{4,3,2,1,0:T(1,128)} %copy-done.1, f32[64,2,4,1,128]{4,3,2,1,0:T(1,128)} %copy-done, f32[2,512,128]{2,1,0:T(8,128)} %select_maximum_fusion.edge_ref, f32[2,16,128]{2,1,0:T(8,128)} %u_ref.1, ...), custom_call_target="tpu_custom_call" | custom-call | tf_op jit(solution)/shard_map/pallas_call | solution.py:114
  72.8 1.6 %bitcast_bitcast_fusion.y_ref = f32[4,64,128]{2,1,0:T(8,128)} fusion(f32[64,512]{1,0:T(8,128)} %get-tuple-element.7), kind=kLoop, calls=%fused_computation.8 | loop fusion | bytes 262144 | tf_op jit(solution)/shard_map/transpose | solution.py:347
  74.4 66.7 %shard_map.92.p_ref = f32[64,64]{1,0:T(8,128)} custom-call(f32[4,64,128]{2,1,0:T(8,128)} %bitcast_bitcast_fusion.y_ref, f32[4,1,128]{2,1,0:T(1,128)} %compare_select_fusion.scale_ref, f32[4,1,128]{2,1,0:T(1,128)} %bitcast.46, f32[25]{0:T(128)} %max.4.w_ref), custom_call_target="tpu_custom_call" | custom-call | tf_op jit(solution)/shard_map/pallas_call | solution.py:276
  141.1 9.2 %shard_map.93 = f32[64,2,4,16,128]{4,3,2,1,0:T(8,128)} custom-call(f32[64,64]{1,0:T(8,128)} %shard_map.92.p_ref, f32[64,2,4,16,128]{4,3,2,1,0:T(8,128)} %get-tuple-element.8.x_ref), custom_call_target="tpu_custom_call" | custom-call | tf_op jit(solution)/shard_map/pallas_call | solution.py:311
  (9 shorter events, 0.0 us)
Async XLA Ops:
  0.0 28.0 %copy-start.4 = (f32[1,1,4,128]{3,2,1,0:T(4,128)S(1)}, f32[1,1,4,128]{3,2,1,0:T(4,128)}, u32[]{:S(2)}) copy-start(f32[1,1,4,128]{3,2,1,0:T(4,128)} %param.16) | copy-start | bytes 6148
  0.0 28.1 %copy-start.3 = (s32[1,1,4,128]{3,2,1,0:T(4,128)S(1)}, s32[1,1,4,128]{3,2,1,0:T(4,128)}, u32[]{:S(2)}) copy-start(s32[1,1,4,128]{3,2,1,0:T(4,128)} %param.13) | copy-start | bytes 6148
  0.0 28.9 %copy-start.5 = (s32[1,1,4]{2,1,0:T(1,128)S(1)}, s32[1,1,4]{2,1,0:T(1,128)}, u32[]{:S(2)}) copy-start(s32[1,1,4]{2,1,0:T(1,128)} %param.14) | copy-start | bytes 52
  0.0 29.6 %copy-start.2 = (s32[1,1,5,5]{3,1,2,0:T(1,128)S(1)}, s32[1,1,5,5]{3,1,2,0:T(1,128)}, u32[]{:S(2)}) copy-start(s32[1,1,5,5]{3,1,2,0:T(1,128)} %param.17) | copy-start | bytes 304
  8.7 21.8 %collective-permute-start.3 = (f32[64,2,4,16]{0,3,2,1:T(8,128)S(1)}, f32[64,2,4,16]{0,3,2,1:T(8,128)S(1)}, u32[]{:S(2)}, u32[]{:S(2)}) collective-permute-start(f32[64,2,4,16]{0,3,2,1:T(8,128)S(1)} %bitcast.43), channel_id=1, source_target_pairs={{0,1},{1,2},{2,3},{3,4},{4,5},{5,6},{6,7},{8,9},{9,10},{10,11},{11... | collective-permute-start | bytes 98312 | tf_op jit(solution)/shard_map/ppermute | solution.py:100
  10.6 19.7 %collective-permute-start.2 = (f32[64,2,4,16]{0,3,2,1:T(8,128)S(1)}, f32[64,2,4,16]{0,3,2,1:T(8,128)S(1)}, u32[]{:S(2)}, u32[]{:S(2)}) collective-permute-start(f32[64,2,4,16]{0,3,2,1:T(8,128)S(1)} %bitcast.44), channel_id=1, source_target_pairs={{1,0},{2,1},{3,2},{4,3},{5,4},{6,5},{7,6},{9,8},{10,9},{11,10},{12... | collective-permute-start | bytes 98312 | tf_op jit(solution)/shard_map/ppermute | solution.py:99
  17.9 15.2 %collective-permute-start.1 = (f32[64,2,4,1,128]{4,3,2,1,0:T(1,128)S(1)}, f32[64,2,4,1,128]{4,3,2,1,0:T(1,128)S(1)}, u32[]{:S(2)}, u32[]{:S(2)}) collective-permute-start(f32[64,2,4,1,128]{4,3,2,1,0:T(1,128)S(1)} %get-tuple-element.9), channel_id=1, source_target_pairs={{0,8},{8,16},{16,24},{24,32},{32,40},{40,48},{48,56},{56,64},{64,7... | collective-permute-start | bytes 786440 | tf_op jit(solution)/shard_map/ppermute | solution.py:92
  21.4 13.1 %collective-permute-start = (f32[64,2,4,1,128]{4,3,2,1,0:T(1,128)S(1)}, f32[64,2,4,1,128]{4,3,2,1,0:T(1,128)S(1)}, u32[]{:S(2)}, u32[]{:S(2)}) collective-permute-start(f32[64,2,4,1,128]{4,3,2,1,0:T(1,128)S(1)} %get-tuple-element.10), channel_id=1, source_target_pairs={{8,0},{16,8},{24,16},{32,24},{40,32},{48,40},{56,48},{64,56},{72,6... | collective-permute-start | bytes 786440 | tf_op jit(solution)/shard_map/ppermute | solution.py:91
  33.1 1.4 copy-start
  34.5 0.7 copy-start.1

commit v11 on v9

--- a/solution.py
+++ b/solution.py
@@ -89,7 +89,7 @@
         "sabci,sl->abcil", jnp.stack([north_halo, south_halo]), place,
         precision=lax.Precision.HIGHEST, preferred_element_type=jnp.float32,
     )
-    block = 8
+    block = 16
     members = cells.shape[0]
     big = pl.BlockSpec((block,) + cells.shape[1:], lambda i: (i, 0, 0, 0, 0))
     thin = pl.BlockSpec((block,) + cells.shape[1:3] + (1, lanes), lambda i: (i, 0, 0, 0, 0))

time: 127 us -> 126 us (level)
  no operation moved by 1% of the time
where the time goes in v11:
time: 126 us
  Pallas kernels  88.6 us (70%)
  matrix products  13.6 us (11%)
  starting transfers between devices  12.9 us (10%)
  local copies, waits for them, and re-layouts  5.78 us (5%)
  waiting for transfers between devices  2.74 us (2%)
  other arithmetic  2.11 us (2%)
    pallas_call x1, Pallas kernels, run_analysis(): pl.pallas_call(functools.partial(analysis_kernel, nx, ny), out_shape=jax....  67.8 us
    pallas_call x1, Pallas kernels, forecast_step(): pl.pallas_call(stencil_kernel, out_shape=(jax.ShapeDtypeStruct(cells.shap...  11.6 us
    pallas_call x1, Pallas kernels, apply_transform(): pl.pallas_call(transform_kernel, out_shape=jax.ShapeDtypeStruct(cells.sha...  9.25 us
    dot_general x1, matrix products, forecast_step(): jnp.einsum('abcil,sl->sabci', cells, pick, precision=lax.Precision.HIGHES...  8.5 us
    ppermute x1, starting transfers between devices, forecast_step(): lax.ppermute(cells[:, :, :, 0:1, :], 'gx', [(i + 1, i) for i in range(nx...  6.66 us
    dot_general x1, matrix products, forecast_step(): jnp.einsum('sabci,sl->abcil', jnp.stack([north_halo, south_halo]), place,...  5.07 us
    slice x1, local copies, waits for them, and re-layouts, forecast_step(): cells[:, :, :, rows - 1:rows, :]  2.79 us
    ppermute x1, waiting for transfers between devices, forecast_step(): lax.ppermute(cells[:, :, :, rows - 1:rows, :], 'gx', [(i, i + 1) for i in...  2.73 us
  transfers between devices with their start and end apart: 4, of which 1 were waited for; matrix products, arithmetic and copies ran while one was open for 8% of the time, Pallas kernels for 0%

profile of v11, /device:TPU:96, one launch (start us, length us, event | category | flops | bytes accessed | tf_op | source)
XLA Modules:
  0.0 125.9 jit_solution(18223294430806766100)
XLA Ops:
  0.0 0.0 copy-start.3
  0.0 0.0 copy-start.4
  0.0 0.0 copy-start.2
  0.0 8.5 %fusion = f32[2,64,2,4,16]{1,0,4,3,2:T(2,128)S(1)} fusion(f32[64,2,4,16,128]{4,3,2,1,0:T(8,128)} %x_ref.1, pred[1,128]{1,0:T(4,128)(4,1)S(1)} %get-tuple-element.15, pred[1,128]{1,0:T(4,128)(4,1)S(1)} %get-tuple-element.16), kind=kOutput, calls=%fused_computation | convolution fusion | flops 25166080 | bytes 4260096 | tf_op jit(solution)/shard_map/abcil,sl->sabci/dot_general | solution.py:82
  8.5 0.1 fusion.14
  8.7 1.9 %collective-permute-start.2 = (f32[64,2,4,16]{0,3,2,1:T(8,128)S(1)}, f32[64,2,4,16]{0,3,2,1:T(8,128)S(1)}, u32[]{:S(2)}, u32[]{:S(2)}) collective-permute-start(f32[64,2,4,16]{0,3,2,1:T(8,128)S(1)} %bitcast.51), channel_id=1, source_target_pairs={{1,0},{2,1},{3,2},{4,3},{5,4},{6,5},{7,6},{9,8},{10,9},{11,10},{12... | collective-permute-start | bytes 98312 | tf_op jit(solution)/shard_map/ppermute | solution.py:86
  10.6 2.4 %collective-permute-start.3 = (f32[64,2,4,16]{0,3,2,1:T(8,128)S(1)}, f32[64,2,4,16]{0,3,2,1:T(8,128)S(1)}, u32[]{:S(2)}, u32[]{:S(2)}) collective-permute-start(f32[64,2,4,16]{0,3,2,1:T(8,128)S(1)} %bitcast.49), channel_id=1, source_target_pairs={{0,1},{1,2},{2,3},{3,4},{4,5},{5,6},{6,7},{8,9},{9,10},{10,11},{11... | collective-permute-start | bytes 98312 | tf_op jit(solution)/shard_map/ppermute | solution.py:87
  13.0 2.8 %fusion.13 = (f32[64,2,4,1,128]{4,3,2,1,0:T(1,128)S(1)}, f32[64,2,4,1,128]{4,3,2,1,0:T(1,128)S(1)}) fusion(f32[64,2,4,16,128]{4,3,2,1,0:T(8,128)} %x_ref.1), kind=kLoop, calls=%fused_computation.33 | loop fusion | bytes 1048576 | tf_op jit(solution)/shard_map/slice | solution.py:78
  15.8 6.7 %collective-permute-start = (f32[64,2,4,1,128]{4,3,2,1,0:T(1,128)S(1)}, f32[64,2,4,1,128]{4,3,2,1,0:T(1,128)S(1)}, u32[]{:S(2)}, u32[]{:S(2)}) collective-permute-start(f32[64,2,4,1,128]{4,3,2,1,0:T(1,128)S(1)} %get-tuple-element.10), channel_id=1, source_target_pairs={{8,0},{16,8},{24,16},{32,24},{40,32},{48,40},{56,48},{64,56},{72,6... | collective-permute-start | bytes 786440 | tf_op jit(solution)/shard_map/ppermute | solution.py:77
  22.5 1.9 %collective-permute-start.1 = (f32[64,2,4,1,128]{4,3,2,1,0:T(1,128)S(1)}, f32[64,2,4,1,128]{4,3,2,1,0:T(1,128)S(1)}, u32[]{:S(2)}, u32[]{:S(2)}) collective-permute-start(f32[64,2,4,1,128]{4,3,2,1,0:T(1,128)S(1)} %get-tuple-element.9), channel_id=1, source_target_pairs={{0,8},{8,16},{16,24},{24,32},{32,40},{40,48},{48,56},{56,64},{64,7... | collective-permute-start | bytes 786440 | tf_op jit(solution)/shard_map/ppermute | solution.py:78
  24.4 0.0 copy-done.3
  24.4 0.1 and_convert_fusion
  24.5 0.0 copy-done.4
  24.5 0.8 fusion.2
  25.3 0.0 copy-done.5
  25.3 0.6 compare_select_fusion.scale_ref
  26.0 0.0 copy-done.2
  26.0 0.1 reshape.175
  26.1 0.1 convert_element_type.26
  26.1 0.5 max.4.w_ref
  26.7 0.0 collective-permute-done.2
  26.7 0.0 collective-permute-done.3
  26.7 0.4 copy.15
  27.1 5.1 %fusion.8.edge_ref = f32[64,2,4,16,128]{4,3,2,1,0:T(8,128)} fusion(f32[2,64,2,4,16]{4,0,3,2,1:T(2,128)S(1)} %copy.15, pred[1,128]{1,0:T(4,128)(4,1)S(1)} %get-tuple-element.16, pred[1,128]{1,0:T(4,128)(4,1)S(1)} %get-tuple-element.15), kind=kOutput, calls=%fused_computation.24 | convolution fusion | flops 25166080 | bytes 4260096 | tf_op jit(solution)/shard_map/sabci,sl->abcil/dot_general | solution.py:88
  32.2 0.0 collective-permute-done.east_ref
  32.2 2.7 %collective-permute-done.1.west_ref = f32[64,2,4,1,128]{4,3,2,1,0:T(1,128)S(1)} collective-permute-done((f32[64,2,4,1,128]{4,3,2,1,0:T(1,128)S(1)}, f32[64,2,4,1,128]{4,3,2,1,0:T(1,128)S(1)}, u32[]{:S(2)}, u32[]{:S(2)}) %collective-permute-start.1) | collective-permute-done | bytes 262176 | tf_op jit(solution)/shard_map/ppermute | solution.py:78
  35.0 0.0 copy-done
  35.0 0.7 copy-done.1
  35.7 11.6 %shard_map.91 = (f32[64,2,4,16,128]{4,3,2,1,0:T(8,128)}, f32[64,512]{1,0:T(8,128)}) custom-call(f32[64,2,4,16,128]{4,3,2,1,0:T(8,128)} %x_ref.1, f32[64,2,4,1,128]{4,3,2,1,0:T(1,128)} %copy-done, f32[64,2,4,1,128]{4,3,2,1,0:T(1,128)} %copy-done.1, f32[64,2,4,16,128]{4,3,2,1,0:T(8,128)} %fusion.8.edge_ref, f32[2,16,128]{2,1,0:T(8,128)} %u_ref.1, ...), custom_call_target="tpu_custom_call" | custom-call | tf_op jit(solution)/shard_map/pallas_call | solution.py:103
  47.2 1.6 %bitcast_bitcast_fusion.y_ref = f32[4,64,128]{2,1,0:T(8,128)} fusion(f32[64,512]{1,0:T(8,128)} %get-tuple-element.7), kind=kLoop, calls=%fused_computation.6 | loop fusion | bytes 262144 | tf_op jit(solution)/shard_map/transpose | solution.py:336
  48.8 67.8 %shard_map.92.p_ref = f32[64,64]{1,0:T(8,128)} custom-call(f32[4,64,128]{2,1,0:T(8,128)} %bitcast_bitcast_fusion.y_ref, f32[4,1,128]{2,1,0:T(1,128)} %compare_select_fusion.scale_ref, f32[4,1,128]{2,1,0:T(1,128)} %bitcast.54, f32[25]{0:T(128)} %max.4.w_ref), custom_call_target="tpu_custom_call" | custom-call | tf_op jit(solution)/shard_map/pallas_call | solution.py:265
  116.6 9.2 %shard_map.93 = f32[64,2,4,16,128]{4,3,2,1,0:T(8,128)} custom-call(f32[64,64]{1,0:T(8,128)} %shard_map.92.p_ref, f32[64,2,4,16,128]{4,3,2,1,0:T(8,128)} %get-tuple-element.8.x_ref), custom_call_target="tpu_custom_call" | custom-call | tf_op jit(solution)/shard_map/pallas_call | solution.py:300
  (9 shorter events, 0.1 us)
Async XLA Ops:
  0.0 24.4 %copy-start.3 = (s32[1,1,4,128]{3,2,1,0:T(4,128)S(1)}, s32[1,1,4,128]{3,2,1,0:T(4,128)}, u32[]{:S(2)}) copy-start(s32[1,1,4,128]{3,2,1,0:T(4,128)} %param.13) | copy-start | bytes 6148
  0.0 24.5 %copy-start.4 = (f32[1,1,4,128]{3,2,1,0:T(4,128)S(1)}, f32[1,1,4,128]{3,2,1,0:T(4,128)}, u32[]{:S(2)}) copy-start(f32[1,1,4,128]{3,2,1,0:T(4,128)} %param.16) | copy-start | bytes 6148
  0.0 25.3 %copy-start.5 = (s32[1,1,4]{2,1,0:T(1,128)S(1)}, s32[1,1,4]{2,1,0:T(1,128)}, u32[]{:S(2)}) copy-start(s32[1,1,4]{2,1,0:T(1,128)} %param.14) | copy-start | bytes 52
  0.0 26.0 %copy-start.2 = (s32[1,1,5,5]{3,1,2,0:T(1,128)S(1)}, s32[1,1,5,5]{3,1,2,0:T(1,128)}, u32[]{:S(2)}) copy-start(s32[1,1,5,5]{3,1,2,0:T(1,128)} %param.17) | copy-start | bytes 304
  8.7 18.0 %collective-permute-start.2 = (f32[64,2,4,16]{0,3,2,1:T(8,128)S(1)}, f32[64,2,4,16]{0,3,2,1:T(8,128)S(1)}, u32[]{:S(2)}, u32[]{:S(2)}) collective-permute-start(f32[64,2,4,16]{0,3,2,1:T(8,128)S(1)} %bitcast.51), channel_id=1, source_target_pairs={{1,0},{2,1},{3,2},{4,3},{5,4},{6,5},{7,6},{9,8},{10,9},{11,10},{12... | collective-permute-start | bytes 98312 | tf_op jit(solution)/shard_map/ppermute | solution.py:86
  10.6 16.1 %collective-permute-start.3 = (f32[64,2,4,16]{0,3,2,1:T(8,128)S(1)}, f32[64,2,4,16]{0,3,2,1:T(8,128)S(1)}, u32[]{:S(2)}, u32[]{:S(2)}) collective-permute-start(f32[64,2,4,16]{0,3,2,1:T(8,128)S(1)} %bitcast.49), channel_id=1, source_target_pairs={{0,1},{1,2},{2,3},{3,4},{4,5},{5,6},{6,7},{8,9},{9,10},{10,11},{11... | collective-permute-start | bytes 98312 | tf_op jit(solution)/shard_map/ppermute | solution.py:87
  15.8 16.4 %collective-permute-start = (f32[64,2,4,1,128]{4,3,2,1,0:T(1,128)S(1)}, f32[64,2,4,1,128]{4,3,2,1,0:T(1,128)S(1)}, u32[]{:S(2)}, u32[]{:S(2)}) collective-permute-start(f32[64,2,4,1,128]{4,3,2,1,0:T(1,128)S(1)} %get-tuple-element.10), channel_id=1, source_target_pairs={{8,0},{16,8},{24,16},{32,24},{40,32},{48,40},{56,48},{64,56},{72,6... | collective-permute-start | bytes 786440 | tf_op jit(solution)/shard_map/ppermute | solution.py:77
  22.5 12.5 %collective-permute-start.1 = (f32[64,2,4,1,128]{4,3,2,1,0:T(1,128)S(1)}, f32[64,2,4,1,128]{4,3,2,1,0:T(1,128)S(1)}, u32[]{:S(2)}, u32[]{:S(2)}) collective-permute-start(f32[64,2,4,1,128]{4,3,2,1,0:T(1,128)S(1)} %get-tuple-element.9), channel_id=1, source_target_pairs={{0,8},{8,16},{16,24},{24,32},{32,40},{40,48},{48,56},{56,64},{64,7... | collective-permute-start | bytes 786440 | tf_op jit(solution)/shard_map/ppermute | solution.py:78
  32.2 2.7 %copy-start = (f32[64,2,4,1,128]{4,3,2,1,0:T(1,128)}, f32[64,2,4,1,128]{4,3,2,1,0:T(1,128)S(1)}, u32[]{:S(2)}) copy-start(f32[64,2,4,1,128]{4,3,2,1,0:T(1,128)S(1)} %collective-permute-done.east_ref) | copy-start | bytes 786436
  34.9 0.7 copy-start.1

commit v12 on v9

--- a/solution.py
+++ b/solution.py
@@ -291,7 +291,7 @@
     mix = p_ref[...]
     for i in range(rows):
         o_ref[:, 0, 0, i, :] = jnp.dot(mix, x_ref[:, 0, 0, i, :],
-                                       precision=lax.Precision.HIGH, preferred_element_type=jnp.float32)
+                                       precision=lax.Precision.HIGHEST, preferred_element_type=jnp.float32)
 
 
 def apply_transform(carried, cells):

time: 127 us -> 128 us (level)
  no operation moved by 1% of the time
where the time goes in v12:
time: 128 us; the launch traced here: 127 us
  Pallas kernels  89.7 us (70%)
  matrix products  13.6 us (11%)
  starting transfers between devices  12.9 us (10%)
  local copies, waits for them, and re-layouts  5.78 us (5%)
  waiting for transfers between devices  2.74 us (2%)
  other arithmetic  2.11 us (2%)
    pallas_call x1, Pallas kernels, run_analysis(): pl.pallas_call(functools.partial(analysis_kernel, nx, ny), out_shape=jax....  67.9 us
    pallas_call x1, Pallas kernels, forecast_step(): pl.pallas_call(stencil_kernel, out_shape=(jax.ShapeDtypeStruct(cells.shap...  11.8 us
    pallas_call x1, Pallas kernels, apply_transform(): pl.pallas_call(transform_kernel, out_shape=jax.ShapeDtypeStruct(cells.sha...  10.1 us
    dot_general x1, matrix products, forecast_step(): jnp.einsum('abcil,sl->sabci', cells, pick, precision=lax.Precision.HIGHES...  8.5 us
    ppermute x1, starting transfers between devices, forecast_step(): lax.ppermute(cells[:, :, :, 0:1, :], 'gx', [(i + 1, i) for i in range(nx...  6.66 us
    dot_general x1, matrix products, forecast_step(): jnp.einsum('sabci,sl->abcil', jnp.stack([north_halo, south_halo]), place,...  5.07 us
    slice x1, local copies, waits for them, and re-layouts, forecast_step(): cells[:, :, :, rows - 1:rows, :]  2.79 us
    ppermute x1, waiting for transfers between devices, forecast_step(): lax.ppermute(cells[:, :, :, rows - 1:rows, :], 'gx', [(i, i + 1) for i in...  2.73 us
  transfers between devices with their start and end apart: 4, of which 1 were waited for; matrix products, arithmetic and copies ran while one was open for 8% of the time, Pallas kernels for 0%

profile of v12, /device:TPU:96, one launch (start us, length us, event | category | flops | bytes accessed | tf_op | source)
XLA Modules:
  0.0 127.0 jit_solution(11742920823615008267)
XLA Ops:
  0.0 0.0 copy-start.3
  0.0 0.0 copy-start.4
  0.0 0.0 copy-start.2
  0.0 8.5 %fusion = f32[2,64,2,4,16]{1,0,4,3,2:T(2,128)S(1)} fusion(f32[64,2,4,16,128]{4,3,2,1,0:T(8,128)} %x_ref.1, pred[1,128]{1,0:T(4,128)(4,1)S(1)} %get-tuple-element.15, pred[1,128]{1,0:T(4,128)(4,1)S(1)} %get-tuple-element.16), kind=kOutput, calls=%fused_computation | convolution fusion | flops 25166080 | bytes 4260096 | tf_op jit(solution)/shard_map/abcil,sl->sabci/dot_general | solution.py:82
  8.5 0.1 fusion.14
  8.7 1.9 %collective-permute-start.2 = (f32[64,2,4,16]{0,3,2,1:T(8,128)S(1)}, f32[64,2,4,16]{0,3,2,1:T(8,128)S(1)}, u32[]{:S(2)}, u32[]{:S(2)}) collective-permute-start(f32[64,2,4,16]{0,3,2,1:T(8,128)S(1)} %bitcast.51), channel_id=1, source_target_pairs={{1,0},{2,1},{3,2},{4,3},{5,4},{6,5},{7,6},{9,8},{10,9},{11,10},{12... | collective-permute-start | bytes 98312 | tf_op jit(solution)/shard_map/ppermute | solution.py:86
  10.6 2.4 %collective-permute-start.3 = (f32[64,2,4,16]{0,3,2,1:T(8,128)S(1)}, f32[64,2,4,16]{0,3,2,1:T(8,128)S(1)}, u32[]{:S(2)}, u32[]{:S(2)}) collective-permute-start(f32[64,2,4,16]{0,3,2,1:T(8,128)S(1)} %bitcast.49), channel_id=1, source_target_pairs={{0,1},{1,2},{2,3},{3,4},{4,5},{5,6},{6,7},{8,9},{9,10},{10,11},{11... | collective-permute-start | bytes 98312 | tf_op jit(solution)/shard_map/ppermute | solution.py:87
  13.0 2.8 %fusion.13 = (f32[64,2,4,1,128]{4,3,2,1,0:T(1,128)S(1)}, f32[64,2,4,1,128]{4,3,2,1,0:T(1,128)S(1)}) fusion(f32[64,2,4,16,128]{4,3,2,1,0:T(8,128)} %x_ref.1), kind=kLoop, calls=%fused_computation.33 | loop fusion | bytes 1048576 | tf_op jit(solution)/shard_map/slice | solution.py:78
  15.8 6.7 %collective-permute-start = (f32[64,2,4,1,128]{4,3,2,1,0:T(1,128)S(1)}, f32[64,2,4,1,128]{4,3,2,1,0:T(1,128)S(1)}, u32[]{:S(2)}, u32[]{:S(2)}) collective-permute-start(f32[64,2,4,1,128]{4,3,2,1,0:T(1,128)S(1)} %get-tuple-element.10), channel_id=1, source_target_pairs={{8,0},{16,8},{24,16},{32,24},{40,32},{48,40},{56,48},{64,56},{72,6... | collective-permute-start | bytes 786440 | tf_op jit(solution)/shard_map/ppermute | solution.py:77
  22.5 1.9 %collective-permute-start.1 = (f32[64,2,4,1,128]{4,3,2,1,0:T(1,128)S(1)}, f32[64,2,4,1,128]{4,3,2,1,0:T(1,128)S(1)}, u32[]{:S(2)}, u32[]{:S(2)}) collective-permute-start(f32[64,2,4,1,128]{4,3,2,1,0:T(1,128)S(1)} %get-tuple-element.9), channel_id=1, source_target_pairs={{0,8},{8,16},{16,24},{24,32},{32,40},{40,48},{48,56},{56,64},{64,7... | collective-permute-start | bytes 786440 | tf_op jit(solution)/shard_map/ppermute | solution.py:78
  24.4 0.0 copy-done.3
  24.4 0.1 and_convert_fusion
  24.5 0.0 copy-done.4
  24.5 0.8 fusion.2
  25.3 0.0 copy-done.5
  25.3 0.6 compare_select_fusion.scale_ref
  26.0 0.0 copy-done.2
  26.0 0.1 reshape.175
  26.1 0.1 convert_element_type.26
  26.1 0.5 max.4.w_ref
  26.7 0.0 collective-permute-done.2
  26.7 0.0 collective-permute-done.3
  26.7 0.4 copy.15
  27.1 5.1 %fusion.8.edge_ref = f32[64,2,4,16,128]{4,3,2,1,0:T(8,128)} fusion(f32[2,64,2,4,16]{4,0,3,2,1:T(2,128)S(1)} %copy.15, pred[1,128]{1,0:T(4,128)(4,1)S(1)} %get-tuple-element.16, pred[1,128]{1,0:T(4,128)(4,1)S(1)} %get-tuple-element.15), kind=kOutput, calls=%fused_computation.24 | convolution fusion | flops 25166080 | bytes 4260096 | tf_op jit(solution)/shard_map/sabci,sl->abcil/dot_general | solution.py:88
  32.2 0.0 collective-permute-done.east_ref
  32.2 2.7 %collective-permute-done.1.west_ref = f32[64,2,4,1,128]{4,3,2,1,0:T(1,128)S(1)} collective-permute-done((f32[64,2,4,1,128]{4,3,2,1,0:T(1,128)S(1)}, f32[64,2,4,1,128]{4,3,2,1,0:T(1,128)S(1)}, u32[]{:S(2)}, u32[]{:S(2)}) %collective-permute-start.1) | collective-permute-done | bytes 262176 | tf_op jit(solution)/shard_map/ppermute | solution.py:78
  35.0 0.0 copy-done
  35.0 0.7 copy-done.1
  35.7 11.8 %shard_map.91 = (f32[64,2,4,16,128]{4,3,2,1,0:T(8,128)}, f32[64,512]{1,0:T(8,128)}) custom-call(f32[64,2,4,16,128]{4,3,2,1,0:T(8,128)} %x_ref.1, f32[64,2,4,1,128]{4,3,2,1,0:T(1,128)} %copy-done, f32[64,2,4,1,128]{4,3,2,1,0:T(1,128)} %copy-done.1, f32[64,2,4,16,128]{4,3,2,1,0:T(8,128)} %fusion.8.edge_ref, f32[2,16,128]{2,1,0:T(8,128)} %u_ref.1, ...), custom_call_target="tpu_custom_call" | custom-call | tf_op jit(solution)/shard_map/pallas_call | solution.py:103
  47.4 1.6 %bitcast_bitcast_fusion.y_ref = f32[4,64,128]{2,1,0:T(8,128)} fusion(f32[64,512]{1,0:T(8,128)} %get-tuple-element.7), kind=kLoop, calls=%fused_computation.6 | loop fusion | bytes 262144 | tf_op jit(solution)/shard_map/transpose | solution.py:336
  49.0 67.9 %shard_map.92.p_ref = f32[64,64]{1,0:T(8,128)} custom-call(f32[4,64,128]{2,1,0:T(8,128)} %bitcast_bitcast_fusion.y_ref, f32[4,1,128]{2,1,0:T(1,128)} %compare_select_fusion.scale_ref, f32[4,1,128]{2,1,0:T(1,128)} %bitcast.54, f32[25]{0:T(128)} %max.4.w_ref), custom_call_target="tpu_custom_call" | custom-call | tf_op jit(solution)/shard_map/pallas_call | solution.py:265
  116.9 10.1 %shard_map.93 = f32[64,2,4,16,128]{4,3,2,1,0:T(8,128)} custom-call(f32[64,64]{1,0:T(8,128)} %shard_map.92.p_ref, f32[64,2,4,16,128]{4,3,2,1,0:T(8,128)} %get-tuple-element.8.x_ref), custom_call_target="tpu_custom_call" | custom-call | tf_op jit(solution)/shard_map/pallas_call | solution.py:300
  (9 shorter events, 0.1 us)
Async XLA Ops:
  0.0 24.4 %copy-start.3 = (s32[1,1,4,128]{3,2,1,0:T(4,128)S(1)}, s32[1,1,4,128]{3,2,1,0:T(4,128)}, u32[]{:S(2)}) copy-start(s32[1,1,4,128]{3,2,1,0:T(4,128)} %param.13) | copy-start | bytes 6148
  0.0 24.5 %copy-start.4 = (f32[1,1,4,128]{3,2,1,0:T(4,128)S(1)}, f32[1,1,4,128]{3,2,1,0:T(4,128)}, u32[]{:S(2)}) copy-start(f32[1,1,4,128]{3,2,1,0:T(4,128)} %param.16) | copy-start | bytes 6148
  0.0 25.3 %copy-start.5 = (s32[1,1,4]{2,1,0:T(1,128)S(1)}, s32[1,1,4]{2,1,0:T(1,128)}, u32[]{:S(2)}) copy-start(s32[1,1,4]{2,1,0:T(1,128)} %param.14) | copy-start | bytes 52
  0.0 26.0 %copy-start.2 = (s32[1,1,5,5]{3,1,2,0:T(1,128)S(1)}, s32[1,1,5,5]{3,1,2,0:T(1,128)}, u32[]{:S(2)}) copy-start(s32[1,1,5,5]{3,1,2,0:T(1,128)} %param.17) | copy-start | bytes 304
  8.7 18.0 %collective-permute-start.2 = (f32[64,2,4,16]{0,3,2,1:T(8,128)S(1)}, f32[64,2,4,16]{0,3,2,1:T(8,128)S(1)}, u32[]{:S(2)}, u32[]{:S(2)}) collective-permute-start(f32[64,2,4,16]{0,3,2,1:T(8,128)S(1)} %bitcast.51), channel_id=1, source_target_pairs={{1,0},{2,1},{3,2},{4,3},{5,4},{6,5},{7,6},{9,8},{10,9},{11,10},{12... | collective-permute-start | bytes 98312 | tf_op jit(solution)/shard_map/ppermute | solution.py:86
  10.6 16.1 %collective-permute-start.3 = (f32[64,2,4,16]{0,3,2,1:T(8,128)S(1)}, f32[64,2,4,16]{0,3,2,1:T(8,128)S(1)}, u32[]{:S(2)}, u32[]{:S(2)}) collective-permute-start(f32[64,2,4,16]{0,3,2,1:T(8,128)S(1)} %bitcast.49), channel_id=1, source_target_pairs={{0,1},{1,2},{2,3},{3,4},{4,5},{5,6},{6,7},{8,9},{9,10},{10,11},{11... | collective-permute-start | bytes 98312 | tf_op jit(solution)/shard_map/ppermute | solution.py:87
  15.8 16.4 %collective-permute-start = (f32[64,2,4,1,128]{4,3,2,1,0:T(1,128)S(1)}, f32[64,2,4,1,128]{4,3,2,1,0:T(1,128)S(1)}, u32[]{:S(2)}, u32[]{:S(2)}) collective-permute-start(f32[64,2,4,1,128]{4,3,2,1,0:T(1,128)S(1)} %get-tuple-element.10), channel_id=1, source_target_pairs={{8,0},{16,8},{24,16},{32,24},{40,32},{48,40},{56,48},{64,56},{72,6... | collective-permute-start | bytes 786440 | tf_op jit(solution)/shard_map/ppermute | solution.py:77
  22.5 12.5 %collective-permute-start.1 = (f32[64,2,4,1,128]{4,3,2,1,0:T(1,128)S(1)}, f32[64,2,4,1,128]{4,3,2,1,0:T(1,128)S(1)}, u32[]{:S(2)}, u32[]{:S(2)}) collective-permute-start(f32[64,2,4,1,128]{4,3,2,1,0:T(1,128)S(1)} %get-tuple-element.9), channel_id=1, source_target_pairs={{0,8},{8,16},{16,24},{24,32},{32,40},{40,48},{48,56},{56,64},{64,7... | collective-permute-start | bytes 786440 | tf_op jit(solution)/shard_map/ppermute | solution.py:78
  32.2 2.7 %copy-start = (f32[64,2,4,1,128]{4,3,2,1,0:T(1,128)}, f32[64,2,4,1,128]{4,3,2,1,0:T(1,128)S(1)}, u32[]{:S(2)}) copy-start(f32[64,2,4,1,128]{4,3,2,1,0:T(1,128)S(1)} %collective-permute-done.east_ref) | copy-start | bytes 786436
  34.9 0.7 copy-start.1

commit v13 on v9

--- a/solution.py
+++ b/solution.py
@@ -192,7 +192,7 @@
         payload[par, half : half + 8, :] = tail
 
         copies = []
-        for k, (dx, dy) in enumerate(OFFSETS):
+        for k, (dx, dy) in sorted(enumerate(OFFSETS), key=lambda item: -abs(item[1][0]) - abs(item[1][1])):
             if dx == 0 and dy == 0:
                 continue
             copy = pltpu.make_async_remote_copy(
@@ -215,17 +215,18 @@
         for k, (dx, dy) in enumerate(OFFSETS):
             if dx == 0 and dy == 0:
                 total[...] += w_ref[k] * payload[par]
+        for k, dx, dy, copy, ok in sorted(copies, key=lambda item: item[0]):
+            arrives = inside(me_x + dx, me_y + dy)
+
+            @pl.when(arrives)
+            def _():
+                copy.wait_recv()
+                total[...] += w_ref[k] * slots[par, k]
+
         for k, dx, dy, copy, ok in copies:
             @pl.when(ok)
             def _():
                 copy.wait_send()
-
-            arrives = inside(me_x + dx, me_y + dy)
-
-            @pl.when(arrives)
-            def _():
-                copy.wait_recv()
-                total[...] += w_ref[k] * slots[par, k]
 
         summed = total[...]
         packed = summed[0:half, :]

time: 127 us -> 129 us (1.016)
  Pallas kernels: 88.9 us -> 90.9 us
    pallas_call x1, Pallas kernels: 67.9 us -> 69.9 us  [run_analysis(): pl.pallas_call(functools.partial(analysis_kernel, nx, ny), out_shape=jax....]
where the time goes in v13:
time: 129 us; the launch traced here: 128 us
  Pallas kernels  90.9 us (70%)
  matrix products  13.6 us (11%)
  starting transfers between devices  12.9 us (10%)
  local copies, waits for them, and re-layouts  5.78 us (4%)
  waiting for transfers between devices  2.74 us (2%)
  other arithmetic  2.11 us (2%)
    pallas_call x1, Pallas kernels, run_analysis(): pl.pallas_call(functools.partial(analysis_kernel, nx, ny), out_shape=jax....  69.9 us
    pallas_call x1, Pallas kernels, forecast_step(): pl.pallas_call(stencil_kernel, out_shape=(jax.ShapeDtypeStruct(cells.shap...  11.8 us
    pallas_call x1, Pallas kernels, apply_transform(): pl.pallas_call(transform_kernel, out_shape=jax.ShapeDtypeStruct(cells.sha...  9.25 us
    dot_general x1, matrix products, forecast_step(): jnp.einsum('abcil,sl->sabci', cells, pick, precision=lax.Precision.HIGHES...  8.5 us
    ppermute x1, starting transfers between devices, forecast_step(): lax.ppermute(cells[:, :, :, 0:1, :], 'gx', [(i + 1, i) for i in range(nx...  6.66 us
    dot_general x1, matrix products, forecast_step(): jnp.einsum('sabci,sl->abcil', jnp.stack([north_halo, south_halo]), place,...  5.07 us
    slice x1, local copies, waits for them, and re-layouts, forecast_step(): cells[:, :, :, rows - 1:rows, :]  2.79 us
    ppermute x1, waiting for transfers between devices, forecast_step(): lax.ppermute(cells[:, :, :, rows - 1:rows, :], 'gx', [(i, i + 1) for i in...  2.73 us
  transfers between devices with their start and end apart: 4, of which 1 were waited for; matrix products, arithmetic and copies ran while one was open for 8% of the time, Pallas kernels for 0%

profile of v13, /device:TPU:96, one launch (start us, length us, event | category | flops | bytes accessed | tf_op | source)
XLA Modules:
  0.0 128.1 jit_solution(1917644174867502964)
XLA Ops:
  0.0 0.0 copy-start.3
  0.0 0.0 copy-start.4
  0.0 0.0 copy-start.2
  0.0 8.5 %fusion = f32[2,64,2,4,16]{1,0,4,3,2:T(2,128)S(1)} fusion(f32[64,2,4,16,128]{4,3,2,1,0:T(8,128)} %x_ref.1, pred[1,128]{1,0:T(4,128)(4,1)S(1)} %get-tuple-element.15, pred[1,128]{1,0:T(4,128)(4,1)S(1)} %get-tuple-element.16), kind=kOutput, calls=%fused_computation | convolution fusion | flops 25166080 | bytes 4260096 | tf_op jit(solution)/shard_map/abcil,sl->sabci/dot_general | solution.py:82
  8.5 0.1 fusion.14
  8.7 1.9 %collective-permute-start.2 = (f32[64,2,4,16]{0,3,2,1:T(8,128)S(1)}, f32[64,2,4,16]{0,3,2,1:T(8,128)S(1)}, u32[]{:S(2)}, u32[]{:S(2)}) collective-permute-start(f32[64,2,4,16]{0,3,2,1:T(8,128)S(1)} %bitcast.51), channel_id=1, source_target_pairs={{1,0},{2,1},{3,2},{4,3},{5,4},{6,5},{7,6},{9,8},{10,9},{11,10},{12... | collective-permute-start | bytes 98312 | tf_op jit(solution)/shard_map/ppermute | solution.py:86
  10.6 2.4 %collective-permute-start.3 = (f32[64,2,4,16]{0,3,2,1:T(8,128)S(1)}, f32[64,2,4,16]{0,3,2,1:T(8,128)S(1)}, u32[]{:S(2)}, u32[]{:S(2)}) collective-permute-start(f32[64,2,4,16]{0,3,2,1:T(8,128)S(1)} %bitcast.49), channel_id=1, source_target_pairs={{0,1},{1,2},{2,3},{3,4},{4,5},{5,6},{6,7},{8,9},{9,10},{10,11},{11... | collective-permute-start | bytes 98312 | tf_op jit(solution)/shard_map/ppermute | solution.py:87
  13.0 2.8 %fusion.13 = (f32[64,2,4,1,128]{4,3,2,1,0:T(1,128)S(1)}, f32[64,2,4,1,128]{4,3,2,1,0:T(1,128)S(1)}) fusion(f32[64,2,4,16,128]{4,3,2,1,0:T(8,128)} %x_ref.1), kind=kLoop, calls=%fused_computation.33 | loop fusion | bytes 1048576 | tf_op jit(solution)/shard_map/slice | solution.py:78
  15.8 6.7 %collective-permute-start = (f32[64,2,4,1,128]{4,3,2,1,0:T(1,128)S(1)}, f32[64,2,4,1,128]{4,3,2,1,0:T(1,128)S(1)}, u32[]{:S(2)}, u32[]{:S(2)}) collective-permute-start(f32[64,2,4,1,128]{4,3,2,1,0:T(1,128)S(1)} %get-tuple-element.10), channel_id=1, source_target_pairs={{8,0},{16,8},{24,16},{32,24},{40,32},{48,40},{56,48},{64,56},{72,6... | collective-permute-start | bytes 786440 | tf_op jit(solution)/shard_map/ppermute | solution.py:77
  22.5 1.9 %collective-permute-start.1 = (f32[64,2,4,1,128]{4,3,2,1,0:T(1,128)S(1)}, f32[64,2,4,1,128]{4,3,2,1,0:T(1,128)S(1)}, u32[]{:S(2)}, u32[]{:S(2)}) collective-permute-start(f32[64,2,4,1,128]{4,3,2,1,0:T(1,128)S(1)} %get-tuple-element.9), channel_id=1, source_target_pairs={{0,8},{8,16},{16,24},{24,32},{32,40},{40,48},{48,56},{56,64},{64,7... | collective-permute-start | bytes 786440 | tf_op jit(solution)/shard_map/ppermute | solution.py:78
  24.4 0.0 copy-done.3
  24.4 0.1 and_convert_fusion
  24.5 0.0 copy-done.4
  24.5 0.8 fusion.2
  25.3 0.0 copy-done.5
  25.3 0.6 compare_select_fusion.scale_ref
  26.0 0.0 copy-done.2
  26.0 0.1 reshape.175
  26.1 0.1 convert_element_type.26
  26.1 0.5 max.4.w_ref
  26.7 0.0 collective-permute-done.2
  26.7 0.0 collective-permute-done.3
  26.7 0.4 copy.15
  27.1 5.1 %fusion.8.edge_ref = f32[64,2,4,16,128]{4,3,2,1,0:T(8,128)} fusion(f32[2,64,2,4,16]{4,0,3,2,1:T(2,128)S(1)} %copy.15, pred[1,128]{1,0:T(4,128)(4,1)S(1)} %get-tuple-element.16, pred[1,128]{1,0:T(4,128)(4,1)S(1)} %get-tuple-element.15), kind=kOutput, calls=%fused_computation.24 | convolution fusion | flops 25166080 | bytes 4260096 | tf_op jit(solution)/shard_map/sabci,sl->abcil/dot_general | solution.py:88
  32.2 0.0 collective-permute-done.east_ref
  32.2 2.7 %collective-permute-done.1.west_ref = f32[64,2,4,1,128]{4,3,2,1,0:T(1,128)S(1)} collective-permute-done((f32[64,2,4,1,128]{4,3,2,1,0:T(1,128)S(1)}, f32[64,2,4,1,128]{4,3,2,1,0:T(1,128)S(1)}, u32[]{:S(2)}, u32[]{:S(2)}) %collective-permute-start.1) | collective-permute-done | bytes 262176 | tf_op jit(solution)/shard_map/ppermute | solution.py:78
  35.0 0.0 copy-done
  35.0 0.7 copy-done.1
  35.7 11.8 %shard_map.91 = (f32[64,2,4,16,128]{4,3,2,1,0:T(8,128)}, f32[64,512]{1,0:T(8,128)}) custom-call(f32[64,2,4,16,128]{4,3,2,1,0:T(8,128)} %x_ref.1, f32[64,2,4,1,128]{4,3,2,1,0:T(1,128)} %copy-done, f32[64,2,4,1,128]{4,3,2,1,0:T(1,128)} %copy-done.1, f32[64,2,4,16,128]{4,3,2,1,0:T(8,128)} %fusion.8.edge_ref, f32[2,16,128]{2,1,0:T(8,128)} %u_ref.1, ...), custom_call_target="tpu_custom_call" | custom-call | tf_op jit(solution)/shard_map/pallas_call | solution.py:103
  47.4 1.6 %bitcast_bitcast_fusion.y_ref = f32[4,64,128]{2,1,0:T(8,128)} fusion(f32[64,512]{1,0:T(8,128)} %get-tuple-element.7), kind=kLoop, calls=%fused_computation.6 | loop fusion | bytes 262144 | tf_op jit(solution)/shard_map/transpose | solution.py:337
  49.0 69.9 %shard_map.92.p_ref = f32[64,64]{1,0:T(8,128)} custom-call(f32[4,64,128]{2,1,0:T(8,128)} %bitcast_bitcast_fusion.y_ref, f32[4,1,128]{2,1,0:T(1,128)} %compare_select_fusion.scale_ref, f32[4,1,128]{2,1,0:T(1,128)} %bitcast.54, f32[25]{0:T(128)} %max.4.w_ref), custom_call_target="tpu_custom_call" | custom-call | tf_op jit(solution)/shard_map/pallas_call | solution.py:266
  118.8 9.2 %shard_map.93 = f32[64,2,4,16,128]{4,3,2,1,0:T(8,128)} custom-call(f32[64,64]{1,0:T(8,128)} %shard_map.92.p_ref, f32[64,2,4,16,128]{4,3,2,1,0:T(8,128)} %get-tuple-element.8.x_ref), custom_call_target="tpu_custom_call" | custom-call | tf_op jit(solution)/shard_map/pallas_call | solution.py:301
  (9 shorter events, 0.1 us)
Async XLA Ops:
  0.0 24.4 %copy-start.3 = (s32[1,1,4,128]{3,2,1,0:T(4,128)S(1)}, s32[1,1,4,128]{3,2,1,0:T(4,128)}, u32[]{:S(2)}) copy-start(s32[1,1,4,128]{3,2,1,0:T(4,128)} %param.13) | copy-start | bytes 6148
  0.0 24.5 %copy-start.4 = (f32[1,1,4,128]{3,2,1,0:T(4,128)S(1)}, f32[1,1,4,128]{3,2,1,0:T(4,128)}, u32[]{:S(2)}) copy-start(f32[1,1,4,128]{3,2,1,0:T(4,128)} %param.16) | copy-start | bytes 6148
  0.0 25.3 %copy-start.5 = (s32[1,1,4]{2,1,0:T(1,128)S(1)}, s32[1,1,4]{2,1,0:T(1,128)}, u32[]{:S(2)}) copy-start(s32[1,1,4]{2,1,0:T(1,128)} %param.14) | copy-start | bytes 52
  0.0 26.0 %copy-start.2 = (s32[1,1,5,5]{3,1,2,0:T(1,128)S(1)}, s32[1,1,5,5]{3,1,2,0:T(1,128)}, u32[]{:S(2)}) copy-start(s32[1,1,5,5]{3,1,2,0:T(1,128)} %param.17) | copy-start | bytes 304
  8.7 18.0 %collective-permute-start.2 = (f32[64,2,4,16]{0,3,2,1:T(8,128)S(1)}, f32[64,2,4,16]{0,3,2,1:T(8,128)S(1)}, u32[]{:S(2)}, u32[]{:S(2)}) collective-permute-start(f32[64,2,4,16]{0,3,2,1:T(8,128)S(1)} %bitcast.51), channel_id=1, source_target_pairs={{1,0},{2,1},{3,2},{4,3},{5,4},{6,5},{7,6},{9,8},{10,9},{11,10},{12... | collective-permute-start | bytes 98312 | tf_op jit(solution)/shard_map/ppermute | solution.py:86
  10.6 16.1 %collective-permute-start.3 = (f32[64,2,4,16]{0,3,2,1:T(8,128)S(1)}, f32[64,2,4,16]{0,3,2,1:T(8,128)S(1)}, u32[]{:S(2)}, u32[]{:S(2)}) collective-permute-start(f32[64,2,4,16]{0,3,2,1:T(8,128)S(1)} %bitcast.49), channel_id=1, source_target_pairs={{0,1},{1,2},{2,3},{3,4},{4,5},{5,6},{6,7},{8,9},{9,10},{10,11},{11... | collective-permute-start | bytes 98312 | tf_op jit(solution)/shard_map/ppermute | solution.py:87
  15.8 16.4 %collective-permute-start = (f32[64,2,4,1,128]{4,3,2,1,0:T(1,128)S(1)}, f32[64,2,4,1,128]{4,3,2,1,0:T(1,128)S(1)}, u32[]{:S(2)}, u32[]{:S(2)}) collective-permute-start(f32[64,2,4,1,128]{4,3,2,1,0:T(1,128)S(1)} %get-tuple-element.10), channel_id=1, source_target_pairs={{8,0},{16,8},{24,16},{32,24},{40,32},{48,40},{56,48},{64,56},{72,6... | collective-permute-start | bytes 786440 | tf_op jit(solution)/shard_map/ppermute | solution.py:77
  22.5 12.5 %collective-permute-start.1 = (f32[64,2,4,1,128]{4,3,2,1,0:T(1,128)S(1)}, f32[64,2,4,1,128]{4,3,2,1,0:T(1,128)S(1)}, u32[]{:S(2)}, u32[]{:S(2)}) collective-permute-start(f32[64,2,4,1,128]{4,3,2,1,0:T(1,128)S(1)} %get-tuple-element.9), channel_id=1, source_target_pairs={{0,8},{8,16},{16,24},{24,32},{32,40},{40,48},{48,56},{56,64},{64,7... | collective-permute-start | bytes 786440 | tf_op jit(solution)/shard_map/ppermute | solution.py:78
  32.2 2.7 %copy-start = (f32[64,2,4,1,128]{4,3,2,1,0:T(1,128)}, f32[64,2,4,1,128]{4,3,2,1,0:T(1,128)S(1)}, u32[]{:S(2)}) copy-start(f32[64,2,4,1,128]{4,3,2,1,0:T(1,128)S(1)} %collective-permute-done.east_ref) | copy-start | bytes 786436
  34.9 0.7 copy-start.1

commit v14 on v9

--- a/solution.py
+++ b/solution.py
@@ -192,7 +192,7 @@
         payload[par, half : half + 8, :] = tail
 
         copies = []
-        for k, (dx, dy) in enumerate(OFFSETS):
+        for k, (dx, dy) in sorted(enumerate(OFFSETS), key=lambda item: abs(item[1][0]) + abs(item[1][1])):
             if dx == 0 and dy == 0:
                 continue
             copy = pltpu.make_async_remote_copy(
@@ -215,7 +215,7 @@
         for k, (dx, dy) in enumerate(OFFSETS):
             if dx == 0 and dy == 0:
                 total[...] += w_ref[k] * payload[par]
-        for k, dx, dy, copy, ok in copies:
+        for k, dx, dy, copy, ok in sorted(copies, key=lambda item: item[0]):
             @pl.when(ok)
             def _():
                 copy.wait_send()

time: 127 us -> 131 us (1.031)
  the two profiles are of different devices: /device:TPU:96 before, /device:TPU:86 now
where the time goes in v14:
time: 131 us
  Pallas kernels  98.9 us (75%)
  matrix products  13.6 us (10%)
  starting transfers between devices  10.2 us (8%)
  local copies, waits for them, and re-layouts  5.86 us (4%)
  other arithmetic  2.11 us (2%)
    pallas_call x1, Pallas kernels, run_analysis(): pl.pallas_call(functools.partial(analysis_kernel, nx, ny), out_shape=jax....  77.9 us
    pallas_call x1, Pallas kernels, forecast_step(): pl.pallas_call(stencil_kernel, out_shape=(jax.ShapeDtypeStruct(cells.shap...  11.7 us
    pallas_call x1, Pallas kernels, apply_transform(): pl.pallas_call(transform_kernel, out_shape=jax.ShapeDtypeStruct(cells.sha...  9.25 us
    dot_general x1, matrix products, forecast_step(): jnp.einsum('abcil,sl->sabci', cells, pick, precision=lax.Precision.HIGHES...  8.5 us
    dot_general x1, matrix products, forecast_step(): jnp.einsum('sabci,sl->abcil', jnp.stack([north_halo, south_halo]), place,...  5.07 us
    ppermute x1, starting transfers between devices, forecast_step(): lax.ppermute(cells[:, :, :, rows - 1:rows, :], 'gx', [(i, i + 1) for i in...  3.48 us
    slice x1, local copies, waits for them, and re-layouts, forecast_step(): cells[:, :, :, rows - 1:rows, :]  2.79 us
  transfers between devices with their start and end apart: 4, of which 0 were waited for; matrix products, arithmetic and copies ran while one was open for 8% of the time, Pallas kernels for 0%

profile of v14, /device:TPU:86, one launch (start us, length us, event | category | flops | bytes accessed | tf_op | source)
XLA Modules:
  0.0 130.8 jit_solution(10347028462466357815)
XLA Ops:
  0.0 0.0 copy-start.3
  0.0 0.0 copy-start.2
  0.0 8.5 %fusion = f32[2,64,2,4,16]{1,0,4,3,2:T(2,128)S(1)} fusion(f32[64,2,4,16,128]{4,3,2,1,0:T(8,128)} %x_ref.1, pred[1,128]{1,0:T(4,128)(4,1)S(1)} %get-tuple-element.15, pred[1,128]{1,0:T(4,128)(4,1)S(1)} %get-tuple-element.16), kind=kOutput, calls=%fused_computation | convolution fusion | flops 25166080 | bytes 4260096 | tf_op jit(solution)/shard_map/abcil,sl->sabci/dot_general | solution.py:82
  8.5 0.1 fusion.14
  8.7 1.9 %collective-permute-start.2 = (f32[64,2,4,16]{0,3,2,1:T(8,128)S(1)}, f32[64,2,4,16]{0,3,2,1:T(8,128)S(1)}, u32[]{:S(2)}, u32[]{:S(2)}) collective-permute-start(f32[64,2,4,16]{0,3,2,1:T(8,128)S(1)} %bitcast.51), channel_id=1, source_target_pairs={{1,0},{2,1},{3,2},{4,3},{5,4},{6,5},{7,6},{9,8},{10,9},{11,10},{12... | collective-permute-start | bytes 98312 | tf_op jit(solution)/shard_map/ppermute | solution.py:86
  10.6 2.4 %collective-permute-start.3 = (f32[64,2,4,16]{0,3,2,1:T(8,128)S(1)}, f32[64,2,4,16]{0,3,2,1:T(8,128)S(1)}, u32[]{:S(2)}, u32[]{:S(2)}) collective-permute-start(f32[64,2,4,16]{0,3,2,1:T(8,128)S(1)} %bitcast.49), channel_id=1, source_target_pairs={{0,1},{1,2},{2,3},{3,4},{4,5},{5,6},{6,7},{8,9},{9,10},{10,11},{11... | collective-permute-start | bytes 98312 | tf_op jit(solution)/shard_map/ppermute | solution.py:87
  13.0 2.8 %fusion.13 = (f32[64,2,4,1,128]{4,3,2,1,0:T(1,128)S(1)}, f32[64,2,4,1,128]{4,3,2,1,0:T(1,128)S(1)}) fusion(f32[64,2,4,16,128]{4,3,2,1,0:T(8,128)} %x_ref.1), kind=kLoop, calls=%fused_computation.33 | loop fusion | bytes 1048576 | tf_op jit(solution)/shard_map/slice | solution.py:78
  15.8 2.4 %collective-permute-start = (f32[64,2,4,1,128]{4,3,2,1,0:T(1,128)S(1)}, f32[64,2,4,1,128]{4,3,2,1,0:T(1,128)S(1)}, u32[]{:S(2)}, u32[]{:S(2)}) collective-permute-start(f32[64,2,4,1,128]{4,3,2,1,0:T(1,128)S(1)} %get-tuple-element.10), channel_id=1, source_target_pairs={{8,0},{16,8},{24,16},{32,24},{40,32},{48,40},{56,48},{64,56},{72,6... | collective-permute-start | bytes 786440 | tf_op jit(solution)/shard_map/ppermute | solution.py:77
  18.2 3.5 %collective-permute-start.1 = (f32[64,2,4,1,128]{4,3,2,1,0:T(1,128)S(1)}, f32[64,2,4,1,128]{4,3,2,1,0:T(1,128)S(1)}, u32[]{:S(2)}, u32[]{:S(2)}) collective-permute-start(f32[64,2,4,1,128]{4,3,2,1,0:T(1,128)S(1)} %get-tuple-element.9), channel_id=1, source_target_pairs={{0,8},{8,16},{16,24},{24,32},{32,40},{40,48},{48,56},{56,64},{64,7... | collective-permute-start | bytes 786440 | tf_op jit(solution)/shard_map/ppermute | solution.py:78
  21.7 0.0 copy-done.3
  21.7 0.1 and_convert_fusion
  21.8 0.0 copy-done.4
  21.8 0.8 fusion.2
  22.6 0.0 copy-done.5
  22.6 0.6 compare_select_fusion.scale_ref
  23.2 0.0 copy-done.2
  23.2 0.1 reshape.175
  23.3 0.1 convert_element_type.26
  23.4 0.5 max.4.w_ref
  23.9 0.0 collective-permute-done.2
  23.9 0.0 collective-permute-done.3
  24.0 0.4 copy.15
  24.4 5.1 %fusion.8.edge_ref = f32[64,2,4,16,128]{4,3,2,1,0:T(8,128)} fusion(f32[2,64,2,4,16]{4,0,3,2,1:T(2,128)S(1)} %copy.15, pred[1,128]{1,0:T(4,128)(4,1)S(1)} %get-tuple-element.16, pred[1,128]{1,0:T(4,128)(4,1)S(1)} %get-tuple-element.15), kind=kOutput, calls=%fused_computation.24 | convolution fusion | flops 25166080 | bytes 4260096 | tf_op jit(solution)/shard_map/sabci,sl->abcil/dot_general | solution.py:88
  29.5 0.0 collective-permute-done.east_ref
  29.5 0.0 collective-permute-done.1.west_ref
  29.5 0.0 copy-start.1
  29.5 0.7 copy-done
  30.2 0.1 copy-done.1
  30.3 11.7 %shard_map.91 = (f32[64,2,4,16,128]{4,3,2,1,0:T(8,128)}, f32[64,512]{1,0:T(8,128)}) custom-call(f32[64,2,4,16,128]{4,3,2,1,0:T(8,128)} %x_ref.1, f32[64,2,4,1,128]{4,3,2,1,0:T(1,128)} %copy-done, f32[64,2,4,1,128]{4,3,2,1,0:T(1,128)} %copy-done.1, f32[64,2,4,16,128]{4,3,2,1,0:T(8,128)} %fusion.8.edge_ref, f32[2,16,128]{2,1,0:T(8,128)} %u_ref.1, ...), custom_call_target="tpu_custom_call" | custom-call | tf_op jit(solution)/shard_map/pallas_call | solution.py:103
  42.0 1.6 %bitcast_bitcast_fusion.y_ref = f32[4,64,128]{2,1,0:T(8,128)} fusion(f32[64,512]{1,0:T(8,128)} %get-tuple-element.7), kind=kLoop, calls=%fused_computation.6 | loop fusion | bytes 262144 | tf_op jit(solution)/shard_map/transpose | solution.py:336
  43.6 77.9 %shard_map.92.p_ref = f32[64,64]{1,0:T(8,128)} custom-call(f32[4,64,128]{2,1,0:T(8,128)} %bitcast_bitcast_fusion.y_ref, f32[4,1,128]{2,1,0:T(1,128)} %compare_select_fusion.scale_ref, f32[4,1,128]{2,1,0:T(1,128)} %bitcast.54, f32[25]{0:T(128)} %max.4.w_ref), custom_call_target="tpu_custom_call" | custom-call | tf_op jit(solution)/shard_map/pallas_call | solution.py:265
  121.5 9.2 %shard_map.93 = f32[64,2,4,16,128]{4,3,2,1,0:T(8,128)} custom-call(f32[64,64]{1,0:T(8,128)} %shard_map.92.p_ref, f32[64,2,4,16,128]{4,3,2,1,0:T(8,128)} %get-tuple-element.8.x_ref), custom_call_target="tpu_custom_call" | custom-call | tf_op jit(solution)/shard_map/pallas_call | solution.py:300
  (9 shorter events, 0.1 us)
Async XLA Ops:
  0.0 21.7 %copy-start.3 = (s32[1,1,4,128]{3,2,1,0:T(4,128)S(1)}, s32[1,1,4,128]{3,2,1,0:T(4,128)}, u32[]{:S(2)}) copy-start(s32[1,1,4,128]{3,2,1,0:T(4,128)} %param.13) | copy-start | bytes 6148
  0.0 21.8 %copy-start.4 = (f32[1,1,4,128]{3,2,1,0:T(4,128)S(1)}, f32[1,1,4,128]{3,2,1,0:T(4,128)}, u32[]{:S(2)}) copy-start(f32[1,1,4,128]{3,2,1,0:T(4,128)} %param.16) | copy-start | bytes 6148
  0.0 22.6 %copy-start.5 = (s32[1,1,4]{2,1,0:T(1,128)S(1)}, s32[1,1,4]{2,1,0:T(1,128)}, u32[]{:S(2)}) copy-start(s32[1,1,4]{2,1,0:T(1,128)} %param.14) | copy-start | bytes 52
  0.0 23.2 %copy-start.2 = (s32[1,1,5,5]{3,1,2,0:T(1,128)S(1)}, s32[1,1,5,5]{3,1,2,0:T(1,128)}, u32[]{:S(2)}) copy-start(s32[1,1,5,5]{3,1,2,0:T(1,128)} %param.17) | copy-start | bytes 304
  8.7 15.3 %collective-permute-start.2 = (f32[64,2,4,16]{0,3,2,1:T(8,128)S(1)}, f32[64,2,4,16]{0,3,2,1:T(8,128)S(1)}, u32[]{:S(2)}, u32[]{:S(2)}) collective-permute-start(f32[64,2,4,16]{0,3,2,1:T(8,128)S(1)} %bitcast.51), channel_id=1, source_target_pairs={{1,0},{2,1},{3,2},{4,3},{5,4},{6,5},{7,6},{9,8},{10,9},{11,10},{12... | collective-permute-start | bytes 98312 | tf_op jit(solution)/shard_map/ppermute | solution.py:86
  10.6 13.4 %collective-permute-start.3 = (f32[64,2,4,16]{0,3,2,1:T(8,128)S(1)}, f32[64,2,4,16]{0,3,2,1:T(8,128)S(1)}, u32[]{:S(2)}, u32[]{:S(2)}) collective-permute-start(f32[64,2,4,16]{0,3,2,1:T(8,128)S(1)} %bitcast.49), channel_id=1, source_target_pairs={{0,1},{1,2},{2,3},{3,4},{4,5},{5,6},{6,7},{8,9},{9,10},{10,11},{11... | collective-permute-start | bytes 98312 | tf_op jit(solution)/shard_map/ppermute | solution.py:87
  15.8 13.7 %collective-permute-start = (f32[64,2,4,1,128]{4,3,2,1,0:T(1,128)S(1)}, f32[64,2,4,1,128]{4,3,2,1,0:T(1,128)S(1)}, u32[]{:S(2)}, u32[]{:S(2)}) collective-permute-start(f32[64,2,4,1,128]{4,3,2,1,0:T(1,128)S(1)} %get-tuple-element.10), channel_id=1, source_target_pairs={{8,0},{16,8},{24,16},{32,24},{40,32},{48,40},{56,48},{64,56},{72,6... | collective-permute-start | bytes 786440 | tf_op jit(solution)/shard_map/ppermute | solution.py:77
  18.2 11.3 %collective-permute-start.1 = (f32[64,2,4,1,128]{4,3,2,1,0:T(1,128)S(1)}, f32[64,2,4,1,128]{4,3,2,1,0:T(1,128)S(1)}, u32[]{:S(2)}, u32[]{:S(2)}) collective-permute-start(f32[64,2,4,1,128]{4,3,2,1,0:T(1,128)S(1)} %get-tuple-element.9), channel_id=1, source_target_pairs={{0,8},{8,16},{16,24},{24,32},{32,40},{40,48},{48,56},{56,64},{64,7... | collective-permute-start | bytes 786440 | tf_op jit(solution)/shard_map/ppermute | solution.py:78
  29.5 0.7 copy-start
  29.5 0.8 copy-start.1

commit v15 on v12

--- a/solution.py
+++ b/solution.py
@@ -289,18 +289,19 @@
 def transform_kernel(p_ref, x_ref, o_ref):
     rows = x_ref.shape[3]
     mix = p_ref[...]
-    for i in range(rows):
-        o_ref[:, 0, 0, i, :] = jnp.dot(mix, x_ref[:, 0, 0, i, :],
-                                       precision=lax.Precision.HIGHEST, preferred_element_type=jnp.float32)
+    for f in range(x_ref.shape[2]):
+        for i in range(rows):
+            o_ref[:, 0, f, i, :] = jnp.dot(mix, x_ref[:, 0, f, i, :],
+                                           precision=lax.Precision.HIGH, preferred_element_type=jnp.float32)
 
 
 def apply_transform(carried, cells):
     members, levels, fields, rows, lanes = cells.shape
-    block = pl.BlockSpec((members, 1, 1, rows, lanes), lambda a, b: (0, a, b, 0, 0))
+    block = pl.BlockSpec((members, 1, 2, rows, lanes), lambda a, b: (0, a, b, 0, 0))
     return pl.pallas_call(
         transform_kernel,
         out_shape=jax.ShapeDtypeStruct(cells.shape, cells.dtype),
-        grid=(levels, fields),
+        grid=(levels, fields // 2),
         in_specs=[pl.BlockSpec((members, members), lambda a, b: (0, 0)), block],
         out_specs=block,
     )(carried, cells)

time: 128 us -> 126 us (0.984)
  Pallas kernels: 89.7 us -> 88 us
    pallas_call x1, Pallas kernels: 10.1 us -> 8.36 us  [apply_transform(): pl.pallas_call(transform_kernel, out_shape=jax.ShapeDtypeStruct(cells.sha...]
where the time goes in v15:
time: 126 us; the launch traced here: 125 us
  Pallas kernels  88 us (70%)
  matrix products  13.6 us (11%)
  starting transfers between devices  12.9 us (10%)
  local copies, waits for them, and re-layouts  5.78 us (5%)
  waiting for transfers between devices  2.74 us (2%)
  other arithmetic  2.11 us (2%)
    pallas_call x1, Pallas kernels, run_analysis(): pl.pallas_call(functools.partial(analysis_kernel, nx, ny), out_shape=jax....  67.9 us
    pallas_call x1, Pallas kernels, forecast_step(): pl.pallas_call(stencil_kernel, out_shape=(jax.ShapeDtypeStruct(cells.shap...  11.8 us
    dot_general x1, matrix products, forecast_step(): jnp.einsum('abcil,sl->sabci', cells, pick, precision=lax.Precision.HIGHES...  8.5 us
    pallas_call x1, Pallas kernels, apply_transform(): pl.pallas_call(transform_kernel, out_shape=jax.ShapeDtypeStruct(cells.sha...  8.36 us
    ppermute x1, starting transfers between devices, forecast_step(): lax.ppermute(cells[:, :, :, 0:1, :], 'gx', [(i + 1, i) for i in range(nx...  6.66 us
    dot_general x1, matrix products, forecast_step(): jnp.einsum('sabci,sl->abcil', jnp.stack([north_halo, south_halo]), place,...  5.07 us
    slice x1, local copies, waits for them, and re-layouts, forecast_step(): cells[:, :, :, rows - 1:rows, :]  2.79 us
    ppermute x1, waiting for transfers between devices, forecast_step(): lax.ppermute(cells[:, :, :, rows - 1:rows, :], 'gx', [(i, i + 1) for i in...  2.73 us
  transfers between devices with their start and end apart: 4, of which 1 were waited for; matrix products, arithmetic and copies ran while one was open for 8% of the time, Pallas kernels for 0%

profile of v15, /device:TPU:96, one launch (start us, length us, event | category | flops | bytes accessed | tf_op | source)
XLA Modules:
  0.0 125.2 jit_solution(2818870129568612509)
XLA Ops:
  0.0 0.0 copy-start.3
  0.0 0.0 copy-start.4
  0.0 0.0 copy-start.2
  0.0 8.5 %fusion = f32[2,64,2,4,16]{1,0,4,3,2:T(2,128)S(1)} fusion(f32[64,2,4,16,128]{4,3,2,1,0:T(8,128)} %x_ref.1, pred[1,128]{1,0:T(4,128)(4,1)S(1)} %get-tuple-element.15, pred[1,128]{1,0:T(4,128)(4,1)S(1)} %get-tuple-element.16), kind=kOutput, calls=%fused_computation | convolution fusion | flops 25166080 | bytes 4260096 | tf_op jit(solution)/shard_map/abcil,sl->sabci/dot_general | solution.py:82
  8.5 0.1 fusion.14
  8.7 1.9 %collective-permute-start.2 = (f32[64,2,4,16]{0,3,2,1:T(8,128)S(1)}, f32[64,2,4,16]{0,3,2,1:T(8,128)S(1)}, u32[]{:S(2)}, u32[]{:S(2)}) collective-permute-start(f32[64,2,4,16]{0,3,2,1:T(8,128)S(1)} %bitcast.51), channel_id=1, source_target_pairs={{1,0},{2,1},{3,2},{4,3},{5,4},{6,5},{7,6},{9,8},{10,9},{11,10},{12... | collective-permute-start | bytes 98312 | tf_op jit(solution)/shard_map/ppermute | solution.py:86
  10.6 2.4 %collective-permute-start.3 = (f32[64,2,4,16]{0,3,2,1:T(8,128)S(1)}, f32[64,2,4,16]{0,3,2,1:T(8,128)S(1)}, u32[]{:S(2)}, u32[]{:S(2)}) collective-permute-start(f32[64,2,4,16]{0,3,2,1:T(8,128)S(1)} %bitcast.49), channel_id=1, source_target_pairs={{0,1},{1,2},{2,3},{3,4},{4,5},{5,6},{6,7},{8,9},{9,10},{10,11},{11... | collective-permute-start | bytes 98312 | tf_op jit(solution)/shard_map/ppermute | solution.py:87
  13.0 2.8 %fusion.13 = (f32[64,2,4,1,128]{4,3,2,1,0:T(1,128)S(1)}, f32[64,2,4,1,128]{4,3,2,1,0:T(1,128)S(1)}) fusion(f32[64,2,4,16,128]{4,3,2,1,0:T(8,128)} %x_ref.1), kind=kLoop, calls=%fused_computation.33 | loop fusion | bytes 1048576 | tf_op jit(solution)/shard_map/slice | solution.py:78
  15.8 6.7 %collective-permute-start = (f32[64,2,4,1,128]{4,3,2,1,0:T(1,128)S(1)}, f32[64,2,4,1,128]{4,3,2,1,0:T(1,128)S(1)}, u32[]{:S(2)}, u32[]{:S(2)}) collective-permute-start(f32[64,2,4,1,128]{4,3,2,1,0:T(1,128)S(1)} %get-tuple-element.10), channel_id=1, source_target_pairs={{8,0},{16,8},{24,16},{32,24},{40,32},{48,40},{56,48},{64,56},{72,6... | collective-permute-start | bytes 786440 | tf_op jit(solution)/shard_map/ppermute | solution.py:77
  22.5 1.9 %collective-permute-start.1 = (f32[64,2,4,1,128]{4,3,2,1,0:T(1,128)S(1)}, f32[64,2,4,1,128]{4,3,2,1,0:T(1,128)S(1)}, u32[]{:S(2)}, u32[]{:S(2)}) collective-permute-start(f32[64,2,4,1,128]{4,3,2,1,0:T(1,128)S(1)} %get-tuple-element.9), channel_id=1, source_target_pairs={{0,8},{8,16},{16,24},{24,32},{32,40},{40,48},{48,56},{56,64},{64,7... | collective-permute-start | bytes 786440 | tf_op jit(solution)/shard_map/ppermute | solution.py:78
  24.4 0.0 copy-done.3
  24.4 0.1 and_convert_fusion
  24.5 0.0 copy-done.4
  24.5 0.8 fusion.2
  25.3 0.0 copy-done.5
  25.3 0.6 compare_select_fusion.scale_ref
  26.0 0.0 copy-done.2
  26.0 0.1 reshape.175
  26.1 0.1 convert_element_type.26
  26.1 0.5 max.4.w_ref
  26.7 0.0 collective-permute-done.2
  26.7 0.0 collective-permute-done.3
  26.7 0.4 copy.15
  27.1 5.1 %fusion.8.edge_ref = f32[64,2,4,16,128]{4,3,2,1,0:T(8,128)} fusion(f32[2,64,2,4,16]{4,0,3,2,1:T(2,128)S(1)} %copy.15, pred[1,128]{1,0:T(4,128)(4,1)S(1)} %get-tuple-element.16, pred[1,128]{1,0:T(4,128)(4,1)S(1)} %get-tuple-element.15), kind=kOutput, calls=%fused_computation.24 | convolution fusion | flops 25166080 | bytes 4260096 | tf_op jit(solution)/shard_map/sabci,sl->abcil/dot_general | solution.py:88
  32.2 0.0 collective-permute-done.east_ref
  32.2 2.7 %collective-permute-done.1.west_ref = f32[64,2,4,1,128]{4,3,2,1,0:T(1,128)S(1)} collective-permute-done((f32[64,2,4,1,128]{4,3,2,1,0:T(1,128)S(1)}, f32[64,2,4,1,128]{4,3,2,1,0:T(1,128)S(1)}, u32[]{:S(2)}, u32[]{:S(2)}) %collective-permute-start.1) | collective-permute-done | bytes 262176 | tf_op jit(solution)/shard_map/ppermute | solution.py:78
  35.0 0.0 copy-done
  35.0 0.7 copy-done.1
  35.7 11.8 %shard_map.91 = (f32[64,2,4,16,128]{4,3,2,1,0:T(8,128)}, f32[64,512]{1,0:T(8,128)}) custom-call(f32[64,2,4,16,128]{4,3,2,1,0:T(8,128)} %x_ref.1, f32[64,2,4,1,128]{4,3,2,1,0:T(1,128)} %copy-done, f32[64,2,4,1,128]{4,3,2,1,0:T(1,128)} %copy-done.1, f32[64,2,4,16,128]{4,3,2,1,0:T(8,128)} %fusion.8.edge_ref, f32[2,16,128]{2,1,0:T(8,128)} %u_ref.1, ...), custom_call_target="tpu_custom_call" | custom-call | tf_op jit(solution)/shard_map/pallas_call | solution.py:103
  47.4 1.6 %bitcast_bitcast_fusion.y_ref = f32[4,64,128]{2,1,0:T(8,128)} fusion(f32[64,512]{1,0:T(8,128)} %get-tuple-element.7), kind=kLoop, calls=%fused_computation.6 | loop fusion | bytes 262144 | tf_op jit(solution)/shard_map/transpose | solution.py:337
  49.0 67.9 %shard_map.92.p_ref = f32[64,64]{1,0:T(8,128)} custom-call(f32[4,64,128]{2,1,0:T(8,128)} %bitcast_bitcast_fusion.y_ref, f32[4,1,128]{2,1,0:T(1,128)} %compare_select_fusion.scale_ref, f32[4,1,128]{2,1,0:T(1,128)} %bitcast.54, f32[25]{0:T(128)} %max.4.w_ref), custom_call_target="tpu_custom_call" | custom-call | tf_op jit(solution)/shard_map/pallas_call | solution.py:265
  116.9 8.4 %shard_map.93 = f32[64,2,4,16,128]{4,3,2,1,0:T(8,128)} custom-call(f32[64,64]{1,0:T(8,128)} %shard_map.92.p_ref, f32[64,2,4,16,128]{4,3,2,1,0:T(8,128)} %get-tuple-element.8.x_ref), custom_call_target="tpu_custom_call" | custom-call | tf_op jit(solution)/shard_map/pallas_call | solution.py:301
  (9 shorter events, 0.1 us)
Async XLA Ops:
  0.0 24.4 %copy-start.3 = (s32[1,1,4,128]{3,2,1,0:T(4,128)S(1)}, s32[1,1,4,128]{3,2,1,0:T(4,128)}, u32[]{:S(2)}) copy-start(s32[1,1,4,128]{3,2,1,0:T(4,128)} %param.13) | copy-start | bytes 6148
  0.0 24.5 %copy-start.4 = (f32[1,1,4,128]{3,2,1,0:T(4,128)S(1)}, f32[1,1,4,128]{3,2,1,0:T(4,128)}, u32[]{:S(2)}) copy-start(f32[1,1,4,128]{3,2,1,0:T(4,128)} %param.16) | copy-start | bytes 6148
  0.0 25.3 %copy-start.5 = (s32[1,1,4]{2,1,0:T(1,128)S(1)}, s32[1,1,4]{2,1,0:T(1,128)}, u32[]{:S(2)}) copy-start(s32[1,1,4]{2,1,0:T(1,128)} %param.14) | copy-start | bytes 52
  0.0 26.0 %copy-start.2 = (s32[1,1,5,5]{3,1,2,0:T(1,128)S(1)}, s32[1,1,5,5]{3,1,2,0:T(1,128)}, u32[]{:S(2)}) copy-start(s32[1,1,5,5]{3,1,2,0:T(1,128)} %param.17) | copy-start | bytes 304
  8.7 18.0 %collective-permute-start.2 = (f32[64,2,4,16]{0,3,2,1:T(8,128)S(1)}, f32[64,2,4,16]{0,3,2,1:T(8,128)S(1)}, u32[]{:S(2)}, u32[]{:S(2)}) collective-permute-start(f32[64,2,4,16]{0,3,2,1:T(8,128)S(1)} %bitcast.51), channel_id=1, source_target_pairs={{1,0},{2,1},{3,2},{4,3},{5,4},{6,5},{7,6},{9,8},{10,9},{11,10},{12... | collective-permute-start | bytes 98312 | tf_op jit(solution)/shard_map/ppermute | solution.py:86
  10.6 16.1 %collective-permute-start.3 = (f32[64,2,4,16]{0,3,2,1:T(8,128)S(1)}, f32[64,2,4,16]{0,3,2,1:T(8,128)S(1)}, u32[]{:S(2)}, u32[]{:S(2)}) collective-permute-start(f32[64,2,4,16]{0,3,2,1:T(8,128)S(1)} %bitcast.49), channel_id=1, source_target_pairs={{0,1},{1,2},{2,3},{3,4},{4,5},{5,6},{6,7},{8,9},{9,10},{10,11},{11... | collective-permute-start | bytes 98312 | tf_op jit(solution)/shard_map/ppermute | solution.py:87
  15.8 16.4 %collective-permute-start = (f32[64,2,4,1,128]{4,3,2,1,0:T(1,128)S(1)}, f32[64,2,4,1,128]{4,3,2,1,0:T(1,128)S(1)}, u32[]{:S(2)}, u32[]{:S(2)}) collective-permute-start(f32[64,2,4,1,128]{4,3,2,1,0:T(1,128)S(1)} %get-tuple-element.10), channel_id=1, source_target_pairs={{8,0},{16,8},{24,16},{32,24},{40,32},{48,40},{56,48},{64,56},{72,6... | collective-permute-start | bytes 786440 | tf_op jit(solution)/shard_map/ppermute | solution.py:77
  22.5 12.5 %collective-permute-start.1 = (f32[64,2,4,1,128]{4,3,2,1,0:T(1,128)S(1)}, f32[64,2,4,1,128]{4,3,2,1,0:T(1,128)S(1)}, u32[]{:S(2)}, u32[]{:S(2)}) collective-permute-start(f32[64,2,4,1,128]{4,3,2,1,0:T(1,128)S(1)} %get-tuple-element.9), channel_id=1, source_target_pairs={{0,8},{8,16},{16,24},{24,32},{32,40},{40,48},{48,56},{56,64},{64,7... | collective-permute-start | bytes 786440 | tf_op jit(solution)/shard_map/ppermute | solution.py:78
  32.2 2.7 %copy-start = (f32[64,2,4,1,128]{4,3,2,1,0:T(1,128)}, f32[64,2,4,1,128]{4,3,2,1,0:T(1,128)S(1)}, u32[]{:S(2)}) copy-start(f32[64,2,4,1,128]{4,3,2,1,0:T(1,128)S(1)} %collective-permute-done.east_ref) | copy-start | bytes 786436
  34.9 0.7 copy-start.1
